TPU v7x, 32 devices: a whole 2x2x4 slice. The times are simulated.
32 devices in a mesh: seq: 4 (over z), mp: 8 (over y, x, core).
Axes of the slice: x: 2, y: 2, z: 4, core: 2. Of those that a mesh axis runs over, the one named last changes fastest.
Arguments:
- ids: int32 [16, 1024], P('seq'), may hold values from 0 to 274
- lengths: int32 [1024], replicated, may hold values from 1 to 16, 12288 in all
- order: int32 [1024], replicated, may hold values from 0 to 1023, each once
- h_init: bfloat16 [2, 1024, 2048], P(None, 'seq', 'mp'), may hold values from -3 to 3
- c_init: float32 [2, 1024, 2048], P(None, 'seq', 'mp'), may hold values from -5 to 5
- embed: bfloat16 [2, 275, 100], replicated, may hold values from -5 to 5
- w_in: bfloat16 [2, 100, 8192], P(None, None, 'mp'), may hold values from -0.625 to 0.625
- w_rec: bfloat16 [2, 2048, 8192], P(None, None, 'mp'), may hold values from -0.125 to 0.125
- bias: float32 [2, 8192], P(None, 'mp'), may hold values from -3 to 3
- w_dec: bfloat16 [2, 2048, 275], P(None, 'mp'), may hold values from -0.75 to 0.75
- b_dec: float32 [2, 275], replicated, may hold values from -3 to 3
Outputs:
- loss: float32 [], replicated
- h_init_grad: float32 [2, 1024, 2048], P(None, 'seq', 'mp')
- c_init_grad: float32 [2, 1024, 2048], P(None, 'seq', 'mp')
- embed_grad: float32 [2, 275, 100], replicated
- w_in_grad: float32 [2, 100, 8192], P(None, None, ('mp', 'seq'))
- w_rec_grad: float32 [2, 2048, 8192], P(None, 'seq', 'mp')
- bias_grad: float32 [2, 8192], P(None, ('mp', 'seq'))
- w_dec_grad: float32 [2, 2048, 275], P(None, ('mp', 'seq'))
- b_dec_grad: float32 [2, 275], replicated
- rms_embed: float32 [2], replicated
- rms_hidden: float32 [2], replicated
- rms_logits: float32 [2], replicated
Inputs may be any that keep to these rules, and one draw needn't show every extreme that they name: `lengths`: they add up to 12288, and the longest stream is valid over all 16 positions. `order`: every stream stands in exactly one slot.
All inputs are finite; a program needn't handle non-finite values.
Results may differ from a plain program's by a relative error of at most 0.018.
Values may be sent and summed in bfloat16 or wider, within the bound.
A program may use at most 256 MiB of HBM per device.

v0:
```python
import jax
import jax.numpy as jnp
from jax import lax
from jax.sharding import PartitionSpec as P


def extended(x, sides, width):
    for axis, dim in sides:
        peers, length = (lax.axis_size(axis), x.shape[dim])
        up = [(i, (i + 1) % peers) for i in range(peers - 1)]
        down = [(j, i) for i, j in up]
        last = lax.slice_in_dim(x, length - width, length, axis=dim)
        leading = lax.slice_in_dim(x, 0, width, axis=dim)
        before = lax.ppermute(last, axis, up)
        after = lax.ppermute(leading, axis, down)
        x = jnp.concatenate([before, x, after], axis=dim)
    return x


def split_gates(pre_gate):
    grouped = pre_gate.reshape(pre_gate.shape[:-1] + (pre_gate.shape[-1] // 4, 4))
    in_gate = jax.nn.sigmoid(grouped[..., 0])
    forget = jax.nn.sigmoid(grouped[..., 1])
    cell_gate = jnp.tanh(grouped[..., 2])
    out_gate = jax.nn.sigmoid(grouped[..., 3])
    return (in_gate, forget, cell_gate, out_gate)


def per_device(ids, lengths, order, h_init, c_init, embed, w_in, w_rec, bias, w_dec, b_dec):
    seq_count = lax.axis_size("seq")
    mp_count = lax.axis_size("mp")
    seq_rank = lax.axis_index("seq")
    mp_rank = lax.axis_index("mp")
    local_time, streams = ids.shape
    length = local_time * seq_count
    per_dev = streams // seq_count
    letter_count = embed.shape[1]
    own_units = w_rec.shape[2] // 4
    all_units = w_rec.shape[1]
    padded = extended(ids, (("seq", 0),), 1)
    slot_pad = jnp.take(padded, order, axis=1)
    slot_ids = slot_pad[1:-1]
    slot_len = jnp.take(lengths, order)
    count = 2.0 * jnp.sum(slot_len - 1).astype(jnp.float32)
    live_total = jnp.sum(slot_len).astype(jnp.float32)
    letters = jnp.arange(letter_count, dtype=jnp.int32)
    onehot = (slot_ids[:, :, None] == letters).astype(jnp.bfloat16)
    letter_rows = jnp.einsum(
        "tbv,dve->tbde", onehot, embed, preferred_element_type=jnp.float32
    ).astype(jnp.bfloat16)
    gates_in = jnp.einsum(
        "tbde,dec->tbdc", letter_rows, w_in, preferred_element_type=jnp.float32
    ).astype(jnp.bfloat16)
    gates_seq = lax.all_to_all(gates_in, "seq", split_axis=1, concat_axis=0, tiled=True)
    own_len = lax.dynamic_slice_in_dim(slot_len, seq_rank * per_dev, per_dev)
    steps = jnp.arange(length, dtype=jnp.int32)

    def step_live(step):
        return jnp.stack([step < own_len, length - 1 - step < own_len])[:, :, None]

    def step_inputs(table, step):
        fore = lax.dynamic_index_in_dim(table, step, 0, keepdims=False)[:, 0]
        back = lax.dynamic_index_in_dim(table, length - 1 - step, 0, keepdims=False)[:, 1]
        return jnp.stack([fore, back])

    def forward_step(carry, step):
        hidden, cell = carry
        whole = lax.all_gather(hidden, "mp", axis=2, tiled=True)
        recurrent = jnp.einsum("dbh,dhc->dbc", whole, w_rec, preferred_element_type=jnp.float32)
        pre_gate = step_inputs(gates_seq, step).astype(jnp.float32) + recurrent + bias[:, None]
        in_gate, forget, cell_gate, out_gate = split_gates(pre_gate)
        new_cell = forget * cell + in_gate * cell_gate
        live = step_live(step)
        cell_next = jnp.where(live, new_cell, cell)
        hidden_next = jnp.where(
            live, out_gate * jnp.tanh(new_cell), hidden.astype(jnp.float32)
        ).astype(jnp.bfloat16)
        return ((hidden_next, cell_next), (hidden, cell, pre_gate, hidden_next))

    final_state, (kept_states, cells, pre_gates, outputs) = lax.scan(
        forward_step, (h_init, c_init), steps
    )
    fore_mask = steps[:, None] < own_len[None, :]
    back_mask = (length - 1 - steps)[:, None] < own_len[None, :]
    live_masks = jnp.stack([fore_mask, back_mask], axis=1).astype(jnp.float32)
    outputs_wide = outputs.astype(jnp.float32)
    hidden_sq_part = jnp.sum(live_masks[..., None] * outputs_wide * outputs_wide, axis=(0, 2, 3))
    time_hidden = jnp.stack([outputs[:, 0], jnp.flip(outputs[:, 1], 0)], axis=2)
    time_major = lax.all_to_all(time_hidden, "seq", split_axis=0, concat_axis=1, tiled=True)
    rows = local_time * streams
    token_hidden = time_major.reshape(rows, 2, own_units)
    tok_dev = rows // mp_count
    piece = token_hidden
    logits = (
        lax.psum_scatter(
            jnp.einsum("rdh,dhv->rdv", piece, w_dec, preferred_element_type=jnp.float32).astype(
                jnp.bfloat16
            ),
            "mp",
            scatter_dimension=0,
            tiled=True,
        ).astype(jnp.float32)
        + b_dec[None]
    )
    first = mp_rank * tok_dev
    ahead = lax.dynamic_slice_in_dim(slot_pad[2:].reshape(rows), first, tok_dev)
    behind = lax.dynamic_slice_in_dim(slot_pad[:-2].reshape(rows), first, tok_dev)
    time_grid = seq_rank * local_time + jnp.arange(local_time, dtype=jnp.int32)[:, None]
    time_rows = lax.dynamic_slice_in_dim(
        jnp.broadcast_to(time_grid, (local_time, streams)).reshape(rows), first, tok_dev
    )
    len_rows = lax.dynamic_slice_in_dim(
        jnp.broadcast_to(slot_len[None, :], (local_time, streams)).reshape(rows), first, tok_dev
    )
    fore_valid = time_rows + 1 < len_rows
    back_valid = (time_rows >= 1) & (time_rows < len_rows)
    valid = jnp.stack([fore_valid, back_valid], axis=1).astype(jnp.float32)
    targets = jnp.stack([ahead, behind], axis=1)
    logit_sq_part = jnp.sum(valid[:, :, None] * logits * logits, axis=(0, 2))
    top = jnp.max(logits, axis=-1, keepdims=True)
    total = jnp.sum(jnp.exp(logits - top), axis=-1, keepdims=True)
    log_total = top + jnp.log(total)
    softmax_out = jnp.exp(logits - log_total)
    target_hot = targets[:, :, None] == letters
    picked = jnp.sum(jnp.where(target_hot, logits, 0.0), axis=-1)
    loss_part = jnp.sum(valid * (log_total[:, :, 0] - picked))
    grad_logits = (
        valid[:, :, None] * (softmax_out - target_hot.astype(jnp.float32)) / count
    ).astype(jnp.bfloat16)
    dec_bias_part = jnp.sum(grad_logits.astype(jnp.float32), axis=0)
    piece = lax.all_gather(grad_logits, "mp", axis=0, tiled=True)
    grad_piece = jnp.einsum("rdv,dhv->rdh", piece, w_dec, preferred_element_type=jnp.float32)
    grad_dec = jnp.einsum("rdh,rdv->dhv", token_hidden, piece, preferred_element_type=jnp.float32)
    grad_from_dec = lax.all_to_all(
        grad_piece.reshape(local_time, streams, 2, own_units).astype(jnp.bfloat16),
        "seq",
        split_axis=1,
        concat_axis=0,
        tiled=True,
    ).astype(jnp.float32)

    def backward_step(carry, inputs):
        grad_hidden, grad_cell = carry
        step, cell, pre_gate = inputs
        grad_hidden = grad_hidden + step_inputs(grad_from_dec, step)
        in_gate, forget, cell_gate, out_gate = split_gates(pre_gate)
        new_cell = forget * cell + in_gate * cell_gate
        squash = jnp.tanh(new_cell)
        live = step_live(step)
        grad_new = jnp.where(
            live, grad_cell + grad_hidden * out_gate * (1.0 - squash * squash), 0.0
        )
        grad_out = jnp.where(live, grad_hidden * squash, 0.0)
        grad_stack = jnp.stack(
            [
                grad_new * cell_gate * in_gate * (1.0 - in_gate),
                grad_new * cell * forget * (1.0 - forget),
                grad_new * in_gate * (1.0 - cell_gate * cell_gate),
                grad_out * out_gate * (1.0 - out_gate),
            ],
            axis=-1,
        )
        grad_pre = grad_stack.reshape(pre_gate.shape).astype(jnp.bfloat16)
        grad_cell_prev = grad_new * forget + jnp.where(live, 0.0, grad_cell)
        held = jnp.where(live, 0.0, grad_hidden)
        terms = jnp.einsum("dbc,dhc->dbh", grad_pre, w_rec, preferred_element_type=jnp.float32)
        through = lax.psum_scatter(
            terms.astype(jnp.bfloat16), "mp", scatter_dimension=2, tiled=True
        ).astype(jnp.float32)
        return ((held + through, grad_cell_prev), grad_pre)

    start_state = jnp.zeros(c_init.shape, jnp.float32)
    (hidden_grad, cell_grad), grad_pres = lax.scan(
        backward_step, (start_state, start_state), (steps, cells, pre_gates), reverse=True
    )
    rec_grad = jnp.einsum(
        "sdbh,sdbc->dhc",
        lax.all_gather(kept_states, "mp", axis=3, tiled=True),
        grad_pres,
        preferred_element_type=jnp.float32,
    )
    gate_bias_grad = jnp.sum(grad_pres.astype(jnp.float32), axis=(0, 2))
    grad_time = jnp.stack([grad_pres[:, 0], jnp.flip(grad_pres[:, 1], 0)], axis=2)
    grad_major = lax.all_to_all(grad_time, "seq", split_axis=0, concat_axis=1, tiled=True)
    in_grad = jnp.einsum(
        "tbde,tbdc->dec", letter_rows, grad_major, preferred_element_type=jnp.float32
    )
    letter_grad = jnp.einsum(
        "tbv,tbdc->dvc", onehot, grad_major, preferred_element_type=jnp.float32
    )
    embed_part = jnp.einsum(
        "dvc,dec->dve", letter_grad, w_in.astype(jnp.float32), precision=lax.Precision.HIGHEST
    )
    rec_part, bias_part, in_part, dec_part = (
        lax.psum_scatter(
            rec_grad.astype(jnp.bfloat16), "seq", scatter_dimension=1, tiled=True
        ).astype(jnp.float32),
        lax.psum_scatter(
            gate_bias_grad.astype(jnp.bfloat16), "seq", scatter_dimension=1, tiled=True
        ).astype(jnp.float32),
        lax.psum_scatter(
            in_grad.astype(jnp.bfloat16), "seq", scatter_dimension=2, tiled=True
        ).astype(jnp.float32),
        lax.psum_scatter(
            grad_dec.astype(jnp.bfloat16), "seq", scatter_dimension=1, tiled=True
        ).astype(jnp.float32),
    )
    loss_sum, hidden_sq, logit_sq, dec_bias_grad, embed_grad = lax.psum(
        (loss_part, hidden_sq_part, logit_sq_part, dec_bias_part, embed_part), ("seq", "mp")
    )
    embed_wide = embed.astype(jnp.float32)
    rms_embed = jnp.sqrt(jnp.mean(embed_wide * embed_wide, axis=(1, 2)))
    rms_hidden = jnp.sqrt(hidden_sq / (all_units * live_total))
    rms_logits = jnp.sqrt(logit_sq / (letter_count * count / 2.0))
    return (
        loss_sum / count,
        hidden_grad,
        cell_grad,
        embed_grad,
        in_part,
        rec_part,
        bias_part,
        dec_part,
        dec_bias_grad,
        rms_embed,
        rms_hidden,
        rms_logits,
    )


def solution(mesh):
    in_specs = (
        P("seq", None),
        P(),
        P(),
        P(None, "seq", "mp"),
        P(None, "seq", "mp"),
        P(),
        P(None, None, "mp"),
        P(None, None, "mp"),
        P(None, "mp"),
        P(None, "mp", None),
        P(),
    )
    out_specs = (
        P(),
        P(None, "seq", "mp"),
        P(None, "seq", "mp"),
        P(),
        P(None, None, ("mp", "seq")),
        P(None, "seq", "mp"),
        P(None, ("mp", "seq")),
        P(None, ("mp", "seq"), None),
        P(),
        P(),
        P(),
        P(),
    )
    return jax.shard_map(
        per_device, mesh=mesh, in_specs=in_specs, out_specs=out_specs, check_vma=False
    )
```

profile of v0, /device:TPU:0, one launch (start us, length us, event | category | flops | bytes accessed | tf_op | source)
XLA Modules:
  0.0 3547.0 jit_solution(18025429574799147192)
XLA Ops:
  35.5 22.1 copy.205
  65.9 362.8 %all-to-all-done = bf16[4,1024,2,1024]{3,0,2,1:T(4,128)(2,1)} async-done(((bf16[4,1024,2,1024]{3,0,2,1:T(4,128)(2,1)}), bf16[4,1024,2,1024]{3,0,2,1:T(4,128)(2,1)}, u32[]{:S(2)}, u32[]{:S(2)}) %all-to-all-start) | async-done | bytes 16777248 | tf_op jit(solution)/shard_map/all_to_all | solution.py:54
  446.4 767.4 %while.41 = (s32[]{:T(128)}, bf16[2,256,256]{2,1,0:T(8,128)(2,1)S(1)}, f32[2,256,256]{2,1,0:T(8,128)S(1)}, bf16[16,2,256,256]{2,3,0,1:T(8,128)(2,1)}, f32[16,2,2...) while((s32[]{:T(128)}, ...), condition=%wide.region_1.2_spmd, body=%wide.region_0.1_spmd.sunk | while | flops 2152858624 | bytes 51395484 | solution.py:80
  842.4 19.1 all-gather.8.cloned.1.call-done
  1217.0 98.0 %all_to_all.60 = bf16[16,256,2,256]{3,1,2,0:T(8,128)(2,1)S(1)} all-to-all(bf16[16,256,2,256]{3,1,2,0:T(8,128)(2,1)S(1)} %pad_maximum_fusion.1), channel_id=1, replica_groups=mesh['seq'=4,'mp'=8] {'seq'}, dimensions={0} | all-to-all | bytes 8388608 | tf_op jit(solution)/shard_map/all_to_all | solution.py:89
  1323.1 49.4 %reduce-scatter.9.cloned.1.call-done = bf16[512,2,275]{0,2,1:T(8,128)(2,1)} async-done(((bf16[4096,2,275]{0,2,1:T(8,128)(2,1)}), bf16[512,2,275]{0,2,1:T(8,128)(2,1)}) %reduce-scatter.9.cloned.1.call-update) | async-done | bytes 563216 | tf_op jit(solution)/shard_map/reduce_scatter | solution.py:95
  1379.7 39.1 %all-gather.4.cloned.1.call-done = bf16[4096,2,275]{0,2,1:T(8,128)(2,1)} async-done(((bf16[512,2,275]{0,2,1:T(8,128)(2,1)}), bf16[4096,2,275]{0,2,1:T(8,128)(2,1)}) %all-gather.4.cloned.1.call-update) | async-done | bytes 4505616 | tf_op jit(solution)/shard_map/all_gather | solution.py:131
  1434.3 93.9 %all-to-all-done.2 = bf16[4,1024,2,256]{3,0,2,1:T(4,128)(2,1)} async-done(((bf16[4,1024,2,256]{3,0,2,1:T(4,128)(2,1)}), bf16[4,1024,2,256]{3,0,2,1:T(4,128)(2,1)}, u32[]{:S(2)}, u32[]{:S(2)}) %all-to-all-start.2) | async-done | bytes 4194336 | tf_op jit(solution)/shard_map/all_to_all | solution.py:134
  1548.0 1216.9 %while.42 = (s32[]{:T(128)}, f32[2,256,256]{2,1,0:T(8,128)}, f32[2,256,256]{2,1,0:T(8,128)}, bf16[16,2,256,1024]{2,1,3,0:T(2,128)(2,1)}, s32[16]{0:T(128)}, /*in...) while((s32[]{:T(128)}, f32[2,256,256]{2,1,0:T(8,128)}, ...), condition=%wide.region_11.12_spmd.clone, body=%wide.region_9.11_spmd.clone.sunk | while | flops 2157708288 | bytes 57681272 | solution.py:173
  1582.3 37.7 %reduce-scatter.19.cloned.1.call-done = bf16[2,256,256]{2,1,0:T(8,128)(2,1)} async-done(((bf16[2,256,2048]{2,1,0:T(8,128)(2,1)}), bf16[2,256,256]{2,1,0:T(8,128)(2,1)}) %reduce-scatter.19.cloned.1.call-update) | async-done | bytes 262160 | tf_op jit(solution)/shard_map/while/body/eval_jaxpr/reduce_scatter | solution.py:167
  1656.6 39.7 %reduce-scatter.19.cloned.1.call-done = bf16[2,256,256]{2,1,0:T(8,128)(2,1)} async-done(((bf16[2,256,2048]{2,1,0:T(8,128)(2,1)}), bf16[2,256,256]{2,1,0:T(8,128)(2,1)}) %reduce-scatter.19.cloned.1.call-update) | async-done | bytes 262160 | tf_op jit(solution)/shard_map/while/body/eval_jaxpr/reduce_scatter | solution.py:167
  1732.8 39.6 %reduce-scatter.19.cloned.1.call-done = bf16[2,256,256]{2,1,0:T(8,128)(2,1)} async-done(((bf16[2,256,2048]{2,1,0:T(8,128)(2,1)}), bf16[2,256,256]{2,1,0:T(8,128)(2,1)}) %reduce-scatter.19.cloned.1.call-update) | async-done | bytes 262160 | tf_op jit(solution)/shard_map/while/body/eval_jaxpr/reduce_scatter | solution.py:167
  1809.0 39.6 %reduce-scatter.19.cloned.1.call-done = bf16[2,256,256]{2,1,0:T(8,128)(2,1)} async-done(((bf16[2,256,2048]{2,1,0:T(8,128)(2,1)}), bf16[2,256,256]{2,1,0:T(8,128)(2,1)}) %reduce-scatter.19.cloned.1.call-update) | async-done | bytes 262160 | tf_op jit(solution)/shard_map/while/body/eval_jaxpr/reduce_scatter | solution.py:167
  1885.2 39.6 %reduce-scatter.19.cloned.1.call-done = bf16[2,256,256]{2,1,0:T(8,128)(2,1)} async-done(((bf16[2,256,2048]{2,1,0:T(8,128)(2,1)}), bf16[2,256,256]{2,1,0:T(8,128)(2,1)}) %reduce-scatter.19.cloned.1.call-update) | async-done | bytes 262160 | tf_op jit(solution)/shard_map/while/body/eval_jaxpr/reduce_scatter | solution.py:167
  1961.4 39.7 %reduce-scatter.19.cloned.1.call-done = bf16[2,256,256]{2,1,0:T(8,128)(2,1)} async-done(((bf16[2,256,2048]{2,1,0:T(8,128)(2,1)}), bf16[2,256,256]{2,1,0:T(8,128)(2,1)}) %reduce-scatter.19.cloned.1.call-update) | async-done | bytes 262160 | tf_op jit(solution)/shard_map/while/body/eval_jaxpr/reduce_scatter | solution.py:167
  2037.5 39.7 %reduce-scatter.19.cloned.1.call-done = bf16[2,256,256]{2,1,0:T(8,128)(2,1)} async-done(((bf16[2,256,2048]{2,1,0:T(8,128)(2,1)}), bf16[2,256,256]{2,1,0:T(8,128)(2,1)}) %reduce-scatter.19.cloned.1.call-update) | async-done | bytes 262160 | tf_op jit(solution)/shard_map/while/body/eval_jaxpr/reduce_scatter | solution.py:167
  2113.8 39.6 %reduce-scatter.19.cloned.1.call-done = bf16[2,256,256]{2,1,0:T(8,128)(2,1)} async-done(((bf16[2,256,2048]{2,1,0:T(8,128)(2,1)}), bf16[2,256,256]{2,1,0:T(8,128)(2,1)}) %reduce-scatter.19.cloned.1.call-update) | async-done | bytes 262160 | tf_op jit(solution)/shard_map/while/body/eval_jaxpr/reduce_scatter | solution.py:167
  2190.0 39.6 %reduce-scatter.19.cloned.1.call-done = bf16[2,256,256]{2,1,0:T(8,128)(2,1)} async-done(((bf16[2,256,2048]{2,1,0:T(8,128)(2,1)}), bf16[2,256,256]{2,1,0:T(8,128)(2,1)}) %reduce-scatter.19.cloned.1.call-update) | async-done | bytes 262160 | tf_op jit(solution)/shard_map/while/body/eval_jaxpr/reduce_scatter | solution.py:167
  2266.1 39.6 %reduce-scatter.19.cloned.1.call-done = bf16[2,256,256]{2,1,0:T(8,128)(2,1)} async-done(((bf16[2,256,2048]{2,1,0:T(8,128)(2,1)}), bf16[2,256,256]{2,1,0:T(8,128)(2,1)}) %reduce-scatter.19.cloned.1.call-update) | async-done | bytes 262160 | tf_op jit(solution)/shard_map/while/body/eval_jaxpr/reduce_scatter | solution.py:167
  2342.3 39.7 %reduce-scatter.19.cloned.1.call-done = bf16[2,256,256]{2,1,0:T(8,128)(2,1)} async-done(((bf16[2,256,2048]{2,1,0:T(8,128)(2,1)}), bf16[2,256,256]{2,1,0:T(8,128)(2,1)}) %reduce-scatter.19.cloned.1.call-update) | async-done | bytes 262160 | tf_op jit(solution)/shard_map/while/body/eval_jaxpr/reduce_scatter | solution.py:167
  2418.5 39.7 %reduce-scatter.19.cloned.1.call-done = bf16[2,256,256]{2,1,0:T(8,128)(2,1)} async-done(((bf16[2,256,2048]{2,1,0:T(8,128)(2,1)}), bf16[2,256,256]{2,1,0:T(8,128)(2,1)}) %reduce-scatter.19.cloned.1.call-update) | async-done | bytes 262160 | tf_op jit(solution)/shard_map/while/body/eval_jaxpr/reduce_scatter | solution.py:167
  2494.7 39.7 %reduce-scatter.19.cloned.1.call-done = bf16[2,256,256]{2,1,0:T(8,128)(2,1)} async-done(((bf16[2,256,2048]{2,1,0:T(8,128)(2,1)}), bf16[2,256,256]{2,1,0:T(8,128)(2,1)}) %reduce-scatter.19.cloned.1.call-update) | async-done | bytes 262160 | tf_op jit(solution)/shard_map/while/body/eval_jaxpr/reduce_scatter | solution.py:167
  2570.9 39.7 %reduce-scatter.19.cloned.1.call-done = bf16[2,256,256]{2,1,0:T(8,128)(2,1)} async-done(((bf16[2,256,2048]{2,1,0:T(8,128)(2,1)}), bf16[2,256,256]{2,1,0:T(8,128)(2,1)}) %reduce-scatter.19.cloned.1.call-update) | async-done | bytes 262160 | tf_op jit(solution)/shard_map/while/body/eval_jaxpr/reduce_scatter | solution.py:167
  2647.1 39.7 %reduce-scatter.19.cloned.1.call-done = bf16[2,256,256]{2,1,0:T(8,128)(2,1)} async-done(((bf16[2,256,2048]{2,1,0:T(8,128)(2,1)}), bf16[2,256,256]{2,1,0:T(8,128)(2,1)}) %reduce-scatter.19.cloned.1.call-update) | async-done | bytes 262160 | tf_op jit(solution)/shard_map/while/body/eval_jaxpr/reduce_scatter | solution.py:167
  2723.4 39.6 %reduce-scatter.19.cloned.1.call-done = bf16[2,256,256]{2,1,0:T(8,128)(2,1)} async-done(((bf16[2,256,2048]{2,1,0:T(8,128)(2,1)}), bf16[2,256,256]{2,1,0:T(8,128)(2,1)}) %reduce-scatter.19.cloned.1.call-update) | async-done | bytes 262160 | tf_op jit(solution)/shard_map/while/body/eval_jaxpr/reduce_scatter | solution.py:167
  2765.5 41.4 %copy.217 = bf16[16,2,256,1024]{3,2,0,1:T(8,128)(2,1)} copy(bf16[16,2,256,1024]{2,1,3,0:T(2,128)(2,1)} %get-tuple-element.370) | data formatting | bytes 33554432 | tf_op jit(solution)/shard_map/while | solution.py:173
  2878.2 347.0 %all-to-all-done.3 = bf16[16,256,2,1024]{3,1,2,0:T(8,128)(2,1)} async-done(((bf16[16,256,2,1024]{3,1,2,0:T(8,128)(2,1)}), bf16[16,256,2,1024]{3,1,2,0:T(8,128)(2,1)}, u32[]{:S(2)}, u32[]{:S(2)}) %all-to-all-start.3) | async-done | bytes 16777248 | tf_op jit(solution)/shard_map/all_to_all | solution.py:184
  3251.1 42.5 %bitcast_convert_fusion = bf16[2,2048,1024]{2,1,0:T(8,128)(2,1)} fusion(bf16[16,2,256,2048]{2,3,0,1:T(8,128)(2,1)} %all-gather.6.cloned.1.call-done, bf16[16,2,256,1024]{3,2,0,1:T(8,128)(2,1)} %copy.217), kind=kOutput, calls=%fused_computation.73 | convolution fusion | flops 34363932672 | bytes 58720256 | tf_op jit(solution)/shard_map/sdbh,sdbc->dhc/dot_general | solution.py:176
  3299.7 37.5 %all-reduce = (f32[]{:T(128)}, f32[2,275]{1,0:T(2,128)}, f32[2]{0:T(128)S(1)}, f32[2]{0:T(128)S(1)}) all-reduce(f32[]{:T(128)} %get-tuple-element.605, f32[2,275]{1,0:T(2,128)S(1)} %copy-done.25, f32[2]{0:T(128)S(1)} %fusion.27, f32[2]{0:T(128)S(1)} %copy-done.26), channel_id=1, replica_groups=mesh['seq'=4,'mp'=8] {'seq','mp'}, use_global_device_ids=true, to_apply=%region_7.8 | all-reduce | flops 555 | bytes 4440 | tf_op jit(solution)/shard_map/psum | solution.py:208
  3342.1 23.3 all-reduce.3.cloned.1.call-done
  3367.2 22.2 reduce-scatter.11.cloned.1.call-done
  3391.1 143.3 %reduce-scatter.13.cloned.1.call-done = bf16[2,512,1024]{2,1,0:T(8,128)(2,1)} async-done(((bf16[2,2048,1024]{2,1,0:T(8,128)(2,1)}), bf16[2,512,1024]{2,1,0:T(8,128)(2,1)}) %reduce-scatter.13.cloned.1.call-update) | async-done | bytes 2097168 | tf_op jit(solution)/shard_map/reduce_scatter | solution.py:195
  (1040 shorter events, 1442.9 us)
Async XLA Ops:
  57.6 371.1 %all-to-all-start = ((bf16[4,1024,2,1024]{3,0,2,1:T(4,128)(2,1)}), bf16[4,1024,2,1024]{3,0,2,1:T(4,128)(2,1)}, u32[]{:S(2)}, u32[]{:S(2)}) async-start(bf16[4,1024,2,1024]{3,0,2,1:T(4,128)(2,1)} %copy.205), calls=%async_computation.1 | async-start | bytes 33554432 | tf_op jit(solution)/shard_map/all_to_all | solution.py:54
  493.6 31.5 all-gather.8.cloned.1.call-start
  733.7 31.5 all-gather.8.cloned.1.call-start
  781.8 31.5 all-gather.8.cloned.1.call-start
  926.0 31.5 all-gather.8.cloned.1.call-start
  1022.1 31.5 all-gather.8.cloned.1.call-start
  1213.8 158.7 %reduce-scatter.9.cloned.1.call-start = ((), (), s32[]{:S(2)}) async-start(), calls=%async_computation.10 | async-start | bytes 5160960 | tf_op jit(solution)/shard_map/reduce_scatter | solution.py:95
  1321.1 97.7 %all-gather.4.cloned.1.call-start = ((), (), s32[]{:S(2)}) async-start(), calls=%async_computation.11 | async-start | bytes 5160960 | tf_op jit(solution)/shard_map/all_gather | solution.py:131
  1429.2 99.0 %all-to-all-start.2 = ((bf16[4,1024,2,256]{3,0,2,1:T(4,128)(2,1)}), bf16[4,1024,2,256]{3,0,2,1:T(4,128)(2,1)}, u32[]{:S(2)}, u32[]{:S(2)}) async-start(bf16[4,1024,2,256]{3,0,2,1:T(4,128)(2,1)} %copy.214), calls=%async_computation.4 | async-start | bytes 8388608 | tf_op jit(solution)/shard_map/all_to_all | solution.py:134
  1548.0 72.1 %reduce-scatter.19.cloned.1.call-start = ((), (), s32[]{:S(2)}) async-start(), calls=%async_computation.19 | async-start | bytes 2359296 | tf_op jit(solution)/shard_map/while/body/eval_jaxpr/reduce_scatter | solution.py:167
  1622.0 74.3 %reduce-scatter.19.cloned.1.call-start = ((), (), s32[]{:S(2)}) async-start(), calls=%async_computation.19 | async-start | bytes 2359296 | tf_op jit(solution)/shard_map/while/body/eval_jaxpr/reduce_scatter | solution.py:167
  1698.1 74.3 %reduce-scatter.19.cloned.1.call-start = ((), (), s32[]{:S(2)}) async-start(), calls=%async_computation.19 | async-start | bytes 2359296 | tf_op jit(solution)/shard_map/while/body/eval_jaxpr/reduce_scatter | solution.py:167
  1774.3 74.3 %reduce-scatter.19.cloned.1.call-start = ((), (), s32[]{:S(2)}) async-start(), calls=%async_computation.19 | async-start | bytes 2359296 | tf_op jit(solution)/shard_map/while/body/eval_jaxpr/reduce_scatter | solution.py:167
  1850.5 74.3 %reduce-scatter.19.cloned.1.call-start = ((), (), s32[]{:S(2)}) async-start(), calls=%async_computation.19 | async-start | bytes 2359296 | tf_op jit(solution)/shard_map/while/body/eval_jaxpr/reduce_scatter | solution.py:167
  1926.7 74.3 %reduce-scatter.19.cloned.1.call-start = ((), (), s32[]{:S(2)}) async-start(), calls=%async_computation.19 | async-start | bytes 2359296 | tf_op jit(solution)/shard_map/while/body/eval_jaxpr/reduce_scatter | solution.py:167
  2002.9 74.3 %reduce-scatter.19.cloned.1.call-start = ((), (), s32[]{:S(2)}) async-start(), calls=%async_computation.19 | async-start | bytes 2359296 | tf_op jit(solution)/shard_map/while/body/eval_jaxpr/reduce_scatter | solution.py:167
  2079.1 74.3 %reduce-scatter.19.cloned.1.call-start = ((), (), s32[]{:S(2)}) async-start(), calls=%async_computation.19 | async-start | bytes 2359296 | tf_op jit(solution)/shard_map/while/body/eval_jaxpr/reduce_scatter | solution.py:167
  2155.3 74.3 %reduce-scatter.19.cloned.1.call-start = ((), (), s32[]{:S(2)}) async-start(), calls=%async_computation.19 | async-start | bytes 2359296 | tf_op jit(solution)/shard_map/while/body/eval_jaxpr/reduce_scatter | solution.py:167
  2231.5 74.3 %reduce-scatter.19.cloned.1.call-start = ((), (), s32[]{:S(2)}) async-start(), calls=%async_computation.19 | async-start | bytes 2359296 | tf_op jit(solution)/shard_map/while/body/eval_jaxpr/reduce_scatter | solution.py:167
  2307.7 74.3 %reduce-scatter.19.cloned.1.call-start = ((), (), s32[]{:S(2)}) async-start(), calls=%async_computation.19 | async-start | bytes 2359296 | tf_op jit(solution)/shard_map/while/body/eval_jaxpr/reduce_scatter | solution.py:167
  2383.8 74.3 %reduce-scatter.19.cloned.1.call-start = ((), (), s32[]{:S(2)}) async-start(), calls=%async_computation.19 | async-start | bytes 2359296 | tf_op jit(solution)/shard_map/while/body/eval_jaxpr/reduce_scatter | solution.py:167
  2460.0 74.3 %reduce-scatter.19.cloned.1.call-start = ((), (), s32[]{:S(2)}) async-start(), calls=%async_computation.19 | async-start | bytes 2359296 | tf_op jit(solution)/shard_map/while/body/eval_jaxpr/reduce_scatter | solution.py:167
  2536.3 74.3 %reduce-scatter.19.cloned.1.call-start = ((), (), s32[]{:S(2)}) async-start(), calls=%async_computation.19 | async-start | bytes 2359296 | tf_op jit(solution)/shard_map/while/body/eval_jaxpr/reduce_scatter | solution.py:167
  2612.5 74.3 %reduce-scatter.19.cloned.1.call-start = ((), (), s32[]{:S(2)}) async-start(), calls=%async_computation.19 | async-start | bytes 2359296 | tf_op jit(solution)/shard_map/while/body/eval_jaxpr/reduce_scatter | solution.py:167
  2688.7 74.3 %reduce-scatter.19.cloned.1.call-start = ((), (), s32[]{:S(2)}) async-start(), calls=%async_computation.19 | async-start | bytes 2359296 | tf_op jit(solution)/shard_map/while/body/eval_jaxpr/reduce_scatter | solution.py:167
  2764.9 486.2 %all-gather.6.cloned.1.call-start = ((), (), s32[]{:S(2)}) async-start(), calls=%async_computation.14 | async-start | bytes 37748736 | tf_op jit(solution)/shard_map/all_gather | solution.py:178
  2844.2 381.0 %all-to-all-start.3 = ((bf16[16,256,2,1024]{3,1,2,0:T(8,128)(2,1)}), bf16[16,256,2,1024]{3,1,2,0:T(8,128)(2,1)}, u32[]{:S(2)}, u32[]{:S(2)}) async-start(bf16[16,256,2,1024]{3,1,2,0:T(8,128)(2,1)} %copy.219), calls=%async_computation.5 | async-start | bytes 33554432 | tf_op jit(solution)/shard_map/all_to_all | solution.py:184
  2851.5 487.5 %reduce-scatter.15.cloned.1.call-start = ((), (), s32[]{:S(2)}) async-start(), calls=%async_computation.16 | async-start | bytes 491520 | tf_op jit(solution)/shard_map/reduce_scatter | solution.py:204
  2858.8 481.7 %reduce-scatter.17.cloned.1.call-start = ((), (), s32[]{:S(2)}) async-start(), calls=%async_computation.17 | async-start | bytes 327680
  2877.7 487.7 %all-reduce.3.cloned.1.call-start = ((), (), s32[]{:S(2)}) async-start(), calls=%async_computation.12 | async-start | bytes 573440 | tf_op jit(solution)/shard_map/psum | solution.py:208
  3241.6 147.9 %reduce-scatter.11.cloned.1.call-start = ((), (), s32[]{:S(2)}) async-start(), calls=%async_computation.13 | async-start | bytes 532480 | tf_op jit(solution)/shard_map/reduce_scatter | solution.py:201
  3250.8 283.6 %reduce-scatter.13.cloned.1.call-start = ((), (), s32[]{:S(2)}) async-start(), calls=%async_computation.15 | async-start | bytes 10485760 | tf_op jit(solution)/shard_map/reduce_scatter | solution.py:195
  (115 other events, 1519.3 us)
Sparse Core Ops, SparseCore 0:
  449.7 27.2 all-gather.7
  496.9 28.1 all-gather.7
  545.1 28.1 all-gather.7
  593.0 28.1 all-gather.7
  640.9 28.1 all-gather.7
  688.8 28.1 all-gather.7
  737.0 28.1 all-gather.7
  785.1 28.1 all-gather.7
  833.3 28.1 all-gather.7
  881.1 28.1 all-gather.7
  929.3 28.1 all-gather.7
  977.2 28.1 all-gather.7
  1025.4 28.1 all-gather.7
  1073.3 28.1 all-gather.7
  1121.2 28.1 all-gather.7
  1169.0 28.1 all-gather.7
  1580.7 39.3 reduce-scatter.18
  1655.0 41.2 reduce-scatter.18
  1731.2 41.2 reduce-scatter.18
  1807.4 41.2 reduce-scatter.18
  1883.6 41.2 reduce-scatter.18
  1959.8 41.2 reduce-scatter.18
  2036.0 41.2 reduce-scatter.18
  2112.2 41.2 reduce-scatter.18
  2188.3 41.2 reduce-scatter.18
  2264.5 41.2 reduce-scatter.18
  2340.7 41.2 reduce-scatter.18
  2416.9 41.2 reduce-scatter.18
  2493.1 41.2 reduce-scatter.18
  2569.3 41.2 reduce-scatter.18
  2645.5 41.2 reduce-scatter.18
  2721.7 41.2 reduce-scatter.18
Sparse Core Ops, SparseCore 1:
  1321.2 51.3 reduce-scatter.8
  1379.8 38.9 all-gather.3
  2767.8 160.6 all-gather.5
  2930.8 28.1 reduce-scatter.14
  2961.9 191.8 reduce-scatter.16
  3241.7 123.7 all-reduce.2
  3367.7 21.7 reduce-scatter.10
  3391.7 142.7 reduce-scatter.12
where the time goes:
time: 3560 us; the launch traced here: 3550 us
  waiting for transfers between devices  2020 us (57%)
  local copies, waits for them, and re-layouts  670 us (19%)
  matrix products  324 us (9%)
  other arithmetic  243 us (7%)
  blocking collectives  135 us (4%)
  loops' own time  111 us (3%)
    reduce_scatter x16, waiting for transfers between devices, backward_step(): lax.psum_scatter(terms.astype(jnp.bfloat16), 'mp', scatter_dimension=2, t...  633 us
    all_to_all x1, waiting for transfers between devices, per_device(): lax.all_to_all(gates_in, 'seq', split_axis=1, concat_axis=0, tiled=True)  363 us
    all_to_all x1, waiting for transfers between devices, per_device(): lax.all_to_all(grad_time, 'seq', split_axis=0, concat_axis=1, tiled=True)  347 us
    all_gather x16, waiting for transfers between devices, forward_step(): whole = lax.all_gather(hidden, 'mp', axis=2, tiled=True)  302 us
    reduce_scatter x1, waiting for transfers between devices, per_device(): lax.psum_scatter(rec_grad.astype(jnp.bfloat16), 'seq', scatter_dimension=...  143 us
    dot_general x16, matrix products, forward_step(): jnp.einsum('dbh,dhc->dbc', whole, w_rec, preferred_element_type=jnp.float32)  124 us
    dot_general x16, matrix products, backward_step(): jnp.einsum('dbc,dhc->dbh', grad_pre, w_rec, preferred_element_type=jnp.fl...  115 us
    all_to_all x1, blocking collectives, per_device(): lax.all_to_all(time_hidden, 'seq', split_axis=0, concat_axis=1, tiled=True)  98 us
  transfers between devices with their start and end apart: 45, of which 40 were waited for; matrix products, arithmetic and copies ran while one was open for 10% of the time, Pallas kernels for 0%

commit v1 on v0

v1 whole, which is shorter than its diff:
```python
import jax
import jax.numpy as jnp
from jax import lax
from jax.sharding import PartitionSpec as P


def column_order(own_units):
    lanes = min(128, own_units)
    source = jnp.arange(4 * lanes, dtype=jnp.int32)
    place = (source % 4) * lanes + source // 4
    matrix = (place[:, None] == jnp.arange(4 * lanes, dtype=jnp.int32)[None, :]).astype(jnp.bfloat16)
    return lanes, matrix


def grouped(x, matrix):
    width = matrix.shape[0]
    parts = x.reshape(x.shape[:-1] + (x.shape[-1] // width, width))
    out = jnp.einsum("...gc,cp->...gp", parts, matrix, preferred_element_type=jnp.float32)
    return out.astype(x.dtype).reshape(x.shape)


def ungrouped(x, matrix):
    return grouped(x, matrix.T)


def ungrouped_wide(x, lanes):
    parts = x.reshape(x.shape[:-1] + (x.shape[-1] // (4 * lanes), 4, lanes))
    return jnp.swapaxes(parts, -1, -2).reshape(x.shape)


def gates_of(pre, lanes):
    parts = pre.reshape(pre.shape[:-1] + (pre.shape[-1] // (4 * lanes), 4, lanes))
    flat = pre.shape[:-1] + (pre.shape[-1] // 4,)
    return tuple(parts[..., k, :].reshape(flat) for k in range(4))


def joined_gates(gates, lanes):
    split = [g.reshape(g.shape[:-1] + (g.shape[-1] // lanes, 1, lanes)) for g in gates]
    joined = jnp.concatenate(split, axis=-2)
    return joined.reshape(gates[0].shape[:-1] + (4 * gates[0].shape[-1],))


def recurrences(step_ids, own_len, h_init, c_init, embed, w_in, w_rec, bias, w_dec, wd_full, b_dec, count, lanes):
    length, per_dev = step_ids.shape[1:]
    letter_count = embed.shape[1]
    steps = jnp.arange(length, dtype=jnp.int32)
    live_steps = jnp.stack(
        [steps[:, None] < own_len[None, :], (length - 1 - steps)[:, None] < own_len[None, :]], axis=1
    )[..., None]
    letters = jnp.arange(letter_count, dtype=jnp.int32)
    onehot = (jnp.swapaxes(step_ids, 0, 1)[..., None] == letters).astype(jnp.bfloat16)
    letter_rows = jnp.einsum(
        "sdbv,dve->sdbe", onehot, embed, preferred_element_type=jnp.float32
    ).astype(jnp.bfloat16)
    gates_in = jnp.einsum(
        "sdbe,dec->sdbc", letter_rows, w_in, preferred_element_type=jnp.float32
    ).astype(jnp.bfloat16)

    def forward_step(carry, inputs):
        hidden, cell = carry
        gate_in, live = inputs
        whole = lax.all_gather(hidden, "mp", axis=2, tiled=True)
        recurrent = jnp.einsum("dbh,dhc->dbc", whole, w_rec, preferred_element_type=jnp.float32)
        pre = gate_in.astype(jnp.float32) + recurrent + bias[:, None]
        in_pre, forget_pre, cell_pre, out_pre = gates_of(pre, lanes)
        in_gate, forget, out_gate = (jax.nn.sigmoid(x) for x in (in_pre, forget_pre, out_pre))
        cell_gate = jnp.tanh(cell_pre)
        new_cell = forget * cell + in_gate * cell_gate
        cell_next = jnp.where(live, new_cell, cell)
        hidden_next = jnp.where(
            live, out_gate * jnp.tanh(new_cell), hidden.astype(jnp.float32)
        ).astype(jnp.bfloat16)
        return ((hidden_next, cell_next), (whole, cell, in_gate, forget, cell_gate, out_gate))

    (last_hidden, last_cell), (wholes, cells, *gates) = lax.scan(
        forward_step, (h_init, c_init), (gates_in, live_steps)
    )
    last_whole = lax.all_gather(last_hidden, "mp", axis=2, tiled=True)
    after = jnp.concatenate([wholes[1:], last_whole[None]], axis=0)
    own = h_init.shape[2]
    mine = lax.dynamic_slice_in_dim(after, lax.axis_index("mp") * own, own, axis=3)
    mine_wide = mine.astype(jnp.float32)
    hidden_sq = jnp.sum(jnp.where(live_steps, mine_wide * mine_wide, 0.0), axis=(0, 2, 3))
    logits = (
        jnp.einsum("sdbh,dhv->sdbv", after, wd_full, preferred_element_type=jnp.float32) + b_dec[None, :, None]
    )
    targets = jnp.swapaxes(jnp.concatenate([step_ids[:, 1:], step_ids[:, :1]], axis=1), 0, 1)
    fore_valid = (steps[:, None] + 1 < own_len[None, :])
    back_valid = (steps[:, None] < length - 1) & ((length - 1 - steps)[:, None] < own_len[None, :])
    valid = jnp.stack([fore_valid, back_valid], axis=1).astype(jnp.float32)
    logit_sq = jnp.sum(valid[..., None] * logits * logits, axis=(0, 2, 3))
    top = jnp.max(logits, axis=-1, keepdims=True)
    log_total = top + jnp.log(jnp.sum(jnp.exp(logits - top), axis=-1, keepdims=True))
    target_hot = targets[..., None] == letters
    picked = jnp.sum(jnp.where(target_hot, logits, 0.0), axis=-1)
    loss = jnp.sum(valid * (log_total[..., 0] - picked))
    grad_logits = (
        valid[..., None] * (jnp.exp(logits - log_total) - target_hot.astype(jnp.float32)) / count
    ).astype(jnp.bfloat16)
    dec_bias = jnp.sum(grad_logits.astype(jnp.float32), axis=(0, 2))
    dec_grad = jnp.einsum("sdbh,sdbv->dhv", mine, grad_logits, preferred_element_type=jnp.float32)

    def backward_step(carry, inputs):
        grad_hidden, grad_cell = carry
        live, cell, in_gate, forget, cell_gate, out_gate, grad_logit = inputs
        grad_hidden = grad_hidden + jnp.einsum(
            "dbv,dhv->dbh", grad_logit, w_dec, preferred_element_type=jnp.float32
        )
        squash = jnp.tanh(forget * cell + in_gate * cell_gate)
        grad_new = jnp.where(live, grad_cell + grad_hidden * out_gate * (1.0 - squash * squash), 0.0)
        grad_out = jnp.where(live, grad_hidden * squash, 0.0)
        grad_pre = joined_gates(
            [
                grad_new * cell_gate * in_gate * (1.0 - in_gate),
                grad_new * cell * forget * (1.0 - forget),
                grad_new * in_gate * (1.0 - cell_gate * cell_gate),
                grad_out * out_gate * (1.0 - out_gate),
            ],
            lanes,
        ).astype(jnp.bfloat16)
        grad_cell_prev = grad_new * forget + jnp.where(live, 0.0, grad_cell)
        held = jnp.where(live, 0.0, grad_hidden)
        terms = jnp.einsum("dbc,dhc->dbh", grad_pre, w_rec, preferred_element_type=jnp.float32)
        through = lax.psum_scatter(
            terms.astype(jnp.bfloat16), "mp", scatter_dimension=2, tiled=True
        ).astype(jnp.float32)
        return ((held + through, grad_cell_prev), grad_pre)

    start = jnp.zeros(c_init.shape, jnp.float32)
    (hidden_grad, cell_grad), grad_pres = lax.scan(
        backward_step, (start, start), (live_steps, cells, *gates, grad_logits), reverse=True
    )
    rec_grad = jnp.einsum("sdbh,sdbc->dhc", wholes, grad_pres, preferred_element_type=jnp.float32)
    letter_grad = jnp.einsum("sdbv,sdbc->dvc", onehot, grad_pres, preferred_element_type=jnp.float32)
    return loss, hidden_sq, logit_sq, dec_bias, dec_grad, hidden_grad, cell_grad, rec_grad, letter_grad


def per_device(ids, lengths, order, h_init, c_init, embed, w_in, w_rec, bias, w_dec, b_dec):
    seq_rank = lax.axis_index("seq")
    first_mp = (lax.axis_index("mp") == 0).astype(jnp.float32)
    streams = ids.shape[1]
    per_dev = h_init.shape[1]
    own_units, all_units = h_init.shape[2], w_rec.shape[1]
    letter_count = embed.shape[1]
    wd_full = lax.all_gather(w_dec, "mp", axis=1, tiled=True)
    whole_ids = lax.all_gather(ids, "seq", axis=0, tiled=True)
    own_order = lax.dynamic_slice_in_dim(order, seq_rank * per_dev, per_dev)
    slot_ids = jnp.take(whole_ids, own_order, axis=1)
    own_len = jnp.take(lengths, own_order)
    live_total = jnp.sum(lengths).astype(jnp.float32)
    count = 2.0 * (jnp.sum(lengths) - streams).astype(jnp.float32)
    step_ids = jnp.stack([slot_ids, jnp.flip(slot_ids, 0)])
    lanes, matrix = column_order(own_units)
    w_rec_grouped = grouped(w_rec, matrix)
    w_in_grouped = grouped(w_in, matrix)
    bias_grouped = jnp.swapaxes(
        bias.reshape(2, own_units // lanes, lanes, 4), -1, -2
    ).reshape(bias.shape)
    loss, hidden_sq, logit_sq, dec_bias, dec_grad, hidden_grad, cell_grad, rec_grad, letter_grad = recurrences(
        step_ids, own_len, h_init, c_init, embed, w_in_grouped, w_rec_grouped, bias_grouped, w_dec, wd_full,
        b_dec, count, lanes,
    )
    embed_wide = embed.astype(jnp.float32)
    in_grad = jnp.einsum("dve,dvc->dec", embed_wide, letter_grad, precision=lax.Precision.HIGHEST)
    bias_grad = jnp.sum(letter_grad, axis=1, keepdims=True)
    embed_part = jnp.einsum(
        "dvc,dec->dve", letter_grad, w_in_grouped.astype(jnp.float32), precision=lax.Precision.HIGHEST
    )
    edge = ungrouped_wide(jnp.concatenate([in_grad, bias_grad], axis=1), lanes)
    rec_part = lax.psum_scatter(rec_grad.astype(jnp.bfloat16), "seq", scatter_dimension=1, tiled=True)
    edge_part = lax.psum_scatter(edge.astype(jnp.bfloat16), "seq", scatter_dimension=2, tiled=True)
    dec_part = lax.psum_scatter(dec_grad.astype(jnp.bfloat16), "seq", scatter_dimension=1, tiled=True)
    loss_sum, hidden_all, logit_all, dec_bias_grad, embed_grad = lax.psum(
        (loss * first_mp, hidden_sq, logit_sq * first_mp, dec_bias * first_mp, embed_part), ("seq", "mp")
    )
    rec_out = ungrouped(rec_part, matrix).astype(jnp.float32)
    rms_embed = jnp.sqrt(jnp.mean(embed_wide * embed_wide, axis=(1, 2)))
    return (
        loss_sum / count,
        hidden_grad,
        cell_grad,
        embed_grad,
        edge_part[:, :-1].astype(jnp.float32),
        rec_out,
        edge_part[:, -1].astype(jnp.float32),
        dec_part.astype(jnp.float32),
        dec_bias_grad,
        rms_embed,
        jnp.sqrt(hidden_all / (all_units * live_total)),
        jnp.sqrt(logit_all / (letter_count * count / 2.0)),
    )


def solution(mesh):
    in_specs = (
        P("seq", None),
        P(),
        P(),
        P(None, "seq", "mp"),
        P(None, "seq", "mp"),
        P(),
        P(None, None, "mp"),
        P(None, None, "mp"),
        P(None, "mp"),
        P(None, "mp", None),
        P(),
    )
    out_specs = (
        P(),
        P(None, "seq", "mp"),
        P(None, "seq", "mp"),
        P(),
        P(None, None, ("mp", "seq")),
        P(None, "seq", "mp"),
        P(None, ("mp", "seq")),
        P(None, ("mp", "seq"), None),
        P(),
        P(),
        P(),
        P(),
    )
    return jax.shard_map(
        per_device, mesh=mesh, in_specs=in_specs, out_specs=out_specs, check_vma=False
    )
```

time: 3560 us -> 2790 us (0.78)
  waiting for transfers between devices: 2020 us -> 1300 us
  other arithmetic: 243 us -> 398 us
  loops' own time: 111 us -> 3.74 us
  blocking collectives: 135 us -> 54.8 us
    all_to_all x3 -> x0, waiting for transfers between devices: 804 us -> none  [the longest x1 363 us: per_device(): lax.all_to_all(gates_in, 'seq', split_axis=1, concat_axis=0, tiled=True)]
    div x0 -> x96, local copies, waits for them, and re-layouts: none -> 173 us  [forward_step(): jax.nn.sigmoid(x)]
    div x0 -> x16, other arithmetic: none -> 170 us  [forward_step(): jax.nn.sigmoid(x)]
    all_gather x16, waiting for transfers between devices: 302 us -> 450 us  [forward_step(): whole = lax.all_gather(hidden, 'mp', axis=2, tiled=True)]
    tanh x0 -> x16, other arithmetic: none -> 133 us  [forward_step(): cell_gate = jnp.tanh(cell_pre)]
    another operation x2, loops' own time: 111 us -> 3.74 us  [the longest x1 2.11 us: recurrences(): lax.scan(backward_step, (start, start), (live_steps, cells, *gates, grad_...]
    all_to_all x1 -> x0, blocking collectives: 98 us -> none  [per_device(): lax.all_to_all(time_hidden, 'seq', split_axis=0, concat_axis=1, tiled=True)]
    while x289 -> x164, local copies, waits for them, and re-layouts: 129 us -> 46.7 us  [the longest x4 35.4 us: recurrences(): lax.scan(forward_step, (h_init, c_init), (gates_in, live_steps))]
  transfers between devices with their start and end apart: 45 -> 38, of which waited for: 40 -> 37; matrix products, arithmetic and copies ran while one was open for 10% -> 7% of each run, Pallas kernels for 0% -> 0%
where the time goes in v1:
time: 2790 us; the launch traced here: 2770 us
  waiting for transfers between devices  1300 us (47%)
  local copies, waits for them, and re-layouts  638 us (23%)
  other arithmetic  398 us (14%)
  matrix products  358 us (13%)
  blocking collectives  54.8 us (2%)
    reduce_scatter x16, waiting for transfers between devices, backward_step(): lax.psum_scatter(terms.astype(jnp.bfloat16), 'mp', scatter_dimension=2, t...  633 us
    all_gather x16, waiting for transfers between devices, forward_step(): whole = lax.all_gather(hidden, 'mp', axis=2, tiled=True)  450 us
    div x96, local copies, waits for them, and re-layouts, forward_step(): jax.nn.sigmoid(x)  173 us
    div x16, other arithmetic, forward_step(): jax.nn.sigmoid(x)  170 us
    reduce_scatter x1, waiting for transfers between devices, per_device(): lax.psum_scatter(rec_grad.astype(jnp.bfloat16), 'seq', scatter_dimension=...  142 us
    tanh x16, other arithmetic, forward_step(): cell_gate = jnp.tanh(cell_pre)  133 us
    dot_general x16, matrix products, backward_step(): jnp.einsum('dbc,dhc->dbh', grad_pre, w_rec, preferred_element_type=jnp.fl...  113 us
    dynamic_update_slice x64, local copies, waits for them, and re-layouts, recurrences(): lax.scan(forward_step, (h_init, c_init), (gates_in, live_steps))  110 us
  transfers between devices with their start and end apart: 38, of which 37 were waited for; matrix products, arithmetic and copies ran while one was open for 7% of the time, Pallas kernels for 0%

profile of v1, /device:TPU:0, one launch (start us, length us, event | category | flops | bytes accessed | tf_op | source)
XLA Modules:
  0.0 2771.6 jit_solution(1599841801548186822)
XLA Ops:
  63.6 1312.1 %while.45 = (s32[]{:T(128)}, bf16[2,256,256]{2,1,0:T(8,128)(2,1)S(1)}, f32[2,256,256]{2,1,0:T(8,128)S(1)}, bf16[16,2,256,2048]{3,2,1,0:T(8,128)(2,1)}, f32[16,2,...) while((s32[]{:T(128)}, ...), condition=%wide.wide.region_1.2_spmd, body=%wide.wide.region_0.1_spmd.sunk | while | flops 2151284736 | bytes 70526840 | solution.py:75
  67.3 29.3 %all-gather.9.cloned.1.call-done = bf16[2,256,2048]{2,1,0:T(8,128)(2,1)} async-done(((bf16[2,256,256]{2,1,0:T(8,128)(2,1)}), bf16[2,256,2048]{2,1,0:T(8,128)(2,1)}) %all-gather.9.cloned.1.call-update) | async-done | bytes 2097168 | tf_op jit(solution)/shard_map/while/body/eval_jaxpr/all_gather | solution.py:62
  150.5 28.2 %all-gather.9.cloned.1.call-done = bf16[2,256,2048]{2,1,0:T(8,128)(2,1)} async-done(((bf16[2,256,256]{2,1,0:T(8,128)(2,1)}), bf16[2,256,2048]{2,1,0:T(8,128)(2,1)}) %all-gather.9.cloned.1.call-update) | async-done | bytes 2097168 | tf_op jit(solution)/shard_map/while/body/eval_jaxpr/all_gather | solution.py:62
  232.6 28.2 %all-gather.9.cloned.1.call-done = bf16[2,256,2048]{2,1,0:T(8,128)(2,1)} async-done(((bf16[2,256,256]{2,1,0:T(8,128)(2,1)}), bf16[2,256,2048]{2,1,0:T(8,128)(2,1)}) %all-gather.9.cloned.1.call-update) | async-done | bytes 2097168 | tf_op jit(solution)/shard_map/while/body/eval_jaxpr/all_gather | solution.py:62
  396.4 27.9 %all-gather.9.cloned.1.call-done = bf16[2,256,2048]{2,1,0:T(8,128)(2,1)} async-done(((bf16[2,256,256]{2,1,0:T(8,128)(2,1)}), bf16[2,256,2048]{2,1,0:T(8,128)(2,1)}) %all-gather.9.cloned.1.call-update) | async-done | bytes 2097168 | tf_op jit(solution)/shard_map/while/body/eval_jaxpr/all_gather | solution.py:62
  478.2 27.9 %all-gather.9.cloned.1.call-done = bf16[2,256,2048]{2,1,0:T(8,128)(2,1)} async-done(((bf16[2,256,256]{2,1,0:T(8,128)(2,1)}), bf16[2,256,2048]{2,1,0:T(8,128)(2,1)}) %all-gather.9.cloned.1.call-update) | async-done | bytes 2097168 | tf_op jit(solution)/shard_map/while/body/eval_jaxpr/all_gather | solution.py:62
  559.9 28.2 %all-gather.9.cloned.1.call-done = bf16[2,256,2048]{2,1,0:T(8,128)(2,1)} async-done(((bf16[2,256,256]{2,1,0:T(8,128)(2,1)}), bf16[2,256,2048]{2,1,0:T(8,128)(2,1)}) %all-gather.9.cloned.1.call-update) | async-done | bytes 2097168 | tf_op jit(solution)/shard_map/while/body/eval_jaxpr/all_gather | solution.py:62
  641.9 28.2 %all-gather.9.cloned.1.call-done = bf16[2,256,2048]{2,1,0:T(8,128)(2,1)} async-done(((bf16[2,256,256]{2,1,0:T(8,128)(2,1)}), bf16[2,256,2048]{2,1,0:T(8,128)(2,1)}) %all-gather.9.cloned.1.call-update) | async-done | bytes 2097168 | tf_op jit(solution)/shard_map/while/body/eval_jaxpr/all_gather | solution.py:62
  723.9 28.2 %all-gather.9.cloned.1.call-done = bf16[2,256,2048]{2,1,0:T(8,128)(2,1)} async-done(((bf16[2,256,256]{2,1,0:T(8,128)(2,1)}), bf16[2,256,2048]{2,1,0:T(8,128)(2,1)}) %all-gather.9.cloned.1.call-update) | async-done | bytes 2097168 | tf_op jit(solution)/shard_map/while/body/eval_jaxpr/all_gather | solution.py:62
  887.7 28.2 %all-gather.9.cloned.1.call-done = bf16[2,256,2048]{2,1,0:T(8,128)(2,1)} async-done(((bf16[2,256,256]{2,1,0:T(8,128)(2,1)}), bf16[2,256,2048]{2,1,0:T(8,128)(2,1)}) %all-gather.9.cloned.1.call-update) | async-done | bytes 2097168 | tf_op jit(solution)/shard_map/while/body/eval_jaxpr/all_gather | solution.py:62
  969.7 27.9 %all-gather.9.cloned.1.call-done = bf16[2,256,2048]{2,1,0:T(8,128)(2,1)} async-done(((bf16[2,256,256]{2,1,0:T(8,128)(2,1)}), bf16[2,256,2048]{2,1,0:T(8,128)(2,1)}) %all-gather.9.cloned.1.call-update) | async-done | bytes 2097168 | tf_op jit(solution)/shard_map/while/body/eval_jaxpr/all_gather | solution.py:62
  1051.5 28.2 %all-gather.9.cloned.1.call-done = bf16[2,256,2048]{2,1,0:T(8,128)(2,1)} async-done(((bf16[2,256,256]{2,1,0:T(8,128)(2,1)}), bf16[2,256,2048]{2,1,0:T(8,128)(2,1)}) %all-gather.9.cloned.1.call-update) | async-done | bytes 2097168 | tf_op jit(solution)/shard_map/while/body/eval_jaxpr/all_gather | solution.py:62
  1470.3 954.0 %while.44 = (s32[]{:T(128)}, f32[2,256,256]{1,2,0:T(8,128)}, f32[2,256,256]{1,2,0:T(8,128)}, bf16[16,2,256,1024]{3,2,1,0:T(8,128)(2,1)}, pred[16,2,256,1]{2,1,3,...) while((s32[]{:T(128)}, f32[2,256,256]{1,2,0:T(8,128)}, ...), condition=%wide.region_10.11_spmd.clone, body=%wide.region_8.10_spmd.clone.sunk | while | flops 2227306496 | bytes 52475628 | solution.py:130
  1488.5 39.5 %reduce-scatter.11.cloned.1.call-done = bf16[2,256,256]{1,2,0:T(8,128)(2,1)} async-done(((bf16[2,256,2048]{1,2,0:T(8,128)(2,1)}), bf16[2,256,256]{1,2,0:T(8,128)(2,1)}) %reduce-scatter.11.cloned.1.call-update) | async-done | bytes 262160 | tf_op jit(solution)/shard_map/while/body/eval_jaxpr/reduce_scatter | solution.py:124
  1548.2 39.5 %reduce-scatter.11.cloned.1.call-done = bf16[2,256,256]{1,2,0:T(8,128)(2,1)} async-done(((bf16[2,256,2048]{1,2,0:T(8,128)(2,1)}), bf16[2,256,256]{1,2,0:T(8,128)(2,1)}) %reduce-scatter.11.cloned.1.call-update) | async-done | bytes 262160 | tf_op jit(solution)/shard_map/while/body/eval_jaxpr/reduce_scatter | solution.py:124
  1607.8 39.5 %reduce-scatter.11.cloned.1.call-done = bf16[2,256,256]{1,2,0:T(8,128)(2,1)} async-done(((bf16[2,256,2048]{1,2,0:T(8,128)(2,1)}), bf16[2,256,256]{1,2,0:T(8,128)(2,1)}) %reduce-scatter.11.cloned.1.call-update) | async-done | bytes 262160 | tf_op jit(solution)/shard_map/while/body/eval_jaxpr/reduce_scatter | solution.py:124
  1667.4 39.6 %reduce-scatter.11.cloned.1.call-done = bf16[2,256,256]{1,2,0:T(8,128)(2,1)} async-done(((bf16[2,256,2048]{1,2,0:T(8,128)(2,1)}), bf16[2,256,256]{1,2,0:T(8,128)(2,1)}) %reduce-scatter.11.cloned.1.call-update) | async-done | bytes 262160 | tf_op jit(solution)/shard_map/while/body/eval_jaxpr/reduce_scatter | solution.py:124
  1727.0 39.6 %reduce-scatter.11.cloned.1.call-done = bf16[2,256,256]{1,2,0:T(8,128)(2,1)} async-done(((bf16[2,256,2048]{1,2,0:T(8,128)(2,1)}), bf16[2,256,256]{1,2,0:T(8,128)(2,1)}) %reduce-scatter.11.cloned.1.call-update) | async-done | bytes 262160 | tf_op jit(solution)/shard_map/while/body/eval_jaxpr/reduce_scatter | solution.py:124
  1786.7 39.5 %reduce-scatter.11.cloned.1.call-done = bf16[2,256,256]{1,2,0:T(8,128)(2,1)} async-done(((bf16[2,256,2048]{1,2,0:T(8,128)(2,1)}), bf16[2,256,256]{1,2,0:T(8,128)(2,1)}) %reduce-scatter.11.cloned.1.call-update) | async-done | bytes 262160 | tf_op jit(solution)/shard_map/while/body/eval_jaxpr/reduce_scatter | solution.py:124
  1846.4 39.5 %reduce-scatter.11.cloned.1.call-done = bf16[2,256,256]{1,2,0:T(8,128)(2,1)} async-done(((bf16[2,256,2048]{1,2,0:T(8,128)(2,1)}), bf16[2,256,256]{1,2,0:T(8,128)(2,1)}) %reduce-scatter.11.cloned.1.call-update) | async-done | bytes 262160 | tf_op jit(solution)/shard_map/while/body/eval_jaxpr/reduce_scatter | solution.py:124
  1905.9 39.6 %reduce-scatter.11.cloned.1.call-done = bf16[2,256,256]{1,2,0:T(8,128)(2,1)} async-done(((bf16[2,256,2048]{1,2,0:T(8,128)(2,1)}), bf16[2,256,256]{1,2,0:T(8,128)(2,1)}) %reduce-scatter.11.cloned.1.call-update) | async-done | bytes 262160 | tf_op jit(solution)/shard_map/while/body/eval_jaxpr/reduce_scatter | solution.py:124
  1965.6 39.5 %reduce-scatter.11.cloned.1.call-done = bf16[2,256,256]{1,2,0:T(8,128)(2,1)} async-done(((bf16[2,256,2048]{1,2,0:T(8,128)(2,1)}), bf16[2,256,256]{1,2,0:T(8,128)(2,1)}) %reduce-scatter.11.cloned.1.call-update) | async-done | bytes 262160 | tf_op jit(solution)/shard_map/while/body/eval_jaxpr/reduce_scatter | solution.py:124
  2025.2 39.5 %reduce-scatter.11.cloned.1.call-done = bf16[2,256,256]{1,2,0:T(8,128)(2,1)} async-done(((bf16[2,256,2048]{1,2,0:T(8,128)(2,1)}), bf16[2,256,256]{1,2,0:T(8,128)(2,1)}) %reduce-scatter.11.cloned.1.call-update) | async-done | bytes 262160 | tf_op jit(solution)/shard_map/while/body/eval_jaxpr/reduce_scatter | solution.py:124
  2084.8 39.6 %reduce-scatter.11.cloned.1.call-done = bf16[2,256,256]{1,2,0:T(8,128)(2,1)} async-done(((bf16[2,256,2048]{1,2,0:T(8,128)(2,1)}), bf16[2,256,256]{1,2,0:T(8,128)(2,1)}) %reduce-scatter.11.cloned.1.call-update) | async-done | bytes 262160 | tf_op jit(solution)/shard_map/while/body/eval_jaxpr/reduce_scatter | solution.py:124
  2144.5 39.5 %reduce-scatter.11.cloned.1.call-done = bf16[2,256,256]{1,2,0:T(8,128)(2,1)} async-done(((bf16[2,256,2048]{1,2,0:T(8,128)(2,1)}), bf16[2,256,256]{1,2,0:T(8,128)(2,1)}) %reduce-scatter.11.cloned.1.call-update) | async-done | bytes 262160 | tf_op jit(solution)/shard_map/while/body/eval_jaxpr/reduce_scatter | solution.py:124
  2204.1 39.5 %reduce-scatter.11.cloned.1.call-done = bf16[2,256,256]{1,2,0:T(8,128)(2,1)} async-done(((bf16[2,256,2048]{1,2,0:T(8,128)(2,1)}), bf16[2,256,256]{1,2,0:T(8,128)(2,1)}) %reduce-scatter.11.cloned.1.call-update) | async-done | bytes 262160 | tf_op jit(solution)/shard_map/while/body/eval_jaxpr/reduce_scatter | solution.py:124
  2263.7 39.6 %reduce-scatter.11.cloned.1.call-done = bf16[2,256,256]{1,2,0:T(8,128)(2,1)} async-done(((bf16[2,256,2048]{1,2,0:T(8,128)(2,1)}), bf16[2,256,256]{1,2,0:T(8,128)(2,1)}) %reduce-scatter.11.cloned.1.call-update) | async-done | bytes 262160 | tf_op jit(solution)/shard_map/while/body/eval_jaxpr/reduce_scatter | solution.py:124
  2323.4 39.5 %reduce-scatter.11.cloned.1.call-done = bf16[2,256,256]{1,2,0:T(8,128)(2,1)} async-done(((bf16[2,256,2048]{1,2,0:T(8,128)(2,1)}), bf16[2,256,256]{1,2,0:T(8,128)(2,1)}) %reduce-scatter.11.cloned.1.call-update) | async-done | bytes 262160 | tf_op jit(solution)/shard_map/while/body/eval_jaxpr/reduce_scatter | solution.py:124
  2383.0 39.6 %reduce-scatter.11.cloned.1.call-done = bf16[2,256,256]{1,2,0:T(8,128)(2,1)} async-done(((bf16[2,256,2048]{1,2,0:T(8,128)(2,1)}), bf16[2,256,256]{1,2,0:T(8,128)(2,1)}) %reduce-scatter.11.cloned.1.call-update) | async-done | bytes 262160 | tf_op jit(solution)/shard_map/while/body/eval_jaxpr/reduce_scatter | solution.py:124
  2445.5 42.9 %bitcast_convert_fusion = bf16[2,2048,1024]{2,1,0:T(8,128)(2,1)} fusion(bf16[16,2,256,2048]{3,2,1,0:T(8,128)(2,1)} %get-tuple-element.342, bf16[16,2,256,1024]{3,2,1,0:T(8,128)(2,1)} %get-tuple-element.351), kind=kOutput, calls=%fused_computation.74 | convolution fusion | flops 34363932672 | bytes 58720256 | tf_op jit(solution)/shard_map/sdbh,sdbc->dhc/dot_general | solution.py:133
  2490.9 39.7 %all-reduce = (f32[]{:T(128)}, f32[2,275]{1,0:T(2,128)}, f32[2]{0:T(128)S(1)}, f32[2]{0:T(128)S(1)}) all-reduce(f32[]{:T(128)S(6)} %mul.239, f32[2,275]{1,0:T(2,128)S(1)} %broadcast_multiply_fusion, f32[2]{0:T(128)S(1)} %copy-done.23, f32[2]{0:T(128)S(1)} %broadcast_multiply_fusion.1), channel_id=1, replica_groups=mesh['seq'=4,'mp'=8] {'seq','mp'}, use_global_device_ids=true, to_apply=%region_6.7 | all-reduce | flops 555 | bytes 4440 | tf_op jit(solution)/shard_map/psum | solution.py:173
  2610.2 141.8 %reduce-scatter.7.cloned.1.call-done = bf16[2,512,1024]{2,1,0:T(8,128)(2,1)} async-done(((bf16[2,2048,1024]{2,1,0:T(8,128)(2,1)}), bf16[2,512,1024]{2,1,0:T(8,128)(2,1)}) %reduce-scatter.7.cloned.1.call-update) | async-done | bytes 2097168 | tf_op jit(solution)/shard_map/reduce_scatter | solution.py:170
  (991 shorter events, 1580.2 us)
Async XLA Ops:
  63.9 32.8 %all-gather.9.cloned.1.call-start = ((), (), s32[]{:S(2)}) async-start(), calls=%async_computation.11 | async-start | bytes 2359296 | tf_op jit(solution)/shard_map/while/body/eval_jaxpr/all_gather | solution.py:62
  147.1 31.7 %all-gather.9.cloned.1.call-start = ((), (), s32[]{:S(2)}) async-start(), calls=%async_computation.11 | async-start | bytes 2359296 | tf_op jit(solution)/shard_map/while/body/eval_jaxpr/all_gather | solution.py:62
  229.1 31.7 %all-gather.9.cloned.1.call-start = ((), (), s32[]{:S(2)}) async-start(), calls=%async_computation.11 | async-start | bytes 2359296 | tf_op jit(solution)/shard_map/while/body/eval_jaxpr/all_gather | solution.py:62
  392.9 31.4 %all-gather.9.cloned.1.call-start = ((), (), s32[]{:S(2)}) async-start(), calls=%async_computation.11 | async-start | bytes 2359296 | tf_op jit(solution)/shard_map/while/body/eval_jaxpr/all_gather | solution.py:62
  556.5 31.7 %all-gather.9.cloned.1.call-start = ((), (), s32[]{:S(2)}) async-start(), calls=%async_computation.11 | async-start | bytes 2359296 | tf_op jit(solution)/shard_map/while/body/eval_jaxpr/all_gather | solution.py:62
  638.5 31.7 %all-gather.9.cloned.1.call-start = ((), (), s32[]{:S(2)}) async-start(), calls=%async_computation.11 | async-start | bytes 2359296 | tf_op jit(solution)/shard_map/while/body/eval_jaxpr/all_gather | solution.py:62
  720.5 31.7 %all-gather.9.cloned.1.call-start = ((), (), s32[]{:S(2)}) async-start(), calls=%async_computation.11 | async-start | bytes 2359296 | tf_op jit(solution)/shard_map/while/body/eval_jaxpr/all_gather | solution.py:62
  802.5 31.4 %all-gather.9.cloned.1.call-start = ((), (), s32[]{:S(2)}) async-start(), calls=%async_computation.11 | async-start | bytes 2359296 | tf_op jit(solution)/shard_map/while/body/eval_jaxpr/all_gather | solution.py:62
  884.3 31.7 %all-gather.9.cloned.1.call-start = ((), (), s32[]{:S(2)}) async-start(), calls=%async_computation.11 | async-start | bytes 2359296 | tf_op jit(solution)/shard_map/while/body/eval_jaxpr/all_gather | solution.py:62
  1048.0 31.7 %all-gather.9.cloned.1.call-start = ((), (), s32[]{:S(2)}) async-start(), calls=%async_computation.11 | async-start | bytes 2359296 | tf_op jit(solution)/shard_map/while/body/eval_jaxpr/all_gather | solution.py:62
  1375.7 50.2 %all-gather.5.cloned.1.call-start = ((), (), s32[]{:S(2)}) async-start(), calls=%async_computation.4 | async-start | bytes 2359296 | tf_op jit(solution)/shard_map/all_gather | solution.py:78
  1376.4 60.9 %all-gather.7.cloned.1.call-start = ((), (), s32[]{:S(2)}) async-start(), calls=%async_computation.5 | async-start | bytes 2580480 | tf_op jit(solution)/shard_map/all_gather | solution.py:145
  1470.5 57.6 %reduce-scatter.11.cloned.1.call-start = ((), (), s32[]{:S(2)}) async-start(), calls=%async_computation.10 | async-start | bytes 2359296 | tf_op jit(solution)/shard_map/while/body/eval_jaxpr/reduce_scatter | solution.py:124
  1529.8 57.8 %reduce-scatter.11.cloned.1.call-start = ((), (), s32[]{:S(2)}) async-start(), calls=%async_computation.10 | async-start | bytes 2359296 | tf_op jit(solution)/shard_map/while/body/eval_jaxpr/reduce_scatter | solution.py:124
  1589.5 57.9 %reduce-scatter.11.cloned.1.call-start = ((), (), s32[]{:S(2)}) async-start(), calls=%async_computation.10 | async-start | bytes 2359296 | tf_op jit(solution)/shard_map/while/body/eval_jaxpr/reduce_scatter | solution.py:124
  1649.1 57.8 %reduce-scatter.11.cloned.1.call-start = ((), (), s32[]{:S(2)}) async-start(), calls=%async_computation.10 | async-start | bytes 2359296 | tf_op jit(solution)/shard_map/while/body/eval_jaxpr/reduce_scatter | solution.py:124
  1708.8 57.9 %reduce-scatter.11.cloned.1.call-start = ((), (), s32[]{:S(2)}) async-start(), calls=%async_computation.10 | async-start | bytes 2359296 | tf_op jit(solution)/shard_map/while/body/eval_jaxpr/reduce_scatter | solution.py:124
  1768.4 57.8 %reduce-scatter.11.cloned.1.call-start = ((), (), s32[]{:S(2)}) async-start(), calls=%async_computation.10 | async-start | bytes 2359296 | tf_op jit(solution)/shard_map/while/body/eval_jaxpr/reduce_scatter | solution.py:124
  1828.0 57.8 %reduce-scatter.11.cloned.1.call-start = ((), (), s32[]{:S(2)}) async-start(), calls=%async_computation.10 | async-start | bytes 2359296 | tf_op jit(solution)/shard_map/while/body/eval_jaxpr/reduce_scatter | solution.py:124
  1887.7 57.8 %reduce-scatter.11.cloned.1.call-start = ((), (), s32[]{:S(2)}) async-start(), calls=%async_computation.10 | async-start | bytes 2359296 | tf_op jit(solution)/shard_map/while/body/eval_jaxpr/reduce_scatter | solution.py:124
  1947.3 57.8 %reduce-scatter.11.cloned.1.call-start = ((), (), s32[]{:S(2)}) async-start(), calls=%async_computation.10 | async-start | bytes 2359296 | tf_op jit(solution)/shard_map/while/body/eval_jaxpr/reduce_scatter | solution.py:124
  2006.9 57.8 %reduce-scatter.11.cloned.1.call-start = ((), (), s32[]{:S(2)}) async-start(), calls=%async_computation.10 | async-start | bytes 2359296 | tf_op jit(solution)/shard_map/while/body/eval_jaxpr/reduce_scatter | solution.py:124
  2066.6 57.8 %reduce-scatter.11.cloned.1.call-start = ((), (), s32[]{:S(2)}) async-start(), calls=%async_computation.10 | async-start | bytes 2359296 | tf_op jit(solution)/shard_map/while/body/eval_jaxpr/reduce_scatter | solution.py:124
  2126.2 57.8 %reduce-scatter.11.cloned.1.call-start = ((), (), s32[]{:S(2)}) async-start(), calls=%async_computation.10 | async-start | bytes 2359296 | tf_op jit(solution)/shard_map/while/body/eval_jaxpr/reduce_scatter | solution.py:124
  2185.8 57.8 %reduce-scatter.11.cloned.1.call-start = ((), (), s32[]{:S(2)}) async-start(), calls=%async_computation.10 | async-start | bytes 2359296 | tf_op jit(solution)/shard_map/while/body/eval_jaxpr/reduce_scatter | solution.py:124
  2245.4 57.8 %reduce-scatter.11.cloned.1.call-start = ((), (), s32[]{:S(2)}) async-start(), calls=%async_computation.10 | async-start | bytes 2359296 | tf_op jit(solution)/shard_map/while/body/eval_jaxpr/reduce_scatter | solution.py:124
  2305.1 57.8 %reduce-scatter.11.cloned.1.call-start = ((), (), s32[]{:S(2)}) async-start(), calls=%async_computation.10 | async-start | bytes 2359296 | tf_op jit(solution)/shard_map/while/body/eval_jaxpr/reduce_scatter | solution.py:124
  2364.7 57.9 %reduce-scatter.11.cloned.1.call-start = ((), (), s32[]{:S(2)}) async-start(), calls=%async_computation.10 | async-start | bytes 2359296 | tf_op jit(solution)/shard_map/while/body/eval_jaxpr/reduce_scatter | solution.py:124
  2424.3 135.9 %all-reduce.3.cloned.1.call-start = ((), (), s32[]{:S(2)}) async-start(), calls=%async_computation.6 | async-start | bytes 573440 | tf_op jit(solution)/shard_map/psum | solution.py:173
  2434.9 149.3 %reduce-scatter.9.cloned.1.call-start = ((), (), s32[]{:S(2)}) async-start(), calls=%async_computation.9 | async-start | bytes 491520 | tf_op jit(solution)/shard_map/reduce_scatter | solution.py:172
  2442.2 164.5 %reduce-scatter.5.cloned.1.call-start = ((), (), s32[]{:S(2)}) async-start(), calls=%async_computation.7 | async-start | bytes 655360 | tf_op jit(solution)/shard_map/reduce_scatter | solution.py:171
  2445.2 306.7 %reduce-scatter.7.cloned.1.call-start = ((), (), s32[]{:S(2)}) async-start(), calls=%async_computation.8 | async-start | bytes 10485760 | tf_op jit(solution)/shard_map/reduce_scatter | solution.py:170
  (108 other events, 5159.5 us)
Sparse Core Ops, SparseCore 0:
  67.3 29.3 all-gather.8
  150.6 28.1 all-gather.8
  232.6 28.1 all-gather.8
  314.2 28.1 all-gather.8
  396.1 28.1 all-gather.8
  477.9 28.1 all-gather.8
  559.9 28.1 all-gather.8
  641.9 28.1 all-gather.8
  723.9 28.1 all-gather.8
  805.7 28.1 all-gather.8
  887.7 28.1 all-gather.8
  969.4 28.1 all-gather.8
  1051.5 28.1 all-gather.8
  1133.2 28.1 all-gather.8
  1215.0 28.1 all-gather.8
  1296.7 28.1 all-gather.8
  1486.8 41.2 reduce-scatter.10
  1546.4 41.1 reduce-scatter.10
  1606.1 41.2 reduce-scatter.10
  1665.7 41.1 reduce-scatter.10
  1725.3 41.2 reduce-scatter.10
  1785.0 41.1 reduce-scatter.10
  1844.6 41.1 reduce-scatter.10
  1904.3 41.1 reduce-scatter.10
  1963.9 41.1 reduce-scatter.10
  2023.5 41.1 reduce-scatter.10
  2083.1 41.1 reduce-scatter.10
  2142.8 41.1 reduce-scatter.10
  2202.4 41.1 reduce-scatter.10
  2262.0 41.1 reduce-scatter.10
  2321.6 41.1 reduce-scatter.10
  2381.3 41.2 reduce-scatter.10
Sparse Core Ops, SparseCore 1:
  1378.6 28.0 all-gather.4
  1408.4 28.9 all-gather.6
  2435.0 125.2 all-reduce.2
  2562.6 21.5 reduce-scatter.8
  2587.1 19.6 reduce-scatter.4
  2609.1 142.8 reduce-scatter.6

commit v2 on v1

--- a/solution.py
+++ b/solution.py
@@ -1,7 +1,13 @@
+import functools
+
 import jax
 import jax.numpy as jnp
 from jax import lax
+from jax.experimental import pallas as pl
+from jax.experimental.pallas import tpu as pltpu
 from jax.sharding import PartitionSpec as P
+
+VMEM_LIMIT = 56 * 2**20
 
 
 def column_order(own_units):
@@ -135,6 +141,489 @@
     return loss, hidden_sq, logit_sq, dec_bias, dec_grad, hidden_grad, cell_grad, rec_grad, letter_grad
 
 
+MESH = pl.DeviceIdType.MESH
+LANES = 128
+VOCAB_PAD = 384
+CHUNK = 32
+NT = (((1,), (1,)), ((), ()))
+TN = (((0,), (0,)), ((), ()))
+
+
+def sigmoid(x):
+    return 0.5 * jnp.tanh(0.5 * x) + 0.5
+
+
+def matmul(left, right, dims=(((1,), (0,)), ((), ()))):
+    return lax.dot_general(left, right, dims, preferred_element_type=jnp.float32)
+
+
+def neighbours():
+    me = lax.axis_index("mp")
+    row, column, core = me // 4, (me // 2) % 2, me % 2
+    sibling = row * 4 + column * 2 + (1 - core)
+    across = (1 - row) * 4 + (1 - column) * 2 + core
+    side = row * 4 + (1 - column) * 2 + core
+    up = (1 - row) * 4 + column * 2 + core
+    return me, sibling, (across, side, up)
+
+
+def greet(peers):
+    seq = lax.axis_index("seq")
+    barrier = pltpu.get_barrier_semaphore()
+    for peer in peers:
+        pl.semaphore_signal(barrier, inc=1, device_id=(seq, peer), device_id_type=MESH)
+    pl.semaphore_wait(barrier, len(peers))
+
+
+def remote(src, dst, send, recv, peer):
+    return pltpu.make_async_remote_copy(
+        src_ref=src, dst_ref=dst, send_sem=send, recv_sem=recv,
+        device_id=(lax.axis_index("seq"), peer), device_id_type=MESH,
+    )
+
+
+def other_core(peer):
+    return (peer // 2) * 2 + (1 - peer % 2)
+
+
+def column_of(table, lane):
+    lanes = lax.broadcasted_iota(jnp.int32, table.shape, 1)
+    return jnp.sum(jnp.where(lanes == lane, table, 0.0), axis=1, keepdims=True)
+
+
+def time_of(direction, step, length):
+    return step if direction == 0 else length - 1 - step
+
+
+def forward_kernel(
+    length, letters, info, inverse, h_in, c_in, embed, w_in, bias, b_dec, wd_hbm, w_hbm,
+    wholes, acts, grads, loss, logit_sq, hidden_sq, dec_bias, dec_grad,
+    w, wd, buf, cell, acc, logit, stage, grad, load_sem, send_sem, recv_sem, save_sem, act_sem, grad_sem,
+):
+    me, sibling, peers = neighbours()
+    blocks, rows, units = buf.shape[2:]
+    groups = units // LANES
+    load_w = pltpu.make_async_copy(w_hbm, w, load_sem.at[0])
+    load_wd = pltpu.make_async_copy(wd_hbm, wd, load_sem.at[1])
+    load_w.start()
+    load_wd.start()
+    greet((sibling,) + peers)
+    for ref in (loss, logit_sq, hidden_sq, dec_bias, dec_grad):
+        ref[...] = jnp.zeros(ref.shape, ref.dtype)
+    cell[...] = c_in[...]
+
+    def direct(d, step):
+        slot, par = step % 3, step % 2
+        block = buf.at[d, slot, me]
+        return [
+            remote(block, block, send_sem.at[d, par, n], recv_sem.at[d, slot, me], peer)
+            for n, peer in enumerate(peers + (sibling,))
+        ]
+
+    def relay(d, step, n):
+        slot, par = step % 3, step % 2
+        block = buf.at[d, slot, peers[n]]
+        return remote(block, block, send_sem.at[d, par, 4 + n], recv_sem.at[d, slot, peers[n]], sibling)
+
+    def arrival(d, step, source):
+        slot = step % 3
+        block = buf.at[d, slot, source]
+        return remote(block, block, send_sem.at[d, step % 2, 0], recv_sem.at[d, slot, source], sibling)
+
+    def save(d, step):
+        return pltpu.make_async_copy(buf.at[d, step % 3], wholes.at[step, d], save_sem.at[d, step % 2])
+
+    def save_acts(d, step):
+        return pltpu.make_async_copy(stage.at[d], acts.at[step, d], act_sem.at[d])
+
+    def save_grad(d, step):
+        return pltpu.make_async_copy(grad.at[d], grads.at[step, d], grad_sem.at[d])
+
+    def finish_sends(d, step):
+        for copy in direct(d, step):
+            copy.wait_send()
+        for n in range(3):
+            relay(d, step, n).wait_send()
+
+    def gates(d, step):
+        slot, later = step % 3, (step + 1) % 3
+        when = time_of(d, step, length)
+
+        def chunk(i, carry):
+            at = pl.ds(pl.multiple_of(i * CHUNK, CHUNK), CHUNK)
+            live = info[d, at, LANES - 1:LANES] > when.astype(jnp.float32)
+            for g in range(groups):
+                lanes = slice(g * LANES, (g + 1) * LANES)
+                pre = [acc[at, (4 * g + k) * LANES:(4 * g + k + 1) * LANES] for k in range(4)]
+                in_gate, forget, out_gate = sigmoid(pre[0]), sigmoid(pre[1]), sigmoid(pre[3])
+                cell_gate = jnp.tanh(pre[2])
+                old = cell[d, at, lanes]
+                new = forget * old + in_gate * cell_gate
+                for k, value in enumerate((in_gate, forget, cell_gate, out_gate, old)):
+                    stage[d, k, at, lanes] = value
+                cell[d, at, lanes] = jnp.where(live, new, old)
+                before = buf[d, slot, me, at, lanes].astype(jnp.float32)
+                hidden = jnp.where(live, out_gate * jnp.tanh(new), before).astype(jnp.bfloat16)
+                buf[d, later, me, at, lanes] = hidden
+                wide = hidden.astype(jnp.float32)
+                hidden_sq[d] += jnp.where(live, wide * wide, 0.0)
+            return carry
+
+        lax.fori_loop(0, rows // CHUNK, chunk, 0)
+
+    def decode(d, step):
+        slot = step % 3
+        total = jnp.broadcast_to(b_dec[d], logit.shape)
+        for b in range(blocks):
+            total += matmul(buf[d, slot, b], wd[d, b])
+        logit[...] = total
+        when = time_of(d, step - 1, length)
+        reach = when + 1 if d == 0 else when
+        scale = inverse[0, 0]
+
+        def chunk(i, carry):
+            at = pl.ds(pl.multiple_of(i * CHUNK, CHUNK), CHUNK)
+            table = info[d, at, :]
+            valid = (table[:, LANES - 1:LANES] > reach.astype(jnp.float32)) & (step < length)
+            target = column_of(table, step)
+            value = logit[at, :]
+            lanes = lax.broadcasted_iota(jnp.int32, value.shape, 1)
+            hot = lanes.astype(jnp.float32) == target
+            top = jnp.max(value, axis=1, keepdims=True)
+            power = jnp.exp(value - top)
+            total = jnp.sum(power, axis=1, keepdims=True)
+            picked = jnp.sum(jnp.where(hot, value, 0.0), axis=1, keepdims=True)
+            loss[d] += jnp.broadcast_to(jnp.where(valid, top + jnp.log(total) - picked, 0.0), (CHUNK, LANES))
+            kept = jnp.where(valid & (lanes < letters), value, 0.0)
+            square = kept * kept
+            logit_sq[d] += sum(square[:, n * LANES:(n + 1) * LANES] for n in range(VOCAB_PAD // LANES))
+            slope = jnp.where(
+                valid, (power * (1.0 / total) - jnp.where(hot, 1.0, 0.0)) * scale, 0.0
+            ).astype(jnp.bfloat16)
+            grad[d, at, :] = slope
+            wide = slope.astype(jnp.float32)
+            dec_bias[d] += sum(wide[n * 8:(n + 1) * 8] for n in range(CHUNK // 8))
+            return carry
+
+        lax.fori_loop(0, rows // CHUNK, chunk, 0)
+        dec_grad[d] += matmul(buf[d, slot, me], grad[d], TN)
+
+    def half(step, d):
+        @pl.when(step < length)
+        def _():
+            ids = column_of(info[d], step)
+            hot = (lax.broadcasted_iota(jnp.int32, (rows, VOCAB_PAD), 1).astype(jnp.float32) == ids)
+            row = matmul(hot.astype(jnp.bfloat16), embed[d]).astype(jnp.bfloat16)
+            acc[...] = matmul(row, w_in[d]).astype(jnp.bfloat16).astype(jnp.float32) + bias[d]
+
+        for n, peer in enumerate(peers):
+            arrival(d, step, peer).wait_recv()
+            relay(d, step, n).start()
+
+        if d == 0:
+            @pl.when(step == 0)
+            def _():
+                load_w.wait()
+                load_wd.wait()
+
+        slot = step % 3
+
+        def advance(block):
+            acc[...] += matmul(buf[d, slot, block], w[d, block])
+
+        @pl.when(step < length)
+        def _():
+            for block in (me,) + peers:
+                advance(block)
+
+        for block in (sibling,) + tuple(other_core(peer) for peer in peers):
+            arrival(d, step, block).wait_recv()
+
+        @pl.when(step < length)
+        def _():
+            save(d, step).start()
+            for block in (sibling,) + tuple(other_core(peer) for peer in peers):
+                advance(block)
+
+            @pl.when(step > 0)
+            def _():
+                save_acts(d, step - 1).wait()
+
+            gates(d, step)
+            save_acts(d, step).start()
+
+            @pl.when(step > 0)
+            def _():
+                save(d, step - 1).wait()
+                finish_sends(d, step - 1)
+
+            for copy in direct(d, step + 1):
+                copy.start()
+
+        @pl.when(step > 0)
+        def _():
+            @pl.when(step > 1)
+            def _():
+                save_grad(d, step - 2).wait()
+
+            decode(d, step)
+            save_grad(d, step - 1).start()
+
+    for d in range(2):
+        buf[d, 0, me] = h_in[d]
+        for copy in direct(d, 0):
+            copy.start()
+
+    def both(step, carry):
+        for d in range(2):
+            half(step, d)
+        return carry
+
+    lax.fori_loop(0, length + 1, both, 0)
+    for d in range(2):
+        save(d, length - 1).wait()
+        save_acts(d, length - 1).wait()
+        save_grad(d, length - 1).wait()
+        finish_sends(d, length - 1)
+        finish_sends(d, length)
+
+
+def backward_kernel(
+    length, info, w_dec, acts, grads, w_hbm,
+    pres, hidden_grad, cell_grad,
+    w, stage, grad, pre, held, own, sent, got, passed, taken, load_sem, act_sem, grad_sem, pre_sem,
+    core_send, core_recv, chip_send, chip_recv,
+):
+    me, sibling, peers = neighbours()
+    rows, units = held.shape[1:]
+    groups = units // LANES
+    load_w = pltpu.make_async_copy(w_hbm, w, load_sem)
+    load_w.start()
+
+    def load_acts(d, step):
+        return pltpu.make_async_copy(acts.at[step, d], stage.at[d], act_sem.at[d])
+
+    def load_grad(d, step):
+        return pltpu.make_async_copy(grads.at[step, d], grad.at[d], grad_sem.at[d])
+
+    def save_pre(d, step):
+        return pltpu.make_async_copy(pre.at[d], pres.at[step, d], pre_sem.at[d])
+
+    for d in range(2):
+        load_acts(d, length - 1).start()
+        load_grad(d, length - 1).start()
+    greet((sibling,) + peers)
+    held[...] = jnp.zeros(held.shape, held.dtype)
+    own[...] = jnp.zeros(own.shape, own.dtype)
+    cell_grad[...] = jnp.zeros(cell_grad.shape, cell_grad.dtype)
+
+    def to_core(d, turn, n):
+        return remote(
+            sent.at[d, n], got.at[d, turn % 2, n], core_send.at[d, n], core_recv.at[d, turn % 2, n], sibling
+        )
+
+    def to_chip(d, turn, n):
+        return remote(
+            passed.at[d, n], taken.at[d, turn % 2, n], chip_send.at[d, n], chip_recv.at[d, turn % 2, n], peers[n]
+        )
+
+    def half(turn, d):
+        step = length - 1 - turn
+        when = time_of(d, step, length)
+        load_acts(d, step).wait()
+        load_grad(d, step).wait()
+        held[d] += matmul(grad[d], w_dec[d], NT)
+
+        @pl.when(turn > 0)
+        def _():
+            for n in range(3):
+                to_chip(d, turn - 1, n).wait_recv()
+            save_pre(d, step + 1).wait()
+
+        def chunk(i, carry):
+            at = pl.ds(pl.multiple_of(i * CHUNK, CHUNK), CHUNK)
+            live = info[d, at, LANES - 1:LANES] > when.astype(jnp.float32)
+            for g in range(groups):
+                lanes = slice(g * LANES, (g + 1) * LANES)
+                through = own[d, at, lanes]
+                for n in range(3):
+                    through += jnp.where(turn > 0, taken[d, (turn + 1) % 2, n, at, lanes].astype(jnp.float32), 0.0)
+                total = held[d, at, lanes] + through
+                in_gate, forget, cell_gate, out_gate, old = (stage[d, k, at, lanes] for k in range(5))
+                squash = jnp.tanh(forget * old + in_gate * cell_gate)
+                later = cell_grad[d, at, lanes]
+                new = jnp.where(live, later + total * out_gate * (1.0 - squash * squash), 0.0)
+                out = jnp.where(live, total * squash, 0.0)
+                values = (
+                    new * cell_gate * in_gate * (1.0 - in_gate),
+                    new * old * forget * (1.0 - forget),
+                    new * in_gate * (1.0 - cell_gate * cell_gate),
+                    out * out_gate * (1.0 - out_gate),
+                )
+                for k, value in enumerate(values):
+                    pre[d, at, (4 * g + k) * LANES:(4 * g + k + 1) * LANES] = value.astype(jnp.bfloat16)
+                cell_grad[d, at, lanes] = new * forget + jnp.where(live, 0.0, later)
+                held[d, at, lanes] = jnp.where(live, 0.0, total)
+            return carry
+
+        lax.fori_loop(0, rows // CHUNK, chunk, 0)
+        save_pre(d, step).start()
+
+        @pl.when(turn < length - 1)
+        def _():
+            load_acts(d, step - 1).start()
+            load_grad(d, step - 1).start()
+
+        @pl.when(turn > 0)
+        def _():
+            for n in range(4):
+                to_core(d, turn - 1, n).wait_send()
+            for n in range(3):
+                to_chip(d, turn - 1, n).wait_send()
+
+        if d == 0:
+            @pl.when(turn == 0)
+            def _():
+                load_w.wait()
+
+        for n, block in enumerate(tuple(other_core(peer) for peer in peers) + (sibling,)):
+            sent[d, n] = matmul(pre[d], w[d, block], NT).astype(jnp.bfloat16)
+            to_core(d, turn, n).start()
+        for n, block in enumerate(peers + (me,)):
+            share = matmul(pre[d], w[d, block], NT)
+            to_core(d, turn, n).wait_recv()
+            share += got[d, turn % 2, n].astype(jnp.float32)
+            if n < 3:
+                passed[d, n] = share.astype(jnp.bfloat16)
+                to_chip(d, turn, n).start()
+            else:
+                own[d] = share
+
+    def both(turn, carry):
+        for d in range(2):
+            half(turn, d)
+        return carry
+
+    lax.fori_loop(0, length, both, 0)
+    for d in range(2):
+        for n in range(3):
+            to_chip(d, length - 1, n).wait_recv()
+        total = held[d] + own[d]
+        for n in range(3):
+            total += taken[d, (length - 1) % 2, n].astype(jnp.float32)
+        hidden_grad[d] = total
+        save_pre(d, 0).wait()
+        for n in range(4):
+            to_core(d, length - 1, n).wait_send()
+        for n in range(3):
+            to_chip(d, length - 1, n).wait_send()
+
+
+def kernel_recurrences(step_ids, own_len, h_init, c_init, embed, w_in, w_rec, bias, w_dec, wd_full, b_dec, count):
+    length, rows = step_ids.shape[1:]
+    letters, width = embed.shape[1:]
+    units, columns = h_init.shape[2], w_rec.shape[2]
+    blocks = w_rec.shape[1] // units
+    any_space, vmem = pl.BlockSpec(memory_space=pl.ANY), pl.BlockSpec(memory_space=pltpu.VMEM)
+    ids = jnp.swapaxes(step_ids, 1, 2).astype(jnp.float32)
+    reach = jnp.broadcast_to(own_len.astype(jnp.float32)[None, :, None], (2, rows, 1))
+    info = jnp.concatenate([ids, jnp.full((2, rows, LANES - 1 - length), -1.0, jnp.float32), reach], axis=2)
+    pad_letters = VOCAB_PAD - letters
+    embed_pad = jnp.pad(embed, ((0, 0), (0, pad_letters), (0, LANES - width)))
+    w_in_pad = jnp.pad(w_in, ((0, 0), (0, LANES - width), (0, 0)))
+    wd_pad = jnp.pad(wd_full, ((0, 0), (0, 0), (0, pad_letters))).reshape(2, blocks, units, VOCAB_PAD)
+    w_dec_pad = jnp.pad(w_dec, ((0, 0), (0, 0), (0, pad_letters)))
+    b_dec_pad = jnp.pad(b_dec, ((0, 0), (0, pad_letters)), constant_values=-1e30)[:, None]
+    w_blocks = w_rec.reshape(2, blocks, units, columns)
+    inverse = (1.0 / count).reshape(1, 1)
+    f32, bf16 = jnp.float32, jnp.bfloat16
+    dma = pltpu.SemaphoreType.DMA
+    shape = jax.ShapeDtypeStruct
+    wholes, acts, grads, loss, logit_sq, hidden_sq, dec_bias, dec_grad = pl.pallas_call(
+        functools.partial(forward_kernel, length, letters),
+        out_shape=(
+            shape((length, 2, blocks, rows, units), bf16),
+            shape((length, 2, 5, rows, units), f32),
+            shape((length, 2, rows, VOCAB_PAD), bf16),
+            shape((2, CHUNK, LANES), f32),
+            shape((2, CHUNK, LANES), f32),
+            shape((2, CHUNK, LANES), f32),
+            shape((2, 8, VOCAB_PAD), f32),
+            shape((2, units, VOCAB_PAD), f32),
+        ),
+        in_specs=[vmem, pl.BlockSpec(memory_space=pltpu.SMEM)] + [vmem] * 6 + [any_space] * 2,
+        out_specs=(any_space,) * 3 + (vmem,) * 5,
+        scratch_shapes=[
+            pltpu.VMEM((2, blocks, units, columns), bf16),
+            pltpu.VMEM((2, blocks, units, VOCAB_PAD), bf16),
+            pltpu.VMEM((2, 3, blocks, rows, units), bf16),
+            pltpu.VMEM((2, rows, units), f32),
+            pltpu.VMEM((rows, columns), f32),
+            pltpu.VMEM((rows, VOCAB_PAD), f32),
+            pltpu.VMEM((2, 5, rows, units), f32),
+            pltpu.VMEM((2, rows, VOCAB_PAD), bf16),
+            dma((2,)),
+            dma((2, 2, 7)),
+            dma((2, 3, blocks)),
+            dma((2, 2)),
+            dma((2,)),
+            dma((2,)),
+        ],
+        compiler_params=pltpu.CompilerParams(
+            collective_id=0, has_side_effects=True, vmem_limit_bytes=VMEM_LIMIT
+        ),
+        name="forward_visits",
+    )(info, inverse, h_init, c_init, embed_pad, w_in_pad, bias[:, None], b_dec_pad, wd_pad, w_blocks)
+    pres, hidden_grad, cell_grad = pl.pallas_call(
+        functools.partial(backward_kernel, length),
+        out_shape=(
+            shape((length, 2, rows, columns), bf16),
+            shape((2, rows, units), f32),
+            shape((2, rows, units), f32),
+        ),
+        in_specs=[vmem] * 2 + [any_space] * 3,
+        out_specs=(any_space, vmem, vmem),
+        scratch_shapes=[
+            pltpu.VMEM((2, blocks, units, columns), bf16),
+            pltpu.VMEM((2, 5, rows, units), f32),
+            pltpu.VMEM((2, rows, VOCAB_PAD), bf16),
+            pltpu.VMEM((2, rows, columns), bf16),
+            pltpu.VMEM((2, rows, units), f32),
+            pltpu.VMEM((2, rows, units), f32),
+            pltpu.VMEM((2, 4, rows, units), bf16),
+            pltpu.VMEM((2, 2, 4, rows, units), bf16),
+            pltpu.VMEM((2, 3, rows, units), bf16),
+            pltpu.VMEM((2, 2, 3, rows, units), bf16),
+            dma,
+            dma((2,)),
+            dma((2,)),
+            dma((2,)),
+            dma((2, 4)),
+            dma((2, 2, 4)),
+            dma((2, 3)),
+            dma((2, 2, 3)),
+        ],
+        compiler_params=pltpu.CompilerParams(
+            collective_id=1, has_side_effects=True, vmem_limit_bytes=VMEM_LIMIT
+        ),
+        name="backward_visits",
+    )(info, w_dec_pad, acts, grads, w_blocks)
+    rec_grad = jnp.einsum("sdnbu,sdbc->dnuc", wholes, pres, preferred_element_type=f32)
+    onehot = (jnp.swapaxes(step_ids, 0, 1)[..., None] == jnp.arange(letters, dtype=jnp.int32)).astype(bf16)
+    letter_grad = jnp.einsum("sdbv,sdbc->dvc", onehot, pres, preferred_element_type=f32)
+    return (
+        jnp.sum(loss[:, :, 0]),
+        jnp.sum(hidden_sq, axis=(1, 2)),
+        jnp.sum(logit_sq, axis=(1, 2)),
+        jnp.sum(dec_bias, axis=1)[:, :letters],
+        dec_grad[:, :, :letters],
+        hidden_grad,
+        cell_grad,
+        rec_grad.reshape(2, blocks * units, columns),
+        letter_grad,
+    )
+
+
 def per_device(ids, lengths, order, h_init, c_init, embed, w_in, w_rec, bias, w_dec, b_dec):
     seq_rank = lax.axis_index("seq")
     first_mp = (lax.axis_index("mp") == 0).astype(jnp.float32)
@@ -156,10 +645,15 @@
     bias_grouped = jnp.swapaxes(
         bias.reshape(2, own_units // lanes, lanes, 4), -1, -2
     ).reshape(bias.shape)
-    loss, hidden_sq, logit_sq, dec_bias, dec_grad, hidden_grad, cell_grad, rec_grad, letter_grad = recurrences(
+    operands = (
         step_ids, own_len, h_init, c_init, embed, w_in_grouped, w_rec_grouped, bias_grouped, w_dec, wd_full,
-        b_dec, count, lanes,
-    )
+        b_dec, count,
+    )
+    if lax.axis_size("mp") == 8 and own_units % LANES == 0 and per_dev % CHUNK == 0:
+        results = kernel_recurrences(*operands)
+    else:
+        results = recurrences(*operands, lanes)
+    loss, hidden_sq, logit_sq, dec_bias, dec_grad, hidden_grad, cell_grad, rec_grad, letter_grad = results
     embed_wide = embed.astype(jnp.float32)
     in_grad = jnp.einsum("dve,dvc->dec", embed_wide, letter_grad, precision=lax.Precision.HIGHEST)
     bias_grad = jnp.sum(letter_grad, axis=1, keepdims=True)

time: 2790 us -> 862 us (0.31)
  waiting for transfers between devices: 1300 us -> 194 us
  local copies, waits for them, and re-layouts: 638 us -> 74.2 us
  Pallas kernels: 0 us -> 421 us
  other arithmetic: 398 us -> 13.4 us
  matrix products: 358 us -> 75.2 us
    reduce_scatter x16 -> x0, waiting for transfers between devices: 633 us -> none  [backward_step(): lax.psum_scatter(terms.astype(jnp.bfloat16), 'mp', scatter_dimension=2, t...]
    all_gather x17 -> x0, waiting for transfers between devices: 450 us -> none  [the longest x16 450 us: forward_step(): whole = lax.all_gather(hidden, 'mp', axis=2, tiled=True)]
    pallas_call x0 -> x2, Pallas kernels: none -> 421 us  [the longest x1 228 us: kernel_recurrences(): pl.pallas_call(functools.partial(forward_kernel, length, letters), out_sh...]
    dot_general x53 -> x2, matrix products: 341 us -> 59.9 us  [the longest x1 51.3 us: kernel_recurrences(): jnp.einsum('sdnbu,sdbc->dnuc', wholes, pres, preferred_element_type=f32)]
    div x96 -> x0, local copies, waits for them, and re-layouts: 173 us -> none  [forward_step(): jax.nn.sigmoid(x)]
    div x16 -> x0, other arithmetic: 170 us -> none  [forward_step(): jax.nn.sigmoid(x)]
    tanh x16 -> x0, other arithmetic: 133 us -> none  [forward_step(): cell_gate = jnp.tanh(cell_pre)]
    dynamic_update_slice x80 -> x0, local copies, waits for them, and re-layouts: 127 us -> none  [the longest x64 110 us: recurrences(): lax.scan(forward_step, (h_init, c_init), (gates_in, live_steps))]
  transfers between devices with their start and end apart: 38 -> 5, of which waited for: 37 -> 4; matrix products, arithmetic and copies ran while one was open for 7% -> 15% of each run, Pallas kernels for 0% -> 0%
where the time goes in v2:
time: 862 us; the launch traced here: 853 us
  Pallas kernels  421 us (49%)
  waiting for transfers between devices  194 us (23%)
  matrix products  75.2 us (9%)
  local copies, waits for them, and re-layouts  74.2 us (9%)
  blocking collectives  56.7 us (7%)
  between operations  18.1 us (2%)
  other arithmetic  13.4 us (2%)
    pallas_call x1, Pallas kernels, kernel_recurrences(): pl.pallas_call(functools.partial(forward_kernel, length, letters), out_sh...  228 us
    pallas_call x1, Pallas kernels, kernel_recurrences(): pl.pallas_call(functools.partial(backward_kernel, length), out_shape=(sha...  193 us
    reduce_scatter x1, waiting for transfers between devices, per_device(): lax.psum_scatter(rec_grad.astype(jnp.bfloat16), 'seq', scatter_dimension=...  142 us
    dot_general x1, matrix products, kernel_recurrences(): jnp.einsum('sdnbu,sdbc->dnuc', wholes, pres, preferred_element_type=f32)  51.3 us
    psum x1, blocking collectives, per_device(): lax.psum((loss * first_mp, hidden_sq, logit_sq * first_mp, dec_bias * fir...  41.6 us
    unnamed x29, local copies, waits for them, and re-layouts  27.4 us
    reduce_scatter x1, waiting for transfers between devices, per_device(): lax.psum_scatter(dec_grad.astype(jnp.bfloat16), 'seq', scatter_dimension=...  22.7 us
    reduce_scatter x1, waiting for transfers between devices, per_device(): lax.psum_scatter(edge.astype(jnp.bfloat16), 'seq', scatter_dimension=2, t...  21.1 us
  transfers between devices with their start and end apart: 5, of which 4 were waited for; matrix products, arithmetic and copies ran while one was open for 15% of the time, Pallas kernels for 0%

profile of v2, /device:TPU:0, one launch (start us, length us, event | category | flops | bytes accessed | tf_op | source)
XLA Modules:
  0.0 852.6 jit_solution(12366767583441431609)
XLA Ops:
  8.0 1.2 copy.113
  9.2 1.3 reduce_sum.67
  11.9 1.9 gather_fusion.1
  15.1 15.1 %all-gather = s32[4,4,1024]{2,1,0:T(4,128)S(1)} all-gather(s32[1,4,1024]{2,1,0:T(4,128)} %bitcast.85), channel_id=1, replica_groups=mesh['seq'=4,'mp'=8] {'seq'}, dimensions={0}, use_global_device_ids=true | all-gather | bytes 81920 | tf_op jit(solution)/shard_map/all_gather | solution.py:635
  34.4 1.3 reshape.125
  40.1 10.4 %fusion.7 = bf16[512,2,2048,2]{2,0,3,1:T(8,128)(2,1)} fusion(bf16[2,256,2,8,512]{4,3,2,1,0:T(8,128)(2,1)} %bitcast.86, s32[512]{0:T(512)S(1)} %fusion.37), kind=kOutput, calls=%fused_computation.11 | convolution fusion | flops 4299685888 | bytes 16779264 | tf_op jit(solution)/shard_map/...gc,cp->...gp/dot_general | solution.py:24
  50.5 10.3 %copy.135 = bf16[256,8,8,256]{3,2,1,0:T(8,128)(2,1)} copy(bf16[256,8,8,256]{3,1,2,0:T(8,128)(2,1)} %bitcast.78) | data formatting | bytes 16777216
  60.7 12.1 %copy.132.w_hbm = bf16[2,8,256,1024]{3,2,1,0:T(8,128)(2,1)} copy(bf16[2,8,256,1024]{2,1,3,0:T(8,128)(2,1)} %bitcast.75) | data formatting | bytes 16777216 | tf_op jit(solution)/shard_map/reshape;reshape | solution.py:537
  74.0 5.2 copy.133
  79.2 2.0 pad.23.clone
  81.2 227.7 %forward_visits.1 = (bf16[16,2,8,256,256]{4,3,2,1,0:T(8,128)(2,1)}, f32[16,2,5,256,256]{4,3,2,1,0:T(8,128)}, bf16[16,2,256,384]{3,2,1,0:T(8,128)(2,1)}, f32[2,32...) custom-call(f32[2,256,128]{2,1,0:T(8,128)} %pad_maximum_fusion.info,, ...), custom_call_target="tpu_custom_call" | custom-call | tf_op jit(solution)/shard_map/forward_visits/pallas_call | solution.py:542
  308.9 193.4 %backward_visits.1 = (bf16[16,2,256,1024]{3,2,1,0:T(8,128)(2,1)}, f32[2,256,256]{2,1,0:T(8,128)}, f32[2,256,256]{2,1,0:T(8,128)}) custom-call(f32[2,256,128]{2,1,0:T(8,128)} %pad_maximum_fusion.info, bf16[2,256,384]{2,1,0:T(8,128)(2,1)} %pad.24.w_dec, f32[16,2,5,256,256]{4,3,2,1,0:T(8,128)} %get-tuple-element.24.acts, ...), custom_call_target="tpu_custom_call" | custom-call | tf_op jit(solution)/shard_map/backward_visits/pallas_call | solution.py:577
  502.3 8.6 %bitcast_reduce_fusion = (bf16[2,1024]{1,0:T(2,128)(2,1)S(1)}, f32[2,275,1024,1]{2,1,3,0:T(8,128)S(1)}) fusion(bf16[16,2,256,1024]{3,2,1,0:T(8,128)(2,1)} %get-tuple-element.28, s32[16,2,256]{2,0,1:T(8,128)S(1)} %get-tuple-element.100), kind=kOutput, calls=%fused_computation.13 | convolution fusion | flops 4616548352 | bytes 19066880 | tf_op jit(solution)/shard_map/sdbv,sdbc->dvc/dot_general | solution.py:613
  510.9 1.9 fusion.13
  512.9 1.9 slice.34
  514.9 1.2 fusion.19
  516.6 1.2 copy.116
  517.9 51.3 %fusion = bf16[2,8,256,1024,1]{3,2,1,0,4:T(8,128)(2,1)} fusion(bf16[16,2,8,256,256]{4,3,2,1,0:T(8,128)(2,1)} %get-tuple-element.29, bf16[16,2,256,1024]{3,2,1,0:T(8,128)(2,1)} %get-tuple-element.28), kind=kOutput, calls=%fused_computation.2 | convolution fusion | flops 34359738368 | bytes 58720256 | tf_op jit(solution)/shard_map/sdnbu,sdbc->dnuc/dot_general | solution.py:611
  569.2 8.0 copy.151
  577.2 8.0 copy.118
  588.4 41.6 %all-reduce.5 = (f32[]{:T(128)}, f32[2,275]{1,0:T(2,128)}, f32[2]{0:T(128)S(1)}, f32[2]{0:T(128)S(1)}) all-reduce(f32[]{:T(128)S(6)} %mul.42, f32[2,275]{1,0:T(2,128)S(1)} %slice_multiply_fusion, f32[2]{0:T(128)S(1)} %reduce_sum.72, f32[2]{0:T(128)S(1)} %broadcast_multiply_fusion), channel_id=1, replica_groups=mesh['seq'=4,'mp'=8] {'seq','mp'}, use_global_device_ids=true, to_apply=%region_2.3 | all-reduce | flops 555 | bytes 4440 | tf_op jit(solution)/shard_map/psum | solution.py:667
  631.1 7.6 all-reduce.8.cloned.1.call-done
  638.8 1.8 copy.121
  640.6 22.7 %reduce-scatter.8.cloned.1.call-done = bf16[2,64,275]{2,1,0:T(8,128)(2,1)} async-done(((bf16[2,256,275]{2,1,0:T(8,128)(2,1)}), bf16[2,64,275]{2,1,0:T(8,128)(2,1)}) %reduce-scatter.8.cloned.1.call-update) | async-done | bytes 70416 | tf_op jit(solution)/shard_map/reduce_scatter | solution.py:666
  663.3 1.6 convert_element_type.99
  664.9 21.1 %reduce-scatter.4.cloned.1.call-done = bf16[2,101,256]{1,2,0:T(8,128)(2,1)} async-done(((bf16[2,101,1024]{1,2,0:T(8,128)(2,1)}), bf16[2,101,256]{1,2,0:T(8,128)(2,1)}) %reduce-scatter.4.cloned.1.call-update) | async-done | bytes 103440 | tf_op jit(solution)/shard_map/reduce_scatter | solution.py:665
  687.7 1.7 convert_reduce_fusion
  689.4 141.5 %reduce-scatter.6.cloned.1.call-done = bf16[2,512,1024]{2,1,0:T(8,128)(2,1)} async-done(((bf16[2,2048,1024]{2,1,0:T(8,128)(2,1)}), bf16[2,512,1024]{2,1,0:T(8,128)(2,1)}) %reduce-scatter.6.cloned.1.call-update) | async-done | bytes 2097168 | tf_op jit(solution)/shard_map/reduce_scatter | solution.py:664
  830.9 2.9 copy.119
  833.7 1.3 convolution_convert_fusion
  835.1 2.7 bitcast_convert_fusion.1
  837.7 5.3 copy.123
  (74 shorter events, 18.6 us)
Async XLA Ops:
  7.2 66.8 %all-gather.3.cloned.1.call-start = ((), (), s32[]{:S(2)}) async-start(), calls=%async_computation.3 | async-start | bytes 2534400 | tf_op jit(solution)/shard_map/all_gather | solution.py:634
  7.9 630.9 %all-reduce.8.cloned.1.call-start = ((), (), s32[]{:S(2)}) async-start(), calls=%async_computation.4 | async-start | bytes 573440 | tf_op jit(solution)/shard_map/psum | solution.py:667
  36.8 13.7 %copy-start = (bf16[2,100,1024]{2,1,0:T(8,128)(2,1)}, bf16[2,100,1024]{2,1,0:T(8,128)(2,1)S(1)}, u32[]{:S(2)}) copy-start(bf16[2,100,1024]{2,1,0:T(8,128)(2,1)S(1)} %reshape.126) | copy-start | bytes 1228804
  502.3 8.6 %copy-start.1 = (bf16[2,100,1024]{2,1,0:T(8,128)(2,1)S(1)}, bf16[2,100,1024]{2,1,0:T(8,128)(2,1)}, u32[]{:S(2)}) copy-start(bf16[2,100,1024]{2,1,0:T(8,128)(2,1)} %copy-done) | copy-start | bytes 1228804
  502.3 12.6 %copy-start.2 = (bf16[2,275,100]{2,0,1:T(2,128)(2,1)S(1)}, bf16[2,275,100]{2,0,1:T(2,128)(2,1)}, u32[]{:S(2)}) copy-start(bf16[2,275,100]{2,0,1:T(2,128)(2,1)} %param.16) | copy-start | bytes 330004
  512.9 150.4 %reduce-scatter.8.cloned.1.call-start = ((), (), s32[]{:S(2)}) async-start(), calls=%async_computation.7 | async-start | bytes 491520 | tf_op jit(solution)/shard_map/reduce_scatter | solution.py:666
  514.9 171.1 %reduce-scatter.4.cloned.1.call-start = ((), (), s32[]{:S(2)}) async-start(), calls=%async_computation.5 | async-start | bytes 655360 | tf_op jit(solution)/shard_map/reduce_scatter | solution.py:665
  517.9 313.0 %reduce-scatter.6.cloned.1.call-start = ((), (), s32[]{:S(2)}) async-start(), calls=%async_computation.6 | async-start | bytes 10485760 | tf_op jit(solution)/shard_map/reduce_scatter | solution.py:664
  585.2 1.7 copy-start.7
  585.2 2.9 copy-start.6
  585.2 3.0 copy-start.5
  585.2 3.1 copy-start.8
  835.1 8.0 copy-start.4
  835.1 8.8 %copy-start.3 = (f32[2,256,256]{2,1,0:T(8,128)S(1)}, f32[2,256,256]{2,1,0:T(8,128)}, u32[]{:S(2)}) copy-start(f32[2,256,256]{2,1,0:T(8,128)} %get-tuple-element.120) | copy-start | bytes 1572868
Sparse Core Ops, SparseCore 0:
  9.9 40.4 all-gather.2
  513.0 125.7 all-reduce.7
  641.7 21.5 reduce-scatter.7
  666.0 19.9 reduce-scatter.3
  688.1 142.6 reduce-scatter.5

commit v3 on v2

--- a/solution.py
+++ b/solution.py
@@ -144,7 +144,7 @@
 MESH = pl.DeviceIdType.MESH
 LANES = 128
 VOCAB_PAD = 384
-CHUNK = 32
+CHUNK = 256
 NT = (((1,), (1,)), ((), ()))
 TN = (((0,), (0,)), ((), ()))
 
@@ -184,6 +184,10 @@
 
 def other_core(peer):
     return (peer // 2) * 2 + (1 - peer % 2)
+
+
+def folded(x):
+    return jnp.sum(x.reshape(x.shape[0] // 8, 8, x.shape[1]), axis=0)
 
 
 def column_of(table, lane):
@@ -266,7 +270,7 @@
                 hidden = jnp.where(live, out_gate * jnp.tanh(new), before).astype(jnp.bfloat16)
                 buf[d, later, me, at, lanes] = hidden
                 wide = hidden.astype(jnp.float32)
-                hidden_sq[d] += jnp.where(live, wide * wide, 0.0)
+                hidden_sq[d] += folded(jnp.where(live, wide * wide, 0.0))
             return carry
 
         lax.fori_loop(0, rows // CHUNK, chunk, 0)
@@ -293,16 +297,16 @@
             power = jnp.exp(value - top)
             total = jnp.sum(power, axis=1, keepdims=True)
             picked = jnp.sum(jnp.where(hot, value, 0.0), axis=1, keepdims=True)
-            loss[d] += jnp.broadcast_to(jnp.where(valid, top + jnp.log(total) - picked, 0.0), (CHUNK, LANES))
+            loss[d] += folded(jnp.broadcast_to(jnp.where(valid, top + jnp.log(total) - picked, 0.0), (CHUNK, LANES)))
             kept = jnp.where(valid & (lanes < letters), value, 0.0)
             square = kept * kept
-            logit_sq[d] += sum(square[:, n * LANES:(n + 1) * LANES] for n in range(VOCAB_PAD // LANES))
+            logit_sq[d] += folded(sum(square[:, n * LANES:(n + 1) * LANES] for n in range(VOCAB_PAD // LANES)))
             slope = jnp.where(
                 valid, (power * (1.0 / total) - jnp.where(hot, 1.0, 0.0)) * scale, 0.0
             ).astype(jnp.bfloat16)
             grad[d, at, :] = slope
             wide = slope.astype(jnp.float32)
-            dec_bias[d] += sum(wide[n * 8:(n + 1) * 8] for n in range(CHUNK // 8))
+            dec_bias[d] += folded(wide)
             return carry
 
         lax.fori_loop(0, rows // CHUNK, chunk, 0)
@@ -389,9 +393,9 @@
 
 
 def backward_kernel(
-    length, info, w_dec, acts, grads, w_hbm,
-    pres, hidden_grad, cell_grad,
-    w, stage, grad, pre, held, own, sent, got, passed, taken, load_sem, act_sem, grad_sem, pre_sem,
+    length, info, ids, w_dec, acts, grads, wholes, w_hbm,
+    rec_out, letter_grad, hidden_grad, cell_grad,
+    w, rec, stage, grad, whole, pre, held, own, sent, got, passed, taken, load_sem, act_sem, grad_sem, whole_sem,
     core_send, core_recv, chip_send, chip_recv,
 ):
     me, sibling, peers = neighbours()
@@ -406,16 +410,25 @@
     def load_grad(d, step):
         return pltpu.make_async_copy(grads.at[step, d], grad.at[d], grad_sem.at[d])
 
-    def save_pre(d, step):
-        return pltpu.make_async_copy(pre.at[d], pres.at[step, d], pre_sem.at[d])
+    def load_whole(d, step):
+        return pltpu.make_async_copy(wholes.at[step, d], whole.at[d], whole_sem.at[d])
 
     for d in range(2):
         load_acts(d, length - 1).start()
         load_grad(d, length - 1).start()
+        load_whole(d, length - 1).start()
     greet((sibling,) + peers)
     held[...] = jnp.zeros(held.shape, held.dtype)
     own[...] = jnp.zeros(own.shape, own.dtype)
     cell_grad[...] = jnp.zeros(cell_grad.shape, cell_grad.dtype)
+    letter_grad[...] = jnp.zeros(letter_grad.shape, letter_grad.dtype)
+
+    def clear(b, carry):
+        for d in range(2):
+            rec[d, b] = jnp.zeros(rec.shape[2:], rec.dtype)
+        return carry
+
+    lax.fori_loop(0, w.shape[1], clear, 0)
 
     def to_core(d, turn, n):
         return remote(
@@ -438,7 +451,6 @@
         def _():
             for n in range(3):
                 to_chip(d, turn - 1, n).wait_recv()
-            save_pre(d, step + 1).wait()
 
         def chunk(i, carry):
             at = pl.ds(pl.multiple_of(i * CHUNK, CHUNK), CHUNK)
@@ -467,7 +479,6 @@
             return carry
 
         lax.fori_loop(0, rows // CHUNK, chunk, 0)
-        save_pre(d, step).start()
 
         @pl.when(turn < length - 1)
         def _():
@@ -498,6 +509,18 @@
                 to_chip(d, turn, n).start()
             else:
                 own[d] = share
+        load_whole(d, step).wait()
+
+        for b in range(w.shape[1]):
+            rec[d, b] += matmul(whole[d, b], pre[d], TN)
+
+        @pl.when(turn < length - 1)
+        def _():
+            load_whole(d, step - 1).start()
+
+        letters = lax.broadcasted_iota(jnp.int32, (VOCAB_PAD, rows), 0).astype(jnp.float32)
+        hot = letters == ids[d, pl.ds(step, 1), :]
+        letter_grad[d] += matmul(hot.astype(jnp.bfloat16), pre[d])
 
     def both(turn, carry):
         for d in range(2):
@@ -512,14 +535,23 @@
         for n in range(3):
             total += taken[d, (length - 1) % 2, n].astype(jnp.float32)
         hidden_grad[d] = total
-        save_pre(d, 0).wait()
         for n in range(4):
             to_core(d, length - 1, n).wait_send()
         for n in range(3):
             to_chip(d, length - 1, n).wait_send()
 
-
-def kernel_recurrences(step_ids, own_len, h_init, c_init, embed, w_in, w_rec, bias, w_dec, wd_full, b_dec, count):
+    def narrow(b, carry):
+        for d in range(2):
+            w[d, b] = rec[d, b].astype(jnp.bfloat16)
+        return carry
+
+    lax.fori_loop(0, w.shape[1], narrow, 0)
+    store = pltpu.make_async_copy(w, rec_out, load_sem)
+    store.start()
+    store.wait()
+
+
+def kernel_step(step_ids, own_len, h_init, c_init, embed, w_in, w_rec, bias, w_dec, wd_full, b_dec, count, matrix):
     length, rows = step_ids.shape[1:]
     letters, width = embed.shape[1:]
     units, columns = h_init.shape[2], w_rec.shape[2]
@@ -545,9 +577,9 @@
             shape((length, 2, blocks, rows, units), bf16),
             shape((length, 2, 5, rows, units), f32),
             shape((length, 2, rows, VOCAB_PAD), bf16),
-            shape((2, CHUNK, LANES), f32),
-            shape((2, CHUNK, LANES), f32),
-            shape((2, CHUNK, LANES), f32),
+            shape((2, 8, LANES), f32),
+            shape((2, 8, LANES), f32),
+            shape((2, 8, LANES), f32),
             shape((2, 8, VOCAB_PAD), f32),
             shape((2, units, VOCAB_PAD), f32),
         ),
@@ -574,19 +606,22 @@
         ),
         name="forward_visits",
     )(info, inverse, h_init, c_init, embed_pad, w_in_pad, bias[:, None], b_dec_pad, wd_pad, w_blocks)
-    pres, hidden_grad, cell_grad = pl.pallas_call(
+    rec_grad, letter_grad, hidden_grad, cell_grad = pl.pallas_call(
         functools.partial(backward_kernel, length),
         out_shape=(
-            shape((length, 2, rows, columns), bf16),
+            shape((2, blocks, units, columns), bf16),
+            shape((2, VOCAB_PAD, columns), f32),
             shape((2, rows, units), f32),
             shape((2, rows, units), f32),
         ),
-        in_specs=[vmem] * 2 + [any_space] * 3,
-        out_specs=(any_space, vmem, vmem),
+        in_specs=[vmem] * 3 + [any_space] * 4,
+        out_specs=(any_space, vmem, vmem, vmem),
         scratch_shapes=[
             pltpu.VMEM((2, blocks, units, columns), bf16),
+            pltpu.VMEM((2, blocks, units, columns), f32),
             pltpu.VMEM((2, 5, rows, units), f32),
             pltpu.VMEM((2, rows, VOCAB_PAD), bf16),
+            pltpu.VMEM((2, blocks, rows, units), bf16),
             pltpu.VMEM((2, rows, columns), bf16),
             pltpu.VMEM((2, rows, units), f32),
             pltpu.VMEM((2, rows, units), f32),
@@ -607,26 +642,364 @@
             collective_id=1, has_side_effects=True, vmem_limit_bytes=VMEM_LIMIT
         ),
         name="backward_visits",
-    )(info, w_dec_pad, acts, grads, w_blocks)
-    rec_grad = jnp.einsum("sdnbu,sdbc->dnuc", wholes, pres, preferred_element_type=f32)
-    onehot = (jnp.swapaxes(step_ids, 0, 1)[..., None] == jnp.arange(letters, dtype=jnp.int32)).astype(bf16)
-    letter_grad = jnp.einsum("sdbv,sdbc->dvc", onehot, pres, preferred_element_type=f32)
+    )(info, step_ids.astype(f32), w_dec_pad, acts, grads, wholes, w_blocks)
+    rec_part, edge_part, dec_part, small = kernel_sums(
+        rec_grad, letter_grad, embed_pad, w_in_pad, matrix, width, letters, dec_grad,
+        (loss, logit_sq, hidden_sq, dec_bias),
+    )
+    at = 2 * TABLE
     return (
-        jnp.sum(loss[:, :, 0]),
-        jnp.sum(hidden_sq, axis=(1, 2)),
-        jnp.sum(logit_sq, axis=(1, 2)),
-        jnp.sum(dec_bias, axis=1)[:, :letters],
-        dec_grad[:, :, :letters],
+        small[at, 0],
+        jnp.sum(small[at + 3:at + 5], axis=1),
+        jnp.sum(small[at + 1:at + 3], axis=1),
+        small[at + 5:at + 5 + 2 * (VOCAB_PAD // LANES)].reshape(2, VOCAB_PAD)[:, :letters],
+        dec_part[:, :, :letters],
         hidden_grad,
         cell_grad,
-        rec_grad.reshape(2, blocks * units, columns),
-        letter_grad,
+        rec_part.reshape(2, -1, columns),
+        edge_part[:, :width],
+        edge_part[:, width],
+        small[:at].reshape(2, TABLE, LANES)[:, :letters, :width],
+    )
+
+
+PIECE = 128
+LAG = 3
+WINDOW = 3
+TABLE = 280
+
+
+def spread(letter_grad, other, dims):
+    high = letter_grad.astype(jnp.bfloat16)
+    low = (letter_grad - high.astype(jnp.float32)).astype(jnp.bfloat16)
+    return matmul(high, other, dims) + matmul(low, other, dims)
+
+
+def reduce_kernel(
+    width, rec_hbm, letter_grad, embed, w_in, matrix, dec_grad, loss, logit_sq, hidden_sq, dec_bias,
+    rec_out, edge_out, dec_out, small_out,
+    own, ahead, behind, edge, edge_in, dec, dec_in, small, part, small_in, part_in, summed,
+    load_sem, line_send, line_recv, back_send, back_recv, edge_send, edge_recv, dec_send, dec_recv,
+    scatter_send, scatter_recv, seq_send, seq_recv, gather_send, gather_recv,
+):
+    seq, me = lax.axis_index("seq"), lax.axis_index("mp")
+    count, parts = own.shape[1], own.shape[2]
+    peers = lax.axis_size("mp")
+    share = small.shape[0] // peers
+    half = seq // (count // 2)
+    place = seq + half * (count - 1 - 2 * seq)
+    onward = 1 - 2 * half
+    inner = count // 2 - 1
+    lag = LAG + (inner - place) * 5
+    load = pltpu.make_async_copy(rec_hbm, own, load_sem)
+    load.start()
+
+    def other_seq(n):
+        return (seq + n) % count
+
+    def other_mp(n):
+        return (me + n) % peers
+
+    barrier = pltpu.get_barrier_semaphore()
+    for n in range(1, count):
+        pl.semaphore_signal(barrier, inc=1, device_id=(other_seq(n), me), device_id_type=MESH)
+    for n in range(1, peers):
+        pl.semaphore_signal(barrier, inc=1, device_id=(seq, other_mp(n)), device_id_type=MESH)
+    pl.semaphore_wait(barrier, count + peers - 2)
+    load.wait()
+
+    def send(src, dst, send_sem, recv_sem, seq_to, mp_to):
+        return pltpu.make_async_remote_copy(
+            src_ref=src, dst_ref=dst, send_sem=send_sem, recv_sem=recv_sem,
+            device_id=(seq_to, mp_to), device_id_type=MESH,
+        )
+
+    def actual(chunk):
+        return chunk + half * (count - 1 - 2 * chunk)
+
+    pieces = 2 * parts
+
+    def slot(k):
+        return k // pieces, (k % pieces) // parts, k % parts
+
+    def piece(chunk, d, r):
+        return own.at[d, actual(chunk), r]
+
+    def line_copy(k, crossing):
+        i, d, r = slot(k)
+        target = behind.at[i, d, r] if crossing else ahead.at[i, d, r]
+        sem = back_recv.at[i, d, r] if crossing else line_recv.at[i, d, r]
+        return send(piece(count - 1 - i, d, r), target, line_send.at[i, d, r], sem, seq + onward, me)
+
+    def back_copy(k):
+        i, d, r = slot(k)
+        return send(
+            piece(i, d, r), behind.at[i, d, r], back_send.at[i, d, r], back_recv.at[i, d, r], seq - onward, me
+        )
+
+    def add(chunk, d, r, term):
+        ref = piece(chunk, d, r)
+        ref[...] = (ref[...].astype(jnp.float32) + term[...].astype(jnp.float32)).astype(jnp.bfloat16)
+
+    def line(k):
+        i, d, r = slot(k)
+
+        @pl.when((place > 0) & (i <= count - 1 - place))
+        def _():
+            line_copy(k, False).wait_recv()
+            add(count - 1 - i, d, r, ahead.at[i, d, r])
+
+        @pl.when((place == 0) & (k >= WINDOW))
+        def _():
+            line_copy(k - WINDOW, False).wait_send()
+
+        @pl.when((i <= count - 2 - place) & (place < inner))
+        def _():
+            line_copy(k, False).start()
+
+        @pl.when((i <= count - 2 - place) & (place == inner))
+        def _():
+            line_copy(k, True).start()
+
+    def back(k):
+        i, d, r = slot(k)
+
+        @pl.when(i <= place)
+        def _():
+            back_copy(k).wait_recv()
+            add(i, d, r, behind.at[i, d, r])
+
+        @pl.when(i < place)
+        def _():
+            back_copy(k).start()
+
+    def advance(k, carry):
+        @pl.when(k < (count - 1) * pieces)
+        def _():
+            line(k)
+
+        @pl.when((k >= lag) & (k - lag < (count // 2) * pieces))
+        def _():
+            back(k - lag)
+
+        return carry
+
+    def edge_copy(n):
+        to = other_seq(n)
+        return send(edge.at[to], edge_in.at[n - 1], edge_send.at[n - 1], edge_recv.at[n - 1], to, me)
+
+    def dec_copy(n):
+        to = other_seq(n)
+        return send(dec.at[to], dec_in.at[n - 1], dec_send.at[n - 1], dec_recv.at[n - 1], to, me)
+
+    def scatter_copy(n):
+        to = other_mp(n)
+        rows = pl.ds(pl.multiple_of(to * share, 8), share)
+        return send(small.at[rows], small_in.at[n - 1], scatter_send.at[n - 1], scatter_recv.at[n - 1], seq, to)
+
+    def seq_copy(n):
+        return send(part, part_in.at[n - 1], seq_send.at[n - 1], seq_recv.at[n - 1], other_seq(n), me)
+
+    own_rows = pl.ds(pl.multiple_of(me * share, 8), share)
+
+    def gather_copy(n):
+        return send(
+            summed.at[own_rows], summed.at[own_rows], gather_send.at[n - 1], gather_recv.at[me], seq, other_mp(n)
+        )
+
+    def gather_arrival(n):
+        source = other_mp(n)
+        rows = pl.ds(pl.multiple_of(source * share, 8), share)
+        return send(summed.at[rows], summed.at[rows], gather_send.at[n - 1], gather_recv.at[source], seq, source)
+
+    start = 6
+    lax.fori_loop(0, 2, advance, 0)
+    first = jnp.where(me == 0, 1.0, 0.0)
+    for d in range(2):
+        small[d * TABLE:(d + 1) * TABLE] = spread(letter_grad[d], w_in[d], NT)[:TABLE]
+    small[2 * TABLE:] = jnp.zeros((small.shape[0] - 2 * TABLE, LANES), jnp.float32)
+    at = 2 * TABLE
+    small[at:at + 1] = jnp.sum(loss[0] + loss[1], axis=0, keepdims=True) * first
+    for d in range(2):
+        small[at + 1 + d:at + 2 + d] = jnp.sum(logit_sq[d], axis=0, keepdims=True) * first
+        small[at + 3 + d:at + 4 + d] = jnp.sum(hidden_sq[d], axis=0, keepdims=True)
+        row = jnp.sum(dec_bias[d], axis=0, keepdims=True) * first
+        for n in range(VOCAB_PAD // LANES):
+            line_at = at + 5 + d * (VOCAB_PAD // LANES) + n
+            small[line_at:line_at + 1] = row[:, n * LANES:(n + 1) * LANES]
+    for n in range(1, peers):
+        scatter_copy(n).start()
+    rows = edge.shape[2]
+    span = matrix.shape[0]
+    wide = own.shape[-1] // count
+    for d in range(2):
+        full = spread_left(embed[d], letter_grad[d]).astype(jnp.bfloat16)
+        flat = [
+            matmul(full[:, g * span:(g + 1) * span], matrix[...], NT).astype(jnp.bfloat16)
+            for g in range(own.shape[-1] // span)
+        ]
+        for q in range(count):
+            group, offset = (q * wide) // span, (q * wide) % span
+            edge[q, d] = flat[group][:rows, offset:offset + wide]
+            depth = dec.shape[2]
+            dec[q, d] = dec_grad[d, q * depth:(q + 1) * depth].astype(jnp.bfloat16)
+    for n in range(1, count):
+        edge_copy(n).start()
+        dec_copy(n).start()
+    lax.fori_loop(2, start, advance, 0)
+    for n in range(1, peers):
+        scatter_copy(n).wait()
+    total = small[own_rows, :]
+    for n in range(1, peers):
+        total += small_in[n - 1]
+    part[...] = total
+    for n in range(1, count):
+        seq_copy(n).start()
+    lax.fori_loop(start, 2 * start, advance, 0)
+    for n in range(1, count):
+        seq_copy(n).wait()
+        total += part_in[n - 1]
+    summed[own_rows, :] = total
+    for n in range(1, peers):
+        gather_copy(n).start()
+    lax.fori_loop(2 * start, (count - 1) * pieces + LAG, advance, 0)
+    for n in range(1, peers):
+        gather_copy(n).wait_send()
+        gather_arrival(n).wait_recv()
+    small_out[...] = summed[...]
+    for n in range(1, count):
+        edge_copy(n).wait()
+        dec_copy(n).wait()
+    for d in range(2):
+        edge_out[d] = edge[seq, d].astype(jnp.float32) + sum(
+            edge_in[n, d].astype(jnp.float32) for n in range(count - 1)
+        )
+        dec_out[d] = dec[seq, d].astype(jnp.float32) + sum(
+            dec_in[n, d].astype(jnp.float32) for n in range(count - 1)
+        )
+        for r in range(parts):
+            for g in range(own.shape[-1] // span):
+                columns = slice(g * span, (g + 1) * span)
+                rec_out[d, r, :, columns] = matmul(own[d, seq, r, :, columns], matrix[...], NT)
+
+    def finish(k, carry):
+        i, d, r = slot(k)
+
+        @pl.when((i <= count - 2 - place) & ((place > 0) | (k >= (count - 1) * pieces - WINDOW)))
+        def _():
+            line_copy(k, False).wait_send()
+
+        @pl.when((i < place) & (k < (count // 2) * pieces))
+        def _():
+            back_copy(k).wait_send()
+
+        return carry
+
+    lax.fori_loop(0, (count - 1) * pieces, finish, 0)
+
+
+def spread_left(other, letter_grad):
+    high = letter_grad.astype(jnp.bfloat16)
+    low = (letter_grad - high.astype(jnp.float32)).astype(jnp.bfloat16)
+    return matmul(other, high, TN) + matmul(other, low, TN)
+
+
+def kernel_sums(rec_grad, letter_grad, embed_pad, w_in_pad, matrix, width, letters, dec_grad, stats):
+    count = lax.axis_size("seq")
+    peers = lax.axis_size("mp")
+    columns = rec_grad.shape[-1]
+    all_rows = rec_grad.shape[1] * rec_grad.shape[2]
+    parts = all_rows // count // PIECE
+    units = dec_grad.shape[1]
+    edge_rows = -(-(width + 1) // 8) * 8
+    small_rows = -(-(2 * TABLE + 16) // (8 * peers)) * 8 * peers
+    share = small_rows // peers
+    f32, bf16 = jnp.float32, jnp.bfloat16
+    dma = pltpu.SemaphoreType.DMA
+    shape = jax.ShapeDtypeStruct
+    vmem = pl.BlockSpec(memory_space=pltpu.VMEM)
+    ones = (jnp.arange(VOCAB_PAD) < letters).astype(bf16)
+    embed_one = embed_pad.at[:, :, width].set(ones[None])
+    return pl.pallas_call(
+        functools.partial(reduce_kernel, width),
+        out_shape=(
+            shape((2, parts, PIECE, columns), f32),
+            shape((2, edge_rows, columns // count), f32),
+            shape((2, units // count, VOCAB_PAD), f32),
+            shape((small_rows, LANES), f32),
+        ),
+        in_specs=[pl.BlockSpec(memory_space=pl.ANY)] + [vmem] * 9,
+        out_specs=(vmem,) * 4,
+        scratch_shapes=[
+            pltpu.VMEM((2, count, parts, PIECE, columns), bf16),
+            pltpu.VMEM((count - 1, 2, parts, PIECE, columns), bf16),
+            pltpu.VMEM((count // 2, 2, parts, PIECE, columns), bf16),
+            pltpu.VMEM((count, 2, edge_rows, columns // count), bf16),
+            pltpu.VMEM((count - 1, 2, edge_rows, columns // count), bf16),
+            pltpu.VMEM((count, 2, units // count, VOCAB_PAD), bf16),
+            pltpu.VMEM((count - 1, 2, units // count, VOCAB_PAD), bf16),
+            pltpu.VMEM((small_rows, LANES), f32),
+            pltpu.VMEM((share, LANES), f32),
+            pltpu.VMEM((peers - 1, share, LANES), f32),
+            pltpu.VMEM((count - 1, share, LANES), f32),
+            pltpu.VMEM((small_rows, LANES), f32),
+            dma,
+            dma((count - 1, 2, parts)),
+            dma((count - 1, 2, parts)),
+            dma((count // 2, 2, parts)),
+            dma((count // 2, 2, parts)),
+            dma((count - 1,)),
+            dma((count - 1,)),
+            dma((count - 1,)),
+            dma((count - 1,)),
+            dma((peers - 1,)),
+            dma((peers - 1,)),
+            dma((count - 1,)),
+            dma((count - 1,)),
+            dma((peers - 1,)),
+            dma((peers,)),
+        ],
+        compiler_params=pltpu.CompilerParams(
+            collective_id=2, has_side_effects=True, vmem_limit_bytes=VMEM_LIMIT
+        ),
+        name="gradient_sums",
+    )(
+        rec_grad.reshape(2, count, parts, PIECE, columns), letter_grad, embed_one, w_in_pad, matrix, dec_grad,
+        *stats,
+    )
+
+
+def plain_step(
+    step_ids, own_len, h_init, c_init, embed, w_in, w_rec, bias, w_dec, wd_full, b_dec, count, matrix
+):
+    lanes = matrix.shape[0] // 4
+    first_mp = (lax.axis_index("mp") == 0).astype(jnp.float32)
+    loss, hidden_sq, logit_sq, dec_bias, dec_grad, hidden_grad, cell_grad, rec_grad, letter_grad = recurrences(
+        step_ids, own_len, h_init, c_init, embed, w_in, w_rec, bias, w_dec, wd_full,
+        b_dec, count, lanes,
+    )
+    embed_wide = embed.astype(jnp.float32)
+    in_grad = jnp.einsum("dve,dvc->dec", embed_wide, letter_grad, precision=lax.Precision.HIGHEST)
+    bias_grad = jnp.sum(letter_grad, axis=1, keepdims=True)
+    embed_part = jnp.einsum(
+        "dvc,dec->dve", letter_grad, w_in.astype(jnp.float32), precision=lax.Precision.HIGHEST
+    )
+    edge = ungrouped_wide(jnp.concatenate([in_grad, bias_grad], axis=1), lanes)
+    rec_part = lax.psum_scatter(rec_grad.astype(jnp.bfloat16), "seq", scatter_dimension=1, tiled=True)
+    edge_part = lax.psum_scatter(edge.astype(jnp.bfloat16), "seq", scatter_dimension=2, tiled=True)
+    dec_part = lax.psum_scatter(dec_grad.astype(jnp.bfloat16), "seq", scatter_dimension=1, tiled=True)
+    loss_sum, hidden_all, logit_all, dec_bias_grad, embed_grad = lax.psum(
+        (loss * first_mp, hidden_sq, logit_sq * first_mp, dec_bias * first_mp, embed_part), ("seq", "mp")
+    )
+    rec_out = ungrouped(rec_part, matrix).astype(jnp.float32)
+    return (
+        loss_sum, hidden_all, logit_all, dec_bias_grad, dec_part.astype(jnp.float32), hidden_grad, cell_grad, rec_out,
+        edge_part[:, :-1].astype(jnp.float32), edge_part[:, -1].astype(jnp.float32), embed_grad,
     )
 
 
 def per_device(ids, lengths, order, h_init, c_init, embed, w_in, w_rec, bias, w_dec, b_dec):
     seq_rank = lax.axis_index("seq")
-    first_mp = (lax.axis_index("mp") == 0).astype(jnp.float32)
     streams = ids.shape[1]
     per_dev = h_init.shape[1]
     own_units, all_units = h_init.shape[2], w_rec.shape[1]
@@ -647,37 +1020,25 @@
     ).reshape(bias.shape)
     operands = (
         step_ids, own_len, h_init, c_init, embed, w_in_grouped, w_rec_grouped, bias_grouped, w_dec, wd_full,
-        b_dec, count,
-    )
-    if lax.axis_size("mp") == 8 and own_units % LANES == 0 and per_dev % CHUNK == 0:
-        results = kernel_recurrences(*operands)
+        b_dec, count, matrix,
+    )
+    fits = own_units % LANES == 0 and per_dev == CHUNK and all_units % (lax.axis_size("seq") * PIECE) == 0
+    if lax.axis_size("mp") == 8 and lax.axis_size("seq") == 4 and fits:
+        results = kernel_step(*operands)
     else:
-        results = recurrences(*operands, lanes)
-    loss, hidden_sq, logit_sq, dec_bias, dec_grad, hidden_grad, cell_grad, rec_grad, letter_grad = results
+        results = plain_step(*operands)
+    loss_sum, hidden_all, logit_all, dec_bias_grad, dec_part, hidden_grad, cell_grad, rec_out, in_out, bias_out, embed_grad = results
     embed_wide = embed.astype(jnp.float32)
-    in_grad = jnp.einsum("dve,dvc->dec", embed_wide, letter_grad, precision=lax.Precision.HIGHEST)
-    bias_grad = jnp.sum(letter_grad, axis=1, keepdims=True)
-    embed_part = jnp.einsum(
-        "dvc,dec->dve", letter_grad, w_in_grouped.astype(jnp.float32), precision=lax.Precision.HIGHEST
-    )
-    edge = ungrouped_wide(jnp.concatenate([in_grad, bias_grad], axis=1), lanes)
-    rec_part = lax.psum_scatter(rec_grad.astype(jnp.bfloat16), "seq", scatter_dimension=1, tiled=True)
-    edge_part = lax.psum_scatter(edge.astype(jnp.bfloat16), "seq", scatter_dimension=2, tiled=True)
-    dec_part = lax.psum_scatter(dec_grad.astype(jnp.bfloat16), "seq", scatter_dimension=1, tiled=True)
-    loss_sum, hidden_all, logit_all, dec_bias_grad, embed_grad = lax.psum(
-        (loss * first_mp, hidden_sq, logit_sq * first_mp, dec_bias * first_mp, embed_part), ("seq", "mp")
-    )
-    rec_out = ungrouped(rec_part, matrix).astype(jnp.float32)
     rms_embed = jnp.sqrt(jnp.mean(embed_wide * embed_wide, axis=(1, 2)))
     return (
         loss_sum / count,
         hidden_grad,
         cell_grad,
         embed_grad,
-        edge_part[:, :-1].astype(jnp.float32),
+        in_out,
         rec_out,
-        edge_part[:, -1].astype(jnp.float32),
-        dec_part.astype(jnp.float32),
+        bias_out,
+        dec_part,
         dec_bias_grad,
         rms_embed,
         jnp.sqrt(hidden_all / (all_units * live_total)),

time: 862 us -> 689 us (0.80)
  waiting for transfers between devices: 194 us -> 0.68 us
  Pallas kernels: 421 us -> 577 us
  matrix products: 75.2 us -> 10.9 us
  blocking collectives: 56.7 us -> 15.1 us
  local copies, waits for them, and re-layouts: 74.2 us -> 54.4 us
    reduce_scatter x3 -> x0, waiting for transfers between devices: 185 us -> none  [the longest x1 142 us: per_device(): lax.psum_scatter(rec_grad.astype(jnp.bfloat16), 'seq', scatter_dimension=...]
    pallas_call x2 -> x3, Pallas kernels: 421 us -> 577 us  [the longest x1 215 us: kernel_step(): pl.pallas_call(functools.partial(backward_kernel, length), out_shape=(sha...]
    dot_general x4 -> x0, matrix products: 63 us -> none  [the longest x1 51.3 us: kernel_recurrences(): jnp.einsum('sdnbu,sdbc->dnuc', wholes, pres, preferred_element_type=f32)]
    psum x1 -> x0, blocking collectives: 41.6 us -> none  [per_device(): lax.psum((loss * first_mp, hidden_sq, logit_sq * first_mp, dec_bias * fir...]
    convert_element_type x3 -> x1, local copies, waits for them, and re-layouts: 9.33 us -> 0.13 us  [kernel_step(): ids = jnp.swapaxes(step_ids, 1, 2).astype(jnp.float32)]
    unnamed x29 -> x31, local copies, waits for them, and re-layouts: 27.4 us -> 27.3 us
  transfers between devices with their start and end apart: 5 -> 1, of which waited for: 4 -> 0; matrix products, arithmetic and copies ran while one was open for 15% -> 7% of each run, Pallas kernels for 0% -> 0%
where the time goes in v3:
time: 689 us; the launch traced here: 683 us
  Pallas kernels  577 us (84%)
  local copies, waits for them, and re-layouts  54.4 us (8%)
  between operations  17.4 us (3%)
  blocking collectives  15.1 us (2%)
  matrix products  10.9 us (2%)
  other arithmetic  7.66 us (1%)
    pallas_call x1, Pallas kernels, kernel_step(): pl.pallas_call(functools.partial(backward_kernel, length), out_shape=(sha...  215 us
    pallas_call x1, Pallas kernels, kernel_step(): pl.pallas_call(functools.partial(forward_kernel, length, letters), out_sh...  202 us
    pallas_call x1, Pallas kernels, kernel_sums(): pl.pallas_call(functools.partial(reduce_kernel, width), out_shape=(shape(...  160 us
    unnamed x31, local copies, waits for them, and re-layouts  27.3 us
    all_gather x1, blocking collectives, per_device(): whole_ids = lax.all_gather(ids, 'seq', axis=0, tiled=True)  15.1 us
  transfers between devices with their start and end apart: 1, of which 0 were waited for; matrix products, arithmetic and copies ran while one was open for 7% of the time, Pallas kernels for 0%

profile of v3, /device:TPU:0, one launch (start us, length us, event | category | flops | bytes accessed | tf_op | source)
XLA Modules:
  0.0 683.3 jit_solution(8178551751771499339)
XLA Ops:
  7.9 1.2 copy.54
  9.1 1.3 reduce_sum.40
  10.5 0.8 compare_select_fusion
  11.2 1.9 gather_fusion.1
  13.2 15.1 %all-gather = s32[4,4,1024]{2,1,0:T(4,128)S(1)} all-gather(s32[1,4,1024]{2,1,0:T(4,128)} %bitcast.62), channel_id=1, replica_groups=mesh['seq'=4,'mp'=8] {'seq'}, dimensions={0}, use_global_device_ids=true | all-gather | bytes 81920 | tf_op jit(solution)/shard_map/all_gather | solution.py:1008
  28.5 0.7 gather_fusion
  29.3 0.8 select_convert_fusion
  30.9 10.4 %fusion.3 = bf16[512,2,2048,2]{2,0,3,1:T(8,128)(2,1)} fusion(bf16[2,256,2,8,512]{4,3,2,1,0:T(8,128)(2,1)} %bitcast.65, s32[512]{0:T(512)S(1)} %fusion.19), kind=kOutput, calls=%fused_computation.5 | convolution fusion | flops 4299685888 | bytes 16779264 | tf_op jit(solution)/shard_map/...gc,cp->...gp/dot_general | solution.py:24
  41.3 10.4 %copy.73 = bf16[256,8,8,256]{3,2,1,0:T(8,128)(2,1)} copy(bf16[256,8,8,256]{3,1,2,0:T(8,128)(2,1)} %bitcast.54) | data formatting | bytes 16777216
  51.7 12.3 %copy.68.w_hbm = bf16[2,8,256,1024]{3,2,1,0:T(8,128)(2,1)} copy(bf16[2,8,256,1024]{2,1,3,0:T(8,128)(2,1)} %bitcast.51) | data formatting | bytes 16777216 | tf_op jit(solution)/shard_map/reshape;reshape | solution.py:569
  66.7 0.9 pad.24.w_in
  67.6 0.7 pad.23.embed
  68.6 0.7 copy.58
  69.9 0.8 pad.22.w_dec
  71.8 0.8 pad_maximum_fusion.info
  72.7 0.9 fusion.7.matrix
  73.6 5.2 copy.71
  78.8 2.0 pad.26.clone
  80.8 202.2 %forward_visits.1 = (bf16[16,2,8,256,256]{4,3,2,1,0:T(8,128)(2,1)}, f32[16,2,5,256,256]{4,3,2,1,0:T(8,128)}, bf16[16,2,256,384]{3,2,1,0:T(8,128)(2,1)}, f32[2,8,...) custom-call(f32[2,256,128]{2,1,0:T(8,128)} %pad_maximum_fusion.info,, ...), custom_call_target="tpu_custom_call" | custom-call | tf_op jit(solution)/shard_map/forward_visits/pallas_call | solution.py:574
  283.2 0.8 scatter.4.embed
  283.9 214.9 %backward_visits.1 = (bf16[2,8,256,1024]{3,2,1,0:T(8,128)(2,1)}, f32[2,384,1024]{2,1,0:T(8,128)}, f32[2,256,256]{2,1,0:T(8,128)}, f32[2,256,256]{2,1,0:T(8,128)}) custom-call(f32[2,256,128]{2,1,0:T(8,128)} %pad_maximum_fusion.info, f32[2,16,256]{2,1,0:T(8,128)} %get-tuple-element.96.ids, bf16[2,256,384]{2,1,0:T(8,128)(2,1)} %pad.22.w_dec, ...), custom_call_target="tpu_custom_call" | custom-call | tf_op jit(solution)/shard_map/backward_visits/pallas_call | solution.py:609
  498.8 160.0 %gradient_sums.1 = (f32[2,4,128,1024]{3,2,1,0:T(8,128)}, f32[2,104,256]{2,1,0:T(8,128)}, f32[2,64,384]{2,1,0:T(8,128)}, f32[576,128]{1,0:T(8,128)}) custom-call(bf16[2,4,4,128,1024]{4,3,2,1,0:T(8,128)(2,1)} %bitcast.53, f32[2,384,1024]{2,1,0:T(8,128)} %get-tuple-element.44.letter_grad, bf16[2,384,128]{2,1,0:T(8,128)(2,1)} %copy-done.1, ...), custom_call_target="tpu_custom_call" | custom-call | tf_op jit(solution)/shard_map/gradient_sums/pallas_call | solution.py:923
  658.9 0.9 slice_reduce_fusion
  659.8 1.0 slice.51
  660.8 0.7 slice.56
  661.5 1.2 slice.50
  662.7 0.9 copy.70
  663.5 0.7 slice.54
  664.2 1.7 copy.64
  668.3 0.8 copy.89
  669.1 0.8 copy.90
  669.9 4.8 copy.91
  (50 shorter events, 7.7 us)
Async XLA Ops:
  7.2 66.4 %all-gather.3.cloned.1.call-start = ((), (), s32[]{:S(2)}) async-start(), calls=%async_computation | async-start | bytes 2534400 | tf_op jit(solution)/shard_map/all_gather | solution.py:1007
  51.7 12.3 %copy-start.5 = (bf16[2,100,1024]{2,0,1:T(2,128)(2,1)S(1)}, bf16[2,100,1024]{2,0,1:T(2,128)(2,1)}, u32[]{:S(2)}) copy-start(bf16[2,100,1024]{2,0,1:T(2,128)(2,1)} %param.19) | copy-start | bytes 1228804
  51.7 15.0 %copy-start.2 = (bf16[2,275,100]{2,0,1:T(2,128)(2,1)S(1)}, bf16[2,275,100]{2,0,1:T(2,128)(2,1)}, u32[]{:S(2)}) copy-start(bf16[2,275,100]{2,0,1:T(2,128)(2,1)} %param.18) | copy-start | bytes 330004
  51.7 16.6 %copy-start.7 = (f32[2,1024]{1,0:T(2,128)S(1)}, f32[2,1024]{1,0:T(2,128)}, u32[]{:S(2)}) copy-start(f32[2,1024]{1,0:T(2,128)} %param.21) | copy-start | bytes 24580
  51.7 17.5 %copy-start.8 = (f32[2,275]{1,0:T(2,128)S(1)}, f32[2,275]{1,0:T(2,128)}, u32[]{:S(2)}) copy-start(f32[2,275]{1,0:T(2,128)} %param.23) | copy-start | bytes 6604
  78.8 204.4 %copy-start = (bf16[2,384,128]{2,1,0:T(8,128)(2,1)S(1)}, bf16[2,384,128]{2,1,0:T(8,128)(2,1)}, u32[]{:S(2)}) copy-start(bf16[2,384,128]{2,1,0:T(8,128)(2,1)} %pad.23.embed) | copy-start | bytes 589828
  283.9 214.9 %copy-start.1 = (bf16[2,384,128]{2,1,0:T(8,128)(2,1)}, bf16[2,384,128]{2,1,0:T(8,128)(2,1)S(1)}, u32[]{:S(2)}) copy-start(bf16[2,384,128]{2,1,0:T(8,128)(2,1)S(1)} %scatter.4.embed) | copy-start | bytes 589828
  498.8 169.5 %copy-start.4 = (f32[2,256,256]{2,1,0:T(8,128)S(1)}, f32[2,256,256]{2,1,0:T(8,128)}, u32[]{:S(2)}) copy-start(f32[2,256,256]{2,1,0:T(8,128)} %get-tuple-element.113) | copy-start | bytes 1572868
  498.8 170.3 %copy-start.3 = (f32[2,256,256]{2,1,0:T(8,128)S(1)}, f32[2,256,256]{2,1,0:T(8,128)}, u32[]{:S(2)}) copy-start(f32[2,256,256]{2,1,0:T(8,128)} %get-tuple-element.114) | copy-start | bytes 1572868
  658.9 15.8 %copy-start.6 = (f32[2,64,384]{2,1,0:T(8,128)S(1)}, f32[2,64,384]{2,1,0:T(8,128)}, u32[]{:S(2)}) copy-start(f32[2,64,384]{2,1,0:T(8,128)} %get-tuple-element.55) | copy-start | bytes 589828
Sparse Core Ops, SparseCore 0:
  9.9 40.4 all-gather.2

commit v4 on v3

--- a/solution.py
+++ b/solution.py
@@ -7,7 +7,7 @@
 from jax.experimental.pallas import tpu as pltpu
 from jax.sharding import PartitionSpec as P
 
-VMEM_LIMIT = 56 * 2**20
+VMEM_LIMIT = 58 * 2**20
 
 
 def column_order(own_units):
@@ -144,7 +144,7 @@
 MESH = pl.DeviceIdType.MESH
 LANES = 128
 VOCAB_PAD = 384
-CHUNK = 256
+SPLIT = 1
 NT = (((1,), (1,)), ((), ()))
 TN = (((0,), (0,)), ((), ()))
 
@@ -167,12 +167,14 @@
     return me, sibling, (across, side, up)
 
 
-def greet(peers):
-    seq = lax.axis_index("seq")
+def greet(peers, seqs=0):
+    seq, me = lax.axis_index("seq"), lax.axis_index("mp")
     barrier = pltpu.get_barrier_semaphore()
     for peer in peers:
         pl.semaphore_signal(barrier, inc=1, device_id=(seq, peer), device_id_type=MESH)
-    pl.semaphore_wait(barrier, len(peers))
+    for n in range(1, seqs):
+        pl.semaphore_signal(barrier, inc=1, device_id=((seq + n) % seqs, me), device_id_type=MESH)
+    pl.semaphore_wait(barrier, len(peers) + max(seqs - 1, 0))
 
 
 def remote(src, dst, send, recv, peer):
@@ -199,197 +201,284 @@
     return step if direction == 0 else length - 1 - step
 
 
+def stream_order():
+    return [d * SPLIT + r for r in range(SPLIT) for d in range(2)]
+
+
 def forward_kernel(
-    length, letters, info, inverse, h_in, c_in, embed, w_in, bias, b_dec, wd_hbm, w_hbm,
-    wholes, acts, grads, loss, logit_sq, hidden_sq, dec_bias, dec_grad,
-    w, wd, buf, cell, acc, logit, stage, grad, load_sem, send_sem, recv_sem, save_sem, act_sem, grad_sem,
+    length, letters, ids_in, lens, order_row, order_column, inverse, h_in, c_in, embed, w_in_raw, bias, b_dec,
+    w_dec, matrix, w_hbm,
+    wholes, acts, grads, w_out, loss, logit_sq, hidden_sq, dec_bias, dec_grad, info, ids, w_in,
+    w, wd, buf, cell, acc, logit, stage, grad, all_ids, table, load_sem, ids_send, ids_recv, wd_send, wd_recv,
+    send_sem, recv_sem, save_sem, act_sem, grad_sem,
 ):
     me, sibling, peers = neighbours()
+    seq, seqs, times = lax.axis_index("seq"), all_ids.shape[0], ids_in.shape[0]
     blocks, rows, units = buf.shape[2:]
-    groups = units // LANES
+    groups, span = units // LANES, matrix.shape[0]
+    columns = w.shape[-1]
     load_w = pltpu.make_async_copy(w_hbm, w, load_sem.at[0])
-    load_wd = pltpu.make_async_copy(wd_hbm, wd, load_sem.at[1])
+    store_w = pltpu.make_async_copy(w, w_out, load_sem.at[1])
     load_w.start()
-    load_wd.start()
-    greet((sibling,) + peers)
+    all_ids[seq, :times] = ids_in[...].astype(jnp.float32)
+    wd[me] = w_dec[...]
+    for s in range(2 * SPLIT):
+        buf[s, 0, me] = h_in[s]
+    greet((sibling,) + peers, seqs)
+
+    def ids_copy(n):
+        to = (seq + n) % seqs
+        block = all_ids.at[seq]
+        return pltpu.make_async_remote_copy(
+            src_ref=block, dst_ref=block, send_sem=ids_send.at[n - 1], recv_sem=ids_recv.at[seq],
+            device_id=(to, me), device_id_type=MESH,
+        )
+
+    def ids_arrival(n):
+        source = (seq + n) % seqs
+        block = all_ids.at[source]
+        return pltpu.make_async_remote_copy(
+            src_ref=block, dst_ref=block, send_sem=ids_send.at[n - 1], recv_sem=ids_recv.at[source],
+            device_id=(source, me), device_id_type=MESH,
+        )
+
+    def direct(s, step):
+        slot, par = step % 3, step % 2
+        block = buf.at[s, slot, me]
+        return [
+            remote(block, block, send_sem.at[s, par, n], recv_sem.at[s, slot, me], peer)
+            for n, peer in enumerate(peers + (sibling,))
+        ]
+
+    def relay(s, step, n):
+        slot, par = step % 3, step % 2
+        block = buf.at[s, slot, peers[n]]
+        return remote(block, block, send_sem.at[s, par, 4 + n], recv_sem.at[s, slot, peers[n]], sibling)
+
+    def arrival(s, step, source):
+        slot = step % 3
+        block = buf.at[s, slot, source]
+        return remote(block, block, send_sem.at[s, step % 2, 0], recv_sem.at[s, slot, source], sibling)
+
+    def wd_copy(n):
+        peer = (peers + (sibling,))[n]
+        return remote(wd.at[me], wd.at[me], wd_send.at[n], wd_recv.at[me], peer)
+
+    def wd_relay(n):
+        block = wd.at[peers[n]]
+        return remote(block, block, wd_send.at[4 + n], wd_recv.at[peers[n]], sibling)
+
+    def wd_arrival(source):
+        return remote(wd.at[source], wd.at[source], wd_send.at[0], wd_recv.at[source], sibling)
+
+    def save(s, step):
+        return pltpu.make_async_copy(buf.at[s, step % 3], wholes.at[step, s], save_sem.at[s, step % 2])
+
+    def save_acts(s, step):
+        return pltpu.make_async_copy(stage.at[s], acts.at[step, s], act_sem.at[s])
+
+    def save_grad(s, step):
+        return pltpu.make_async_copy(grad.at[s], grads.at[step, s], grad_sem.at[s])
+
+    def finish_sends(s, step):
+        for copy in direct(s, step):
+            copy.wait_send()
+        for n in range(3):
+            relay(s, step, n).wait_send()
+
+    for n in range(1, seqs):
+        ids_copy(n).start()
+    for s in stream_order():
+        for copy in direct(s, 0):
+            copy.start()
+    for n in range(4):
+        wd_copy(n).start()
     for ref in (loss, logit_sq, hidden_sq, dec_bias, dec_grad):
         ref[...] = jnp.zeros(ref.shape, ref.dtype)
     cell[...] = c_in[...]
-
-    def direct(d, step):
-        slot, par = step % 3, step % 2
-        block = buf.at[d, slot, me]
-        return [
-            remote(block, block, send_sem.at[d, par, n], recv_sem.at[d, slot, me], peer)
-            for n, peer in enumerate(peers + (sibling,))
-        ]
-
-    def relay(d, step, n):
-        slot, par = step % 3, step % 2
-        block = buf.at[d, slot, peers[n]]
-        return remote(block, block, send_sem.at[d, par, 4 + n], recv_sem.at[d, slot, peers[n]], sibling)
-
-    def arrival(d, step, source):
+    for d in range(2):
+        for g in range(columns // span):
+            part = slice(g * span, (g + 1) * span)
+            w_in[d, :, part] = matmul(w_in_raw[d, :, part], matrix[...]).astype(jnp.bfloat16)
+    load_w.wait()
+
+    def regroup(b, carry):
+        for d in range(2):
+            for g in range(columns // span):
+                part = slice(g * span, (g + 1) * span)
+                w[d, b, :, part] = matmul(w[d, b, :, part], matrix[...]).astype(jnp.bfloat16)
+        return carry
+
+    lax.fori_loop(0, blocks, regroup, 0)
+    store_w.start()
+    for n in range(1, seqs):
+        ids_arrival(n).wait_recv()
+    streams = order_row.shape[1]
+    total_streams = lens.shape[1]
+    pick_column = (
+        lax.broadcasted_iota(jnp.int32, (streams, total_streams), 1) == order_column[...]
+    ).astype(jnp.bfloat16)
+    pick_row = (
+        lax.broadcasted_iota(jnp.int32, (total_streams, streams), 0) == order_row[...]
+    ).astype(jnp.bfloat16)
+    table[...] = jnp.zeros(table.shape, table.dtype)
+    for d in range(2):
+        for t in range(length):
+            row = t if d == 0 else length - 1 - t
+            table[t:t + 1] = all_ids[row // times, row % times:row % times + 1]
+        table[LANES - 1:] = lens[...].astype(jnp.float32)
+        high = jnp.floor(table[...] * (1.0 / 16.0))
+        low = (table[...] - 16.0 * high).astype(jnp.bfloat16)
+        high = high.astype(jnp.bfloat16)
+        values = 16.0 * matmul(pick_column, high, NT) + matmul(pick_column, low, NT)
+        for r in range(SPLIT):
+            info[d * SPLIT + r] = values[r * rows:(r + 1) * rows]
+        values = 16.0 * matmul(high[:length], pick_row) + matmul(low[:length], pick_row)
+        for r in range(SPLIT):
+            ids[d * SPLIT + r] = values[:, r * rows:(r + 1) * rows]
+
+    def gates(s, step):
+        slot, later = step % 3, (step + 1) % 3
+        d = s // SPLIT
+        when = time_of(d, step, length)
+        live = info[s, :, LANES - 1:] > when.astype(jnp.float32)
+        for g in range(groups):
+            lanes = slice(g * LANES, (g + 1) * LANES)
+            pre = [acc[:, (4 * g + k) * LANES:(4 * g + k + 1) * LANES] for k in range(4)]
+            in_gate, forget, out_gate = sigmoid(pre[0]), sigmoid(pre[1]), sigmoid(pre[3])
+            cell_gate = jnp.tanh(pre[2])
+            old = cell[s, :, lanes]
+            new = forget * old + in_gate * cell_gate
+            for k, value in enumerate((in_gate, forget, cell_gate, out_gate, old)):
+                stage[s, k, :, lanes] = value
+            cell[s, :, lanes] = jnp.where(live, new, old)
+            before = buf[s, slot, me, :, lanes].astype(jnp.float32)
+            hidden = jnp.where(live, out_gate * jnp.tanh(new), before).astype(jnp.bfloat16)
+            buf[s, later, me, :, lanes] = hidden
+            wide = hidden.astype(jnp.float32)
+            hidden_sq[d] += folded(jnp.where(live, wide * wide, 0.0))
+
+    def decode(s, step):
         slot = step % 3
-        block = buf.at[d, slot, source]
-        return remote(block, block, send_sem.at[d, step % 2, 0], recv_sem.at[d, slot, source], sibling)
-
-    def save(d, step):
-        return pltpu.make_async_copy(buf.at[d, step % 3], wholes.at[step, d], save_sem.at[d, step % 2])
-
-    def save_acts(d, step):
-        return pltpu.make_async_copy(stage.at[d], acts.at[step, d], act_sem.at[d])
-
-    def save_grad(d, step):
-        return pltpu.make_async_copy(grad.at[d], grads.at[step, d], grad_sem.at[d])
-
-    def finish_sends(d, step):
-        for copy in direct(d, step):
-            copy.wait_send()
-        for n in range(3):
-            relay(d, step, n).wait_send()
-
-    def gates(d, step):
-        slot, later = step % 3, (step + 1) % 3
-        when = time_of(d, step, length)
-
-        def chunk(i, carry):
-            at = pl.ds(pl.multiple_of(i * CHUNK, CHUNK), CHUNK)
-            live = info[d, at, LANES - 1:LANES] > when.astype(jnp.float32)
-            for g in range(groups):
-                lanes = slice(g * LANES, (g + 1) * LANES)
-                pre = [acc[at, (4 * g + k) * LANES:(4 * g + k + 1) * LANES] for k in range(4)]
-                in_gate, forget, out_gate = sigmoid(pre[0]), sigmoid(pre[1]), sigmoid(pre[3])
-                cell_gate = jnp.tanh(pre[2])
-                old = cell[d, at, lanes]
-                new = forget * old + in_gate * cell_gate
-                for k, value in enumerate((in_gate, forget, cell_gate, out_gate, old)):
-                    stage[d, k, at, lanes] = value
-                cell[d, at, lanes] = jnp.where(live, new, old)
-                before = buf[d, slot, me, at, lanes].astype(jnp.float32)
-                hidden = jnp.where(live, out_gate * jnp.tanh(new), before).astype(jnp.bfloat16)
-                buf[d, later, me, at, lanes] = hidden
-                wide = hidden.astype(jnp.float32)
-                hidden_sq[d] += folded(jnp.where(live, wide * wide, 0.0))
-            return carry
-
-        lax.fori_loop(0, rows // CHUNK, chunk, 0)
-
-    def decode(d, step):
-        slot = step % 3
+        d = s // SPLIT
         total = jnp.broadcast_to(b_dec[d], logit.shape)
         for b in range(blocks):
-            total += matmul(buf[d, slot, b], wd[d, b])
+            total += matmul(buf[s, slot, b], wd[b, d])
         logit[...] = total
         when = time_of(d, step - 1, length)
         reach = when + 1 if d == 0 else when
-        scale = inverse[0, 0]
-
-        def chunk(i, carry):
-            at = pl.ds(pl.multiple_of(i * CHUNK, CHUNK), CHUNK)
-            table = info[d, at, :]
-            valid = (table[:, LANES - 1:LANES] > reach.astype(jnp.float32)) & (step < length)
-            target = column_of(table, step)
-            value = logit[at, :]
-            lanes = lax.broadcasted_iota(jnp.int32, value.shape, 1)
-            hot = lanes.astype(jnp.float32) == target
-            top = jnp.max(value, axis=1, keepdims=True)
-            power = jnp.exp(value - top)
-            total = jnp.sum(power, axis=1, keepdims=True)
-            picked = jnp.sum(jnp.where(hot, value, 0.0), axis=1, keepdims=True)
-            loss[d] += folded(jnp.broadcast_to(jnp.where(valid, top + jnp.log(total) - picked, 0.0), (CHUNK, LANES)))
-            kept = jnp.where(valid & (lanes < letters), value, 0.0)
-            square = kept * kept
-            logit_sq[d] += folded(sum(square[:, n * LANES:(n + 1) * LANES] for n in range(VOCAB_PAD // LANES)))
-            slope = jnp.where(
-                valid, (power * (1.0 / total) - jnp.where(hot, 1.0, 0.0)) * scale, 0.0
-            ).astype(jnp.bfloat16)
-            grad[d, at, :] = slope
-            wide = slope.astype(jnp.float32)
-            dec_bias[d] += folded(wide)
-            return carry
-
-        lax.fori_loop(0, rows // CHUNK, chunk, 0)
-        dec_grad[d] += matmul(buf[d, slot, me], grad[d], TN)
-
-    def half(step, d):
+        lookup = info[s]
+        valid = (lookup[:, LANES - 1:] > reach.astype(jnp.float32)) & (step < length)
+        target = column_of(lookup, step)
+        value = logit[...]
+        lanes = lax.broadcasted_iota(jnp.int32, value.shape, 1)
+        hot = lanes.astype(jnp.float32) == target
+        top = jnp.max(value, axis=1, keepdims=True)
+        power = jnp.exp(value - top)
+        total = jnp.sum(power, axis=1, keepdims=True)
+        picked = jnp.sum(jnp.where(hot, value, 0.0), axis=1, keepdims=True)
+        loss[d] += folded(jnp.broadcast_to(jnp.where(valid, top + jnp.log(total) - picked, 0.0), (rows, LANES)))
+        kept = jnp.where(valid & (lanes < letters), value, 0.0)
+        square = kept * kept
+        logit_sq[d] += folded(sum(square[:, n * LANES:(n + 1) * LANES] for n in range(VOCAB_PAD // LANES)))
+        slope = jnp.where(
+            valid, (power * (1.0 / total) - jnp.where(hot, 1.0, 0.0)) * inverse[0, 0], 0.0
+        ).astype(jnp.bfloat16)
+        grad[s] = slope
+        dec_bias[d] += folded(slope.astype(jnp.float32))
+        dec_grad[d] += matmul(buf[s, slot, me], grad[s], TN)
+
+    others = tuple(other_core(peer) for peer in peers)
+
+    def half(step, s):
+        d = s // SPLIT
+
         @pl.when(step < length)
         def _():
-            ids = column_of(info[d], step)
-            hot = (lax.broadcasted_iota(jnp.int32, (rows, VOCAB_PAD), 1).astype(jnp.float32) == ids)
+            now = column_of(info[s], step)
+            hot = (lax.broadcasted_iota(jnp.int32, (rows, VOCAB_PAD), 1).astype(jnp.float32) == now)
             row = matmul(hot.astype(jnp.bfloat16), embed[d]).astype(jnp.bfloat16)
             acc[...] = matmul(row, w_in[d]).astype(jnp.bfloat16).astype(jnp.float32) + bias[d]
 
         for n, peer in enumerate(peers):
-            arrival(d, step, peer).wait_recv()
-            relay(d, step, n).start()
-
-        if d == 0:
-            @pl.when(step == 0)
+            arrival(s, step, peer).wait_recv()
+            relay(s, step, n).start()
+
+        if s == 0:
+            @pl.when(step == 1)
             def _():
-                load_w.wait()
-                load_wd.wait()
+                for n, peer in enumerate(peers):
+                    wd_arrival(peer).wait_recv()
+                    wd_relay(n).start()
 
         slot = step % 3
 
         def advance(block):
-            acc[...] += matmul(buf[d, slot, block], w[d, block])
+            acc[...] += matmul(buf[s, slot, block], w[d, block])
 
         @pl.when(step < length)
         def _():
             for block in (me,) + peers:
                 advance(block)
 
-        for block in (sibling,) + tuple(other_core(peer) for peer in peers):
-            arrival(d, step, block).wait_recv()
+        for block in (sibling,) + others:
+            arrival(s, step, block).wait_recv()
 
         @pl.when(step < length)
         def _():
-            save(d, step).start()
-            for block in (sibling,) + tuple(other_core(peer) for peer in peers):
+            save(s, step).start()
+            for block in (sibling,) + others:
                 advance(block)
 
             @pl.when(step > 0)
             def _():
-                save_acts(d, step - 1).wait()
-
-            gates(d, step)
-            save_acts(d, step).start()
+                save_acts(s, step - 1).wait()
+
+            gates(s, step)
+            save_acts(s, step).start()
 
             @pl.when(step > 0)
             def _():
-                save(d, step - 1).wait()
-                finish_sends(d, step - 1)
-
-            for copy in direct(d, step + 1):
+                save(s, step - 1).wait()
+                finish_sends(s, step - 1)
+
+            for copy in direct(s, step + 1):
                 copy.start()
+
+        if s == 0:
+            @pl.when(step == 1)
+            def _():
+                for block in (sibling,) + others:
+                    wd_arrival(block).wait_recv()
 
         @pl.when(step > 0)
         def _():
             @pl.when(step > 1)
             def _():
-                save_grad(d, step - 2).wait()
-
-            decode(d, step)
-            save_grad(d, step - 1).start()
-
-    for d in range(2):
-        buf[d, 0, me] = h_in[d]
-        for copy in direct(d, 0):
-            copy.start()
-
-    def both(step, carry):
-        for d in range(2):
-            half(step, d)
+                save_grad(s, step - 2).wait()
+
+            decode(s, step)
+            save_grad(s, step - 1).start()
+
+    def every(step, carry):
+        for s in stream_order():
+            half(step, s)
         return carry
 
-    lax.fori_loop(0, length + 1, both, 0)
-    for d in range(2):
-        save(d, length - 1).wait()
-        save_acts(d, length - 1).wait()
-        save_grad(d, length - 1).wait()
-        finish_sends(d, length - 1)
-        finish_sends(d, length)
+    lax.fori_loop(0, length + 1, every, 0)
+    store_w.wait()
+    for n in range(1, seqs):
+        ids_copy(n).wait_send()
+    for n in range(4):
+        wd_copy(n).wait_send()
+    for n in range(3):
+        wd_relay(n).wait_send()
+    for s in stream_order():
+        save(s, length - 1).wait()
+        save_acts(s, length - 1).wait()
+        save_grad(s, length - 1).wait()
+        finish_sends(s, length - 1)
+        finish_sends(s, length)
 
 
 def backward_kernel(
@@ -404,19 +493,19 @@
     load_w = pltpu.make_async_copy(w_hbm, w, load_sem)
     load_w.start()
 
-    def load_acts(d, step):
-        return pltpu.make_async_copy(acts.at[step, d], stage.at[d], act_sem.at[d])
-
-    def load_grad(d, step):
-        return pltpu.make_async_copy(grads.at[step, d], grad.at[d], grad_sem.at[d])
-
-    def load_whole(d, step):
-        return pltpu.make_async_copy(wholes.at[step, d], whole.at[d], whole_sem.at[d])
-
-    for d in range(2):
-        load_acts(d, length - 1).start()
-        load_grad(d, length - 1).start()
-        load_whole(d, length - 1).start()
+    def load_acts(s, step):
+        return pltpu.make_async_copy(acts.at[step, s], stage.at[s], act_sem.at[s])
+
+    def load_grad(s, step):
+        return pltpu.make_async_copy(grads.at[step, s], grad.at[s], grad_sem.at[s])
+
+    def load_whole(s, step):
+        return pltpu.make_async_copy(wholes.at[step, s], whole.at[s], whole_sem.at[s])
+
+    for s in stream_order():
+        load_acts(s, length - 1).start()
+        load_grad(s, length - 1).start()
+        load_whole(s, length - 1).start()
     greet((sibling,) + peers)
     held[...] = jnp.zeros(held.shape, held.dtype)
     own[...] = jnp.zeros(own.shape, own.dtype)
@@ -429,116 +518,115 @@
         return carry
 
     lax.fori_loop(0, w.shape[1], clear, 0)
-
-    def to_core(d, turn, n):
+    load_w.wait()
+
+    def to_core(s, turn, n):
         return remote(
-            sent.at[d, n], got.at[d, turn % 2, n], core_send.at[d, n], core_recv.at[d, turn % 2, n], sibling
+            sent.at[s, n], got.at[s, turn % 2, n], core_send.at[s, n], core_recv.at[s, turn % 2, n], sibling
         )
 
-    def to_chip(d, turn, n):
+    def to_chip(s, turn, n):
         return remote(
-            passed.at[d, n], taken.at[d, turn % 2, n], chip_send.at[d, n], chip_recv.at[d, turn % 2, n], peers[n]
+            passed.at[s, n], taken.at[s, turn % 2, n], chip_send.at[s, n], chip_recv.at[s, turn % 2, n], peers[n]
         )
 
-    def half(turn, d):
+    def half(turn, s):
         step = length - 1 - turn
+        d = s // SPLIT
         when = time_of(d, step, length)
-        load_acts(d, step).wait()
-        load_grad(d, step).wait()
-        held[d] += matmul(grad[d], w_dec[d], NT)
+        load_acts(s, step).wait()
+        load_grad(s, step).wait()
+        held[s] += matmul(grad[s], w_dec[d], NT)
 
         @pl.when(turn > 0)
         def _():
             for n in range(3):
-                to_chip(d, turn - 1, n).wait_recv()
-
-        def chunk(i, carry):
-            at = pl.ds(pl.multiple_of(i * CHUNK, CHUNK), CHUNK)
-            live = info[d, at, LANES - 1:LANES] > when.astype(jnp.float32)
-            for g in range(groups):
-                lanes = slice(g * LANES, (g + 1) * LANES)
-                through = own[d, at, lanes]
-                for n in range(3):
-                    through += jnp.where(turn > 0, taken[d, (turn + 1) % 2, n, at, lanes].astype(jnp.float32), 0.0)
-                total = held[d, at, lanes] + through
-                in_gate, forget, cell_gate, out_gate, old = (stage[d, k, at, lanes] for k in range(5))
-                squash = jnp.tanh(forget * old + in_gate * cell_gate)
-                later = cell_grad[d, at, lanes]
-                new = jnp.where(live, later + total * out_gate * (1.0 - squash * squash), 0.0)
-                out = jnp.where(live, total * squash, 0.0)
-                values = (
-                    new * cell_gate * in_gate * (1.0 - in_gate),
-                    new * old * forget * (1.0 - forget),
-                    new * in_gate * (1.0 - cell_gate * cell_gate),
-                    out * out_gate * (1.0 - out_gate),
-                )
-                for k, value in enumerate(values):
-                    pre[d, at, (4 * g + k) * LANES:(4 * g + k + 1) * LANES] = value.astype(jnp.bfloat16)
-                cell_grad[d, at, lanes] = new * forget + jnp.where(live, 0.0, later)
-                held[d, at, lanes] = jnp.where(live, 0.0, total)
-            return carry
-
-        lax.fori_loop(0, rows // CHUNK, chunk, 0)
+                to_chip(s, turn - 1, n).wait_recv()
+
+        live = info[s, :, LANES - 1:] > when.astype(jnp.float32)
+        for g in range(groups):
+            lanes = slice(g * LANES, (g + 1) * LANES)
+            through = own[s, :, lanes]
+            for n in range(3):
+                through += jnp.where(turn > 0, taken[s, (turn + 1) % 2, n, :, lanes].astype(jnp.float32), 0.0)
+            total = held[s, :, lanes] + through
+            in_gate, forget, cell_gate, out_gate, old = (stage[s, k, :, lanes] for k in range(5))
+            squash = jnp.tanh(forget * old + in_gate * cell_gate)
+            later = cell_grad[s, :, lanes]
+            new = jnp.where(live, later + total * out_gate * (1.0 - squash * squash), 0.0)
+            out = jnp.where(live, total * squash, 0.0)
+            values = (
+                new * cell_gate * in_gate * (1.0 - in_gate),
+                new * old * forget * (1.0 - forget),
+                new * in_gate * (1.0 - cell_gate * cell_gate),
+                out * out_gate * (1.0 - out_gate),
+            )
+            for k, value in enumerate(values):
+                pre[s, :, (4 * g + k) * LANES:(4 * g + k + 1) * LANES] = value.astype(jnp.bfloat16)
+            cell_grad[s, :, lanes] = new * forget + jnp.where(live, 0.0, later)
+            held[s, :, lanes] = jnp.where(live, 0.0, total)
 
         @pl.when(turn < length - 1)
         def _():
-            load_acts(d, step - 1).start()
-            load_grad(d, step - 1).start()
+            load_acts(s, step - 1).start()
+            load_grad(s, step - 1).start()
 
         @pl.when(turn > 0)
         def _():
             for n in range(4):
-                to_core(d, turn - 1, n).wait_send()
+                to_core(s, turn - 1, n).wait_send()
             for n in range(3):
-                to_chip(d, turn - 1, n).wait_send()
-
-        if d == 0:
-            @pl.when(turn == 0)
+                to_chip(s, turn - 1, n).wait_send()
+
+        for n, block in enumerate(tuple(other_core(peer) for peer in peers) + (sibling,)):
+            sent[s, n] = matmul(pre[s], w[d, block], NT).astype(jnp.bfloat16)
+            to_core(s, turn, n).start()
+        for n, block in enumerate(peers + (me,)):
+            part = matmul(pre[s], w[d, block], NT)
+            to_core(s, turn, n).wait_recv()
+            part += got[s, turn % 2, n].astype(jnp.float32)
+            if n < 3:
+                passed[s, n] = part.astype(jnp.bfloat16)
+                to_chip(s, turn, n).start()
+            else:
+                own[s] = part
+
+        if s % SPLIT == SPLIT - 1:
+            both = range(s - SPLIT + 1, s + 1)
+            for i in both:
+                load_whole(i, step).wait()
+            for b in range(w.shape[1]):
+                rec[d, b] += sum(matmul(whole[i, b], pre[i], TN) for i in both)
+
+            @pl.when(turn < length - 1)
             def _():
-                load_w.wait()
-
-        for n, block in enumerate(tuple(other_core(peer) for peer in peers) + (sibling,)):
-            sent[d, n] = matmul(pre[d], w[d, block], NT).astype(jnp.bfloat16)
-            to_core(d, turn, n).start()
-        for n, block in enumerate(peers + (me,)):
-            share = matmul(pre[d], w[d, block], NT)
-            to_core(d, turn, n).wait_recv()
-            share += got[d, turn % 2, n].astype(jnp.float32)
-            if n < 3:
-                passed[d, n] = share.astype(jnp.bfloat16)
-                to_chip(d, turn, n).start()
-            else:
-                own[d] = share
-        load_whole(d, step).wait()
-
-        for b in range(w.shape[1]):
-            rec[d, b] += matmul(whole[d, b], pre[d], TN)
-
-        @pl.when(turn < length - 1)
-        def _():
-            load_whole(d, step - 1).start()
-
-        letters = lax.broadcasted_iota(jnp.int32, (VOCAB_PAD, rows), 0).astype(jnp.float32)
-        hot = letters == ids[d, pl.ds(step, 1), :]
-        letter_grad[d] += matmul(hot.astype(jnp.bfloat16), pre[d])
-
-    def both(turn, carry):
-        for d in range(2):
-            half(turn, d)
+                for i in both:
+                    load_whole(i, step - 1).start()
+
+            letters = lax.broadcasted_iota(jnp.int32, (VOCAB_PAD, rows), 0).astype(jnp.float32)
+            terms = []
+            for i in both:
+                hot = letters == ids[i, pl.ds(step, 1), :]
+                terms.append(matmul(hot.astype(jnp.bfloat16), pre[i]))
+            letter_grad[d] += sum(terms)
+
+    def every(turn, carry):
+        for s in stream_order():
+            half(turn, s)
         return carry
 
-    lax.fori_loop(0, length, both, 0)
-    for d in range(2):
+    lax.fori_loop(0, length, every, 0)
+    for s in stream_order():
         for n in range(3):
-            to_chip(d, length - 1, n).wait_recv()
-        total = held[d] + own[d]
+            to_chip(s, length - 1, n).wait_recv()
+        total = held[s] + own[s]
         for n in range(3):
-            total += taken[d, (length - 1) % 2, n].astype(jnp.float32)
-        hidden_grad[d] = total
+            total += taken[s, (length - 1) % 2, n].astype(jnp.float32)
+        hidden_grad[s] = total
         for n in range(4):
-            to_core(d, length - 1, n).wait_send()
+            to_core(s, length - 1, n).wait_send()
         for n in range(3):
-            to_chip(d, length - 1, n).wait_send()
+            to_chip(s, length - 1, n).wait_send()
 
     def narrow(b, carry):
         for d in range(2):
@@ -551,100 +639,114 @@
     store.wait()
 
 
-def kernel_step(step_ids, own_len, h_init, c_init, embed, w_in, w_rec, bias, w_dec, wd_full, b_dec, count, matrix):
-    length, rows = step_ids.shape[1:]
+def kernel_step(ids, lengths, order, count, h_init, c_init, embed, w_in, w_rec, bias, w_dec, b_dec, matrix):
+    seqs = lax.axis_size("seq")
+    local_times, all_streams = ids.shape
+    length = local_times * seqs
+    per_dev, units = h_init.shape[1:]
+    streams, rows = 2 * SPLIT, per_dev // SPLIT
     letters, width = embed.shape[1:]
-    units, columns = h_init.shape[2], w_rec.shape[2]
+    columns = w_rec.shape[2]
     blocks = w_rec.shape[1] // units
     any_space, vmem = pl.BlockSpec(memory_space=pl.ANY), pl.BlockSpec(memory_space=pltpu.VMEM)
-    ids = jnp.swapaxes(step_ids, 1, 2).astype(jnp.float32)
-    reach = jnp.broadcast_to(own_len.astype(jnp.float32)[None, :, None], (2, rows, 1))
-    info = jnp.concatenate([ids, jnp.full((2, rows, LANES - 1 - length), -1.0, jnp.float32), reach], axis=2)
+    own_order = lax.dynamic_slice_in_dim(order, lax.axis_index("seq") * per_dev, per_dev)
     pad_letters = VOCAB_PAD - letters
     embed_pad = jnp.pad(embed, ((0, 0), (0, pad_letters), (0, LANES - width)))
     w_in_pad = jnp.pad(w_in, ((0, 0), (0, LANES - width), (0, 0)))
-    wd_pad = jnp.pad(wd_full, ((0, 0), (0, 0), (0, pad_letters))).reshape(2, blocks, units, VOCAB_PAD)
     w_dec_pad = jnp.pad(w_dec, ((0, 0), (0, 0), (0, pad_letters)))
     b_dec_pad = jnp.pad(b_dec, ((0, 0), (0, pad_letters)), constant_values=-1e30)[:, None]
-    w_blocks = w_rec.reshape(2, blocks, units, columns)
-    inverse = (1.0 / count).reshape(1, 1)
+    bias_grouped = jnp.swapaxes(bias.reshape(2, units // LANES, LANES, 4), -1, -2).reshape(2, 1, columns)
     f32, bf16 = jnp.float32, jnp.bfloat16
     dma = pltpu.SemaphoreType.DMA
     shape = jax.ShapeDtypeStruct
-    wholes, acts, grads, loss, logit_sq, hidden_sq, dec_bias, dec_grad = pl.pallas_call(
+    wholes, acts, grads, w_grouped, loss, logit_sq, hidden_sq, dec_bias, dec_grad, info, slot_ids, w_in_grouped = pl.pallas_call(
         functools.partial(forward_kernel, length, letters),
         out_shape=(
-            shape((length, 2, blocks, rows, units), bf16),
-            shape((length, 2, 5, rows, units), f32),
-            shape((length, 2, rows, VOCAB_PAD), bf16),
+            shape((length, streams, blocks, rows, units), bf16),
+            shape((length, streams, 5, rows, units), f32),
+            shape((length, streams, rows, VOCAB_PAD), bf16),
+            shape((2, blocks, units, columns), bf16),
             shape((2, 8, LANES), f32),
             shape((2, 8, LANES), f32),
             shape((2, 8, LANES), f32),
             shape((2, 8, VOCAB_PAD), f32),
             shape((2, units, VOCAB_PAD), f32),
+            shape((streams, rows, LANES), f32),
+            shape((streams, length, rows), f32),
+            shape((2, LANES, columns), bf16),
         ),
-        in_specs=[vmem, pl.BlockSpec(memory_space=pltpu.SMEM)] + [vmem] * 6 + [any_space] * 2,
-        out_specs=(any_space,) * 3 + (vmem,) * 5,
+        in_specs=[vmem] * 4 + [pl.BlockSpec(memory_space=pltpu.SMEM)] + [vmem] * 8 + [any_space],
+        out_specs=(any_space,) * 4 + (vmem,) * 8,
         scratch_shapes=[
             pltpu.VMEM((2, blocks, units, columns), bf16),
-            pltpu.VMEM((2, blocks, units, VOCAB_PAD), bf16),
-            pltpu.VMEM((2, 3, blocks, rows, units), bf16),
-            pltpu.VMEM((2, rows, units), f32),
+            pltpu.VMEM((blocks, 2, units, VOCAB_PAD), bf16),
+            pltpu.VMEM((streams, 3, blocks, rows, units), bf16),
+            pltpu.VMEM((streams, rows, units), f32),
             pltpu.VMEM((rows, columns), f32),
             pltpu.VMEM((rows, VOCAB_PAD), f32),
-            pltpu.VMEM((2, 5, rows, units), f32),
-            pltpu.VMEM((2, rows, VOCAB_PAD), bf16),
+            pltpu.VMEM((streams, 5, rows, units), f32),
+            pltpu.VMEM((streams, rows, VOCAB_PAD), bf16),
+            pltpu.VMEM((seqs, 8, all_streams), f32),
+            pltpu.VMEM((LANES, all_streams), f32),
             dma((2,)),
-            dma((2, 2, 7)),
-            dma((2, 3, blocks)),
-            dma((2, 2)),
-            dma((2,)),
-            dma((2,)),
+            dma((seqs - 1,)),
+            dma((seqs,)),
+            dma((7,)),
+            dma((blocks,)),
+            dma((streams, 2, 7)),
+            dma((streams, 3, blocks)),
+            dma((streams, 2)),
+            dma((streams,)),
+            dma((streams,)),
         ],
         compiler_params=pltpu.CompilerParams(
             collective_id=0, has_side_effects=True, vmem_limit_bytes=VMEM_LIMIT
         ),
         name="forward_visits",
-    )(info, inverse, h_init, c_init, embed_pad, w_in_pad, bias[:, None], b_dec_pad, wd_pad, w_blocks)
+    )(
+        ids, lengths[None], own_order[None], own_order[:, None], (1.0 / count).reshape(1, 1),
+        h_init.reshape(streams, rows, units), c_init.reshape(streams, rows, units), embed_pad, w_in_pad,
+        bias_grouped, b_dec_pad, w_dec_pad, matrix, w_rec.reshape(2, blocks, units, columns),
+    )
     rec_grad, letter_grad, hidden_grad, cell_grad = pl.pallas_call(
         functools.partial(backward_kernel, length),
         out_shape=(
             shape((2, blocks, units, columns), bf16),
             shape((2, VOCAB_PAD, columns), f32),
-            shape((2, rows, units), f32),
-            shape((2, rows, units), f32),
+            shape((streams, rows, units), f32),
+            shape((streams, rows, units), f32),
         ),
         in_specs=[vmem] * 3 + [any_space] * 4,
         out_specs=(any_space, vmem, vmem, vmem),
         scratch_shapes=[
             pltpu.VMEM((2, blocks, units, columns), bf16),
             pltpu.VMEM((2, blocks, units, columns), f32),
-            pltpu.VMEM((2, 5, rows, units), f32),
-            pltpu.VMEM((2, rows, VOCAB_PAD), bf16),
-            pltpu.VMEM((2, blocks, rows, units), bf16),
-            pltpu.VMEM((2, rows, columns), bf16),
-            pltpu.VMEM((2, rows, units), f32),
-            pltpu.VMEM((2, rows, units), f32),
-            pltpu.VMEM((2, 4, rows, units), bf16),
-            pltpu.VMEM((2, 2, 4, rows, units), bf16),
-            pltpu.VMEM((2, 3, rows, units), bf16),
-            pltpu.VMEM((2, 2, 3, rows, units), bf16),
+            pltpu.VMEM((streams, 5, rows, units), f32),
+            pltpu.VMEM((streams, rows, VOCAB_PAD), bf16),
+            pltpu.VMEM((streams, blocks, rows, units), bf16),
+            pltpu.VMEM((streams, rows, columns), bf16),
+            pltpu.VMEM((streams, rows, units), f32),
+            pltpu.VMEM((streams, rows, units), f32),
+            pltpu.VMEM((streams, 4, rows, units), bf16),
+            pltpu.VMEM((streams, 2, 4, rows, units), bf16),
+            pltpu.VMEM((streams, 3, rows, units), bf16),
+            pltpu.VMEM((streams, 2, 3, rows, units), bf16),
             dma,
-            dma((2,)),
-            dma((2,)),
-            dma((2,)),
-            dma((2, 4)),
-            dma((2, 2, 4)),
-            dma((2, 3)),
-            dma((2, 2, 3)),
+            dma((streams,)),
+            dma((streams,)),
+            dma((streams,)),
+            dma((streams, 4)),
+            dma((streams, 2, 4)),
+            dma((streams, 3)),
+            dma((streams, 2, 3)),
         ],
         compiler_params=pltpu.CompilerParams(
             collective_id=1, has_side_effects=True, vmem_limit_bytes=VMEM_LIMIT
         ),
         name="backward_visits",
-    )(info, step_ids.astype(f32), w_dec_pad, acts, grads, wholes, w_blocks)
+    )(info, slot_ids, w_dec_pad, acts, grads, wholes, w_grouped)
     rec_part, edge_part, dec_part, small = kernel_sums(
-        rec_grad, letter_grad, embed_pad, w_in_pad, matrix, width, letters, dec_grad,
+        rec_grad, letter_grad, embed_pad, w_in_grouped, matrix, width, letters, dec_grad,
         (loss, logit_sq, hidden_sq, dec_bias),
     )
     at = 2 * TABLE
@@ -654,8 +756,8 @@
         jnp.sum(small[at + 1:at + 3], axis=1),
         small[at + 5:at + 5 + 2 * (VOCAB_PAD // LANES)].reshape(2, VOCAB_PAD)[:, :letters],
         dec_part[:, :, :letters],
-        hidden_grad,
-        cell_grad,
+        hidden_grad.reshape(h_init.shape),
+        cell_grad.reshape(h_init.shape),
         rec_part.reshape(2, -1, columns),
         edge_part[:, :width],
         edge_part[:, width],
@@ -969,20 +1071,30 @@
     )
 
 
-def plain_step(
-    step_ids, own_len, h_init, c_init, embed, w_in, w_rec, bias, w_dec, wd_full, b_dec, count, matrix
-):
+def plain_step(ids, lengths, order, count, h_init, c_init, embed, w_in, w_rec, bias, w_dec, b_dec, matrix):
+    first_mp = (lax.axis_index("mp") == 0).astype(jnp.float32)
+    per_dev, own_units = h_init.shape[1:]
     lanes = matrix.shape[0] // 4
-    first_mp = (lax.axis_index("mp") == 0).astype(jnp.float32)
+    wd_full = lax.all_gather(w_dec, "mp", axis=1, tiled=True)
+    whole_ids = lax.all_gather(ids, "seq", axis=0, tiled=True)
+    own_order = lax.dynamic_slice_in_dim(order, lax.axis_index("seq") * per_dev, per_dev)
+    slot_ids = jnp.take(whole_ids, own_order, axis=1)
+    own_len = jnp.take(lengths, own_order)
+    step_ids = jnp.stack([slot_ids, jnp.flip(slot_ids, 0)])
+    w_rec_grouped = grouped(w_rec, matrix)
+    w_in_grouped = grouped(w_in, matrix)
+    bias_grouped = jnp.swapaxes(
+        bias.reshape(2, own_units // lanes, lanes, 4), -1, -2
+    ).reshape(bias.shape)
     loss, hidden_sq, logit_sq, dec_bias, dec_grad, hidden_grad, cell_grad, rec_grad, letter_grad = recurrences(
-        step_ids, own_len, h_init, c_init, embed, w_in, w_rec, bias, w_dec, wd_full,
+        step_ids, own_len, h_init, c_init, embed, w_in_grouped, w_rec_grouped, bias_grouped, w_dec, wd_full,
         b_dec, count, lanes,
     )
     embed_wide = embed.astype(jnp.float32)
     in_grad = jnp.einsum("dve,dvc->dec", embed_wide, letter_grad, precision=lax.Precision.HIGHEST)
     bias_grad = jnp.sum(letter_grad, axis=1, keepdims=True)
     embed_part = jnp.einsum(
-        "dvc,dec->dve", letter_grad, w_in.astype(jnp.float32), precision=lax.Precision.HIGHEST
+        "dvc,dec->dve", letter_grad, w_in_grouped.astype(jnp.float32), precision=lax.Precision.HIGHEST
     )
     edge = ungrouped_wide(jnp.concatenate([in_grad, bias_grad], axis=1), lanes)
     rec_part = lax.psum_scatter(rec_grad.astype(jnp.bfloat16), "seq", scatter_dimension=1, tiled=True)
@@ -999,35 +1111,23 @@
 
 
 def per_device(ids, lengths, order, h_init, c_init, embed, w_in, w_rec, bias, w_dec, b_dec):
-    seq_rank = lax.axis_index("seq")
     streams = ids.shape[1]
-    per_dev = h_init.shape[1]
-    own_units, all_units = h_init.shape[2], w_rec.shape[1]
-    letter_count = embed.shape[1]
-    wd_full = lax.all_gather(w_dec, "mp", axis=1, tiled=True)
-    whole_ids = lax.all_gather(ids, "seq", axis=0, tiled=True)
-    own_order = lax.dynamic_slice_in_dim(order, seq_rank * per_dev, per_dev)
-    slot_ids = jnp.take(whole_ids, own_order, axis=1)
-    own_len = jnp.take(lengths, own_order)
+    per_dev, own_units = h_init.shape[1:]
+    all_units, letter_count = w_rec.shape[1], embed.shape[1]
     live_total = jnp.sum(lengths).astype(jnp.float32)
     count = 2.0 * (jnp.sum(lengths) - streams).astype(jnp.float32)
-    step_ids = jnp.stack([slot_ids, jnp.flip(slot_ids, 0)])
-    lanes, matrix = column_order(own_units)
-    w_rec_grouped = grouped(w_rec, matrix)
-    w_in_grouped = grouped(w_in, matrix)
-    bias_grouped = jnp.swapaxes(
-        bias.reshape(2, own_units // lanes, lanes, 4), -1, -2
-    ).reshape(bias.shape)
-    operands = (
-        step_ids, own_len, h_init, c_init, embed, w_in_grouped, w_rec_grouped, bias_grouped, w_dec, wd_full,
-        b_dec, count, matrix,
-    )
-    fits = own_units % LANES == 0 and per_dev == CHUNK and all_units % (lax.axis_size("seq") * PIECE) == 0
+    _, matrix = column_order(own_units)
+    operands = (ids, lengths, order, count, h_init, c_init, embed, w_in, w_rec, bias, w_dec, b_dec, matrix)
+    fits = own_units % LANES == 0 and per_dev % (SPLIT * LANES) == 0 and per_dev <= 256
+    fits = fits and all_units % (lax.axis_size("seq") * PIECE) == 0 and letter_count <= TABLE
     if lax.axis_size("mp") == 8 and lax.axis_size("seq") == 4 and fits:
         results = kernel_step(*operands)
     else:
         results = plain_step(*operands)
-    loss_sum, hidden_all, logit_all, dec_bias_grad, dec_part, hidden_grad, cell_grad, rec_out, in_out, bias_out, embed_grad = results
+    (
+        loss_sum, hidden_all, logit_all, dec_bias_grad, dec_part, hidden_grad, cell_grad, rec_out, in_out, bias_out,
+        embed_grad,
+    ) = results
     embed_wide = embed.astype(jnp.float32)
     rms_embed = jnp.sqrt(jnp.mean(embed_wide * embed_wide, axis=(1, 2)))
     return (

time: 689 us -> 637 us (0.925)
  local copies, waits for them, and re-layouts: 54.4 us -> 26 us
  Pallas kernels: 577 us -> 598 us
  blocking collectives: 15.1 us -> 0 us
  between operations: 17.4 us -> 3.95 us
  matrix products: 10.9 us -> 0 us
    pallas_call x1, Pallas kernels: 202 us -> 223 us  [kernel_step(): pl.pallas_call(functools.partial(forward_kernel, length, letters), out_sh...]
    all_gather x1 -> x0, blocking collectives: 15.1 us -> none  [per_device(): whole_ids = lax.all_gather(ids, 'seq', axis=0, tiled=True)]
    unnamed x31 -> x24, local copies, waits for them, and re-layouts: 27.3 us -> 14.1 us
    another operation x2 -> x1, local copies, waits for them, and re-layouts: 12.4 us -> 0.11 us  [the longest x1 12.3 us: kernel_step(): w_blocks = w_rec.reshape(2, blocks, units, columns)]
    dot_general x2 -> x0, matrix products: 10.9 us -> none  [grouped(): jnp.einsum('...gc,cp->...gp', parts, matrix, preferred_element_type=jnp.f...]
  transfers between devices with their start and end apart: 1 -> 0, of which waited for: 0 -> 0; matrix products, arithmetic and copies ran while one was open for 7% -> 0% of each run, Pallas kernels for 0% -> 0%
where the time goes in v4:
time: 637 us; the launch traced here: 633 us
  Pallas kernels  598 us (94%)
  local copies, waits for them, and re-layouts  26 us (4%)
    pallas_call x1, Pallas kernels, kernel_step(): pl.pallas_call(functools.partial(forward_kernel, length, letters), out_sh...  223 us
    pallas_call x1, Pallas kernels, kernel_step(): pl.pallas_call(functools.partial(backward_kernel, length), out_shape=(sha...  215 us
    pallas_call x1, Pallas kernels, kernel_sums(): pl.pallas_call(functools.partial(reduce_kernel, width), out_shape=(shape(...  160 us
    unnamed x24, local copies, waits for them, and re-layouts  14.1 us

profile of v4, /device:TPU:0, one launch (start us, length us, event | category | flops | bytes accessed | tf_op | source)
XLA Modules:
  0.0 633.0 jit_solution(8456532959989163065)
XLA Ops:
  0.6 0.8 dynamic_slice.3
  1.4 0.8 copy.33.order_column
  2.2 1.3 reduce_sum.40
  4.2 1.2 copy.32
  5.5 0.8 pad.21.w_dec
  6.3 0.9 fusion.matrix
  7.2 0.9 copy.29
  8.1 0.7 pad.18.embed
  8.8 1.1 copy.30
  9.9 0.9 pad.19.w_in_raw
  10.8 1.0 reshape.103
  11.8 0.7 copy.31
  12.5 0.7 pad.20
  13.2 0.6 broadcast_in_dim.21.b_dec
  13.7 223.2 %forward_visits.1 = (bf16[16,2,8,256,256]{4,3,2,1,0:T(8,128)(2,1)}, f32[16,2,5,256,256]{4,3,2,1,0:T(8,128)}, bf16[16,2,256,384]{3,2,1,0:T(8,128)(2,1)}, bf16[2,8...) custom-call(s32[4,1024]{1,0:T(4,128)} %ids_in.1, ...), custom_call_target="tpu_custom_call" | custom-call | tf_op jit(solution)/shard_map/forward_visits/pallas_call | solution.py:662
  236.9 215.2 %backward_visits.1 = (bf16[2,8,256,1024]{3,2,1,0:T(8,128)(2,1)}, f32[2,384,1024]{2,1,0:T(8,128)}, f32[2,256,256]{2,1,0:T(8,128)}, f32[2,256,256]{2,1,0:T(8,128)}) custom-call(f32[2,256,128]{2,1,0:T(8,128)} %get-tuple-element.44.info, f32[2,16,256]{2,1,0:T(8,128)} %get-tuple-element.45.ids, bf16[2,256,384]{2,1,0:T(8,128)(2,1)} %pad.21.w_dec, ...), custom_call_target="tpu_custom_call" | custom-call | tf_op jit(solution)/shard_map/backward_visits/pallas_call | solution.py:711
  452.3 0.8 scatter.4.embed
  453.1 0.7 copy-done.1
  453.8 160.0 %gradient_sums.1 = (f32[2,4,128,1024]{3,2,1,0:T(8,128)}, f32[2,104,256]{2,1,0:T(8,128)}, f32[2,64,384]{2,1,0:T(8,128)}, f32[576,128]{1,0:T(8,128)}) custom-call(bf16[2,4,4,128,1024]{4,3,2,1,0:T(8,128)(2,1)} %bitcast.19, f32[2,384,1024]{2,1,0:T(8,128)} %get-tuple-element.51.letter_grad, bf16[2,384,128]{2,1,0:T(8,128)(2,1)} %copy-done.1, ...), custom_call_target="tpu_custom_call" | custom-call | tf_op jit(solution)/shard_map/gradient_sums/pallas_call | solution.py:1025
  613.8 0.9 slice_reduce_fusion
  615.9 1.0 slice.51
  616.8 0.9 copy.37
  617.7 1.7 copy.35
  619.4 0.7 slice.56
  620.1 0.6 reshape.109
  620.7 0.7 slice.54
  621.4 0.6 copy.39
  622.0 1.2 slice.50
  624.8 0.8 copy.45
  625.6 0.8 copy.46
  626.4 4.8 copy.47
  631.2 0.7 copy.48
  (19 shorter events, 1.6 us)
Async XLA Ops:
  1.4 12.3 %copy-start.6 = (s32[256]{0:T(256)}, s32[256]{0:T(256)S(1)}, u32[]{:S(2)}) copy-start(s32[256]{0:T(256)S(1)} %dynamic_slice.3) | copy-start | bytes 3076
  236.9 215.4 %copy-start = (bf16[2,384,128]{2,1,0:T(8,128)(2,1)S(1)}, bf16[2,384,128]{2,1,0:T(8,128)(2,1)}, u32[]{:S(2)}) copy-start(bf16[2,384,128]{2,1,0:T(8,128)(2,1)} %pad.18.embed) | copy-start | bytes 589828
  452.1 171.7 %copy-start.2 = (bf16[2,275,100]{2,0,1:T(2,128)(2,1)S(1)}, bf16[2,275,100]{2,0,1:T(2,128)(2,1)}, u32[]{:S(2)}) copy-start(bf16[2,275,100]{2,0,1:T(2,128)(2,1)} %param.18) | copy-start | bytes 330004
  452.2 172.6 %copy-start.4 = (f32[2,256,256]{2,1,0:T(8,128)S(1)}, f32[2,256,256]{2,1,0:T(8,128)}, u32[]{:S(2)}) copy-start(f32[2,256,256]{2,1,0:T(8,128)} %get-tuple-element.105) | copy-start | bytes 1572868
  452.3 173.3 %copy-start.3 = (f32[2,256,256]{2,1,0:T(8,128)S(1)}, f32[2,256,256]{2,1,0:T(8,128)}, u32[]{:S(2)}) copy-start(f32[2,256,256]{2,1,0:T(8,128)} %get-tuple-element.106) | copy-start | bytes 1572868
  453.1 0.7 copy-start.1
  613.8 17.4 %copy-start.5 = (f32[2,64,384]{2,1,0:T(8,128)S(1)}, f32[2,64,384]{2,1,0:T(8,128)}, u32[]{:S(2)}) copy-start(f32[2,64,384]{2,1,0:T(8,128)} %get-tuple-element.63) | copy-start | bytes 589828

commit v5 on v4

--- a/solution.py
+++ b/solution.py
@@ -144,7 +144,6 @@
 MESH = pl.DeviceIdType.MESH
 LANES = 128
 VOCAB_PAD = 384
-SPLIT = 1
 NT = (((1,), (1,)), ((), ()))
 TN = (((0,), (0,)), ((), ()))
 
@@ -192,6 +191,18 @@
     return jnp.sum(x.reshape(x.shape[0] // 8, 8, x.shape[1]), axis=0)
 
 
+def regroup_matrix(span):
+    source = lax.broadcasted_iota(jnp.int32, (span, span), 0)
+    place = (source & 3) * (span // 4) + (source >> 2)
+    return (place == lax.broadcasted_iota(jnp.int32, (span, span), 1)).astype(jnp.bfloat16)
+
+
+def padded(ref, value):
+    ref[...] = jnp.zeros(ref.shape, ref.dtype)
+    for d in range(2):
+        ref[d, :value.shape[1], :value.shape[2]] = value[d]
+
+
 def column_of(table, lane):
     lanes = lax.broadcasted_iota(jnp.int32, table.shape, 1)
     return jnp.sum(jnp.where(lanes == lane, table, 0.0), axis=1, keepdims=True)
@@ -201,15 +212,10 @@
     return step if direction == 0 else length - 1 - step
 
 
-def stream_order():
-    return [d * SPLIT + r for r in range(SPLIT) for d in range(2)]
-
-
 def forward_kernel(
-    length, letters, ids_in, lens, order_row, order_column, inverse, h_in, c_in, embed, w_in_raw, bias, b_dec,
-    w_dec, matrix, w_hbm,
+    length, letters, ids_in, lens, order, h_in, c_in, embed_in, w_in_raw, bias, b_dec_in, w_dec_in, w_hbm,
     wholes, acts, grads, w_out, loss, logit_sq, hidden_sq, dec_bias, dec_grad, info, ids, w_in,
-    w, wd, buf, cell, acc, logit, stage, grad, all_ids, table, load_sem, ids_send, ids_recv, wd_send, wd_recv,
+    w, wd, buf, cell, acc, logit, stage, grad, all_ids, table, matrix, embed, b_dec, inverse, load_sem, ids_send, ids_recv, wd_send, wd_recv,
     send_sem, recv_sem, save_sem, act_sem, grad_sem,
 ):
     me, sibling, peers = neighbours()
@@ -221,8 +227,8 @@
     store_w = pltpu.make_async_copy(w, w_out, load_sem.at[1])
     load_w.start()
     all_ids[seq, :times] = ids_in[...].astype(jnp.float32)
-    wd[me] = w_dec[...]
-    for s in range(2 * SPLIT):
+    matrix[...] = regroup_matrix(span)
+    for s in range(2):
         buf[s, 0, me] = h_in[s]
     greet((sibling,) + peers, seqs)
 
@@ -242,23 +248,30 @@
             device_id=(source, me), device_id_type=MESH,
         )
 
+    across, side, up = peers
+    depth = rows // 2
+
+    def transfer(s, step, block, h, index, peer):
+        slot, par = step % 3, step % 2
+        ref = buf.at[s, slot, block, h * depth:(h + 1) * depth]
+        return remote(ref, ref, send_sem.at[s, par, index], recv_sem.at[s, slot, block, h], peer)
+
+    def transfer_whole(s, step, block, index):
+        slot, par = step % 3, step % 2
+        ref = buf.at[s, slot, block]
+        return remote(ref, ref, send_sem.at[s, par, index], recv_sem.at[s, slot, block, 0], sibling)
+
     def direct(s, step):
-        slot, par = step % 3, step % 2
-        block = buf.at[s, slot, me]
-        return [
-            remote(block, block, send_sem.at[s, par, n], recv_sem.at[s, slot, me], peer)
-            for n, peer in enumerate(peers + (sibling,))
-        ]
-
-    def relay(s, step, n):
-        slot, par = step % 3, step % 2
-        block = buf.at[s, slot, peers[n]]
-        return remote(block, block, send_sem.at[s, par, 4 + n], recv_sem.at[s, slot, peers[n]], sibling)
-
-    def arrival(s, step, source):
-        slot = step % 3
-        block = buf.at[s, slot, source]
-        return remote(block, block, send_sem.at[s, step % 2, 0], recv_sem.at[s, slot, source], sibling)
+        plan = ((0, side), (1, up), (1, side), (0, up))
+        return [transfer(s, step, me, h, n, peer) for n, (h, peer) in enumerate(plan)]
+
+    def pass_on(s, step):
+        for n, (block, h, peer) in enumerate(((side, 0, up), (up, 1, side))):
+            transfer(s, step, block, h, 0, sibling).wait_recv()
+            transfer(s, step, block, h, 4 + n, peer).start()
+
+    def core_copies(s, step):
+        return [transfer_whole(s, step, block, 6 + n) for n, block in enumerate((me, side, up, across))]
 
     def wd_copy(n):
         peer = (peers + (sibling,))[n]
@@ -281,25 +294,34 @@
         return pltpu.make_async_copy(grad.at[s], grads.at[step, s], grad_sem.at[s])
 
     def finish_sends(s, step):
-        for copy in direct(s, step):
+        for copy in direct(s, step) + core_copies(s, step):
             copy.wait_send()
-        for n in range(3):
-            relay(s, step, n).wait_send()
+        for n, (block, h, peer) in enumerate(((side, 0, up), (up, 1, side))):
+            transfer(s, step, block, h, 4 + n, peer).wait_send()
 
     for n in range(1, seqs):
         ids_copy(n).start()
-    for s in stream_order():
+    for s in range(2):
         for copy in direct(s, 0):
             copy.start()
+        transfer_whole(s, 0, me, 6).start()
+    padded(wd.at[me], w_dec_in)
     for n in range(4):
         wd_copy(n).start()
+    padded(embed, embed_in)
+    padded(w_in, w_in_raw)
+    b_dec[...] = jnp.full(b_dec.shape, -1e30, jnp.float32)
+    for d in range(2):
+        b_dec[d, :, :letters] = b_dec_in[d:d + 1]
+    lengths = lens[...].astype(jnp.float32)
+    inverse[...] = 0.5 / (jnp.sum(lengths, axis=1, keepdims=True) - lens.shape[1])
     for ref in (loss, logit_sq, hidden_sq, dec_bias, dec_grad):
         ref[...] = jnp.zeros(ref.shape, ref.dtype)
     cell[...] = c_in[...]
     for d in range(2):
         for g in range(columns // span):
             part = slice(g * span, (g + 1) * span)
-            w_in[d, :, part] = matmul(w_in_raw[d, :, part], matrix[...]).astype(jnp.bfloat16)
+            w_in[d, :, part] = matmul(w_in[d, :, part], matrix[...]).astype(jnp.bfloat16)
     load_w.wait()
 
     def regroup(b, carry):
@@ -313,33 +335,37 @@
     store_w.start()
     for n in range(1, seqs):
         ids_arrival(n).wait_recv()
-    streams = order_row.shape[1]
+    streams = rows
+    order_row = order[:, pl.ds(pl.multiple_of(seq * rows, LANES), rows)]
+    square = (rows, rows)
+    diagonal = lax.broadcasted_iota(jnp.int32, square, 0) == lax.broadcasted_iota(jnp.int32, square, 1)
+    order_column = jnp.sum(
+        jnp.where(diagonal, jnp.broadcast_to(order_row.astype(jnp.float32), square), 0.0), axis=1, keepdims=True
+    ).astype(jnp.int32)
     total_streams = lens.shape[1]
     pick_column = (
-        lax.broadcasted_iota(jnp.int32, (streams, total_streams), 1) == order_column[...]
+        lax.broadcasted_iota(jnp.int32, (streams, total_streams), 1) == order_column
     ).astype(jnp.bfloat16)
     pick_row = (
-        lax.broadcasted_iota(jnp.int32, (total_streams, streams), 0) == order_row[...]
+        lax.broadcasted_iota(jnp.int32, (total_streams, streams), 0) == order_row
     ).astype(jnp.bfloat16)
     table[...] = jnp.zeros(table.shape, table.dtype)
     for d in range(2):
         for t in range(length):
             row = t if d == 0 else length - 1 - t
             table[t:t + 1] = all_ids[row // times, row % times:row % times + 1]
-        table[LANES - 1:] = lens[...].astype(jnp.float32)
+        table[LANES - 1:] = lengths
         high = jnp.floor(table[...] * (1.0 / 16.0))
         low = (table[...] - 16.0 * high).astype(jnp.bfloat16)
         high = high.astype(jnp.bfloat16)
         values = 16.0 * matmul(pick_column, high, NT) + matmul(pick_column, low, NT)
-        for r in range(SPLIT):
-            info[d * SPLIT + r] = values[r * rows:(r + 1) * rows]
+        info[d] = values
         values = 16.0 * matmul(high[:length], pick_row) + matmul(low[:length], pick_row)
-        for r in range(SPLIT):
-            ids[d * SPLIT + r] = values[:, r * rows:(r + 1) * rows]
+        ids[d] = values
 
     def gates(s, step):
         slot, later = step % 3, (step + 1) % 3
-        d = s // SPLIT
+        d = s
         when = time_of(d, step, length)
         live = info[s, :, LANES - 1:] > when.astype(jnp.float32)
         for g in range(groups):
@@ -360,7 +386,7 @@
 
     def decode(s, step):
         slot = step % 3
-        d = s // SPLIT
+        d = s
         total = jnp.broadcast_to(b_dec[d], logit.shape)
         for b in range(blocks):
             total += matmul(buf[s, slot, b], wd[b, d])
@@ -382,7 +408,7 @@
         square = kept * kept
         logit_sq[d] += folded(sum(square[:, n * LANES:(n + 1) * LANES] for n in range(VOCAB_PAD // LANES)))
         slope = jnp.where(
-            valid, (power * (1.0 / total) - jnp.where(hot, 1.0, 0.0)) * inverse[0, 0], 0.0
+            valid, (power * (1.0 / total) - jnp.where(hot, 1.0, 0.0)) * inverse[...], 0.0
         ).astype(jnp.bfloat16)
         grad[s] = slope
         dec_bias[d] += folded(slope.astype(jnp.float32))
@@ -391,7 +417,7 @@
     others = tuple(other_core(peer) for peer in peers)
 
     def half(step, s):
-        d = s // SPLIT
+        d = s
 
         @pl.when(step < length)
         def _():
@@ -400,9 +426,10 @@
             row = matmul(hot.astype(jnp.bfloat16), embed[d]).astype(jnp.bfloat16)
             acc[...] = matmul(row, w_in[d]).astype(jnp.bfloat16).astype(jnp.float32) + bias[d]
 
-        for n, peer in enumerate(peers):
-            arrival(s, step, peer).wait_recv()
-            relay(s, step, n).start()
+        for n, (block, halves) in enumerate(((side, (1,)), (up, (0,)), (across, (0, 1)))):
+            for h in halves:
+                transfer(s, step, block, h, 0, sibling).wait_recv()
+            transfer_whole(s, step, block, 7 + n).start()
 
         if s == 0:
             @pl.when(step == 1)
@@ -422,20 +449,28 @@
                 advance(block)
 
         for block in (sibling,) + others:
-            arrival(s, step, block).wait_recv()
+            transfer_whole(s, step, block, 6).wait_recv()
 
         @pl.when(step < length)
         def _():
-            save(s, step).start()
             for block in (sibling,) + others:
                 advance(block)
+
+        if s == 0:
+            pass_on(1, step)
+        else:
+            @pl.when(step < length)
+            def _():
+                pass_on(0, step + 1)
+
+        @pl.when(step < length)
+        def _():
 
             @pl.when(step > 0)
             def _():
                 save_acts(s, step - 1).wait()
 
             gates(s, step)
-            save_acts(s, step).start()
 
             @pl.when(step > 0)
             def _():
@@ -444,6 +479,9 @@
 
             for copy in direct(s, step + 1):
                 copy.start()
+            transfer_whole(s, step + 1, me, 6).start()
+            save_acts(s, step).start()
+            save(s, step).start()
 
         if s == 0:
             @pl.when(step == 1)
@@ -461,10 +499,11 @@
             save_grad(s, step - 1).start()
 
     def every(step, carry):
-        for s in stream_order():
+        for s in range(2):
             half(step, s)
         return carry
 
+    pass_on(0, 0)
     lax.fori_loop(0, length + 1, every, 0)
     store_w.wait()
     for n in range(1, seqs):
@@ -473,7 +512,7 @@
         wd_copy(n).wait_send()
     for n in range(3):
         wd_relay(n).wait_send()
-    for s in stream_order():
+    for s in range(2):
         save(s, length - 1).wait()
         save_acts(s, length - 1).wait()
         save_grad(s, length - 1).wait()
@@ -482,10 +521,10 @@
 
 
 def backward_kernel(
-    length, info, ids, w_dec, acts, grads, wholes, w_hbm,
-    rec_out, letter_grad, hidden_grad, cell_grad,
-    w, rec, stage, grad, whole, pre, held, own, sent, got, passed, taken, load_sem, act_sem, grad_sem, whole_sem,
-    core_send, core_recv, chip_send, chip_recv,
+    length, info, ids, w_dec_in, dec_grad, acts, grads, wholes, w_hbm,
+    rec_out, letter_grad, hidden_grad, cell_grad, dec_out,
+    w, rec, stage, grad, whole, pre, held, own, sent, got, passed, taken, kept, middle, w_dec, dec, dec_in, load_sem, act_sem,
+    grad_sem, whole_sem, core_send, core_recv, chip_send, chip_recv, middle_send, middle_recv, dec_send, dec_recv,
 ):
     me, sibling, peers = neighbours()
     rows, units = held.shape[1:]
@@ -502,11 +541,26 @@
     def load_whole(s, step):
         return pltpu.make_async_copy(wholes.at[step, s], whole.at[s], whole_sem.at[s])
 
-    for s in stream_order():
+    for s in range(2):
         load_acts(s, length - 1).start()
         load_grad(s, length - 1).start()
         load_whole(s, length - 1).start()
-    greet((sibling,) + peers)
+    seq, seqs, tall = lax.axis_index("seq"), dec.shape[0], dec.shape[2]
+    for q in range(seqs):
+        for d in range(2):
+            dec[q, d] = dec_grad[d, q * tall:(q + 1) * tall].astype(jnp.bfloat16)
+    greet((sibling,) + peers, seqs)
+
+    def dec_copy(n):
+        to = (seq + n) % seqs
+        return pltpu.make_async_remote_copy(
+            src_ref=dec.at[to], dst_ref=dec_in.at[n - 1], send_sem=dec_send.at[n - 1], recv_sem=dec_recv.at[n - 1],
+            device_id=(to, me), device_id_type=MESH,
+        )
+
+    for n in range(1, seqs):
+        dec_copy(n).start()
+    padded(w_dec, w_dec_in)
     held[...] = jnp.zeros(held.shape, held.dtype)
     own[...] = jnp.zeros(own.shape, own.dtype)
     cell_grad[...] = jnp.zeros(cell_grad.shape, cell_grad.dtype)
@@ -525,14 +579,35 @@
             sent.at[s, n], got.at[s, turn % 2, n], core_send.at[s, n], core_recv.at[s, turn % 2, n], sibling
         )
 
-    def to_chip(s, turn, n):
+    across, side, up = peers
+    depth = rows // 2
+
+    def to_chip(s, turn, n, h):
+        part = slice(h * depth, (h + 1) * depth)
         return remote(
-            passed.at[s, n], taken.at[s, turn % 2, n], chip_send.at[s, n], chip_recv.at[s, turn % 2, n], peers[n]
+            passed.at[s, n, part], taken.at[s, turn % 2, n - 1, part],
+            chip_send.at[s, n - 1, h], chip_recv.at[s, turn % 2, n - 1, h], peers[n],
         )
+
+    def to_middle(s, turn, h):
+        return remote(
+            passed.at[s, 0, h * depth:(h + 1) * depth], middle.at[s, turn % 2, h],
+            middle_send.at[s, h], middle_recv.at[s, turn % 2, h], peers[1 + h],
+        )
+
+    def chip_copies(s, turn):
+        return [to_chip(s, turn, n, h) for n in (1, 2) for h in range(2)]
+
+    def pass_on(s, turn):
+        for h in range(2):
+            to_middle(s, turn, h).wait_recv()
+            total = kept[s, h] + middle[s, turn % 2, h].astype(jnp.float32)
+            passed[s, 2 - h, h * depth:(h + 1) * depth] = total.astype(jnp.bfloat16)
+            to_chip(s, turn, 2 - h, h).start()
 
     def half(turn, s):
         step = length - 1 - turn
-        d = s // SPLIT
+        d = s
         when = time_of(d, step, length)
         load_acts(s, step).wait()
         load_grad(s, step).wait()
@@ -540,14 +615,14 @@
 
         @pl.when(turn > 0)
         def _():
-            for n in range(3):
-                to_chip(s, turn - 1, n).wait_recv()
+            for copy in chip_copies(s, turn - 1):
+                copy.wait_recv()
 
         live = info[s, :, LANES - 1:] > when.astype(jnp.float32)
         for g in range(groups):
             lanes = slice(g * LANES, (g + 1) * LANES)
             through = own[s, :, lanes]
-            for n in range(3):
+            for n in range(2):
                 through += jnp.where(turn > 0, taken[s, (turn + 1) % 2, n, :, lanes].astype(jnp.float32), 0.0)
             total = held[s, :, lanes] + through
             in_gate, forget, cell_gate, out_gate, old = (stage[s, k, :, lanes] for k in range(5))
@@ -566,17 +641,21 @@
             cell_grad[s, :, lanes] = new * forget + jnp.where(live, 0.0, later)
             held[s, :, lanes] = jnp.where(live, 0.0, total)
 
-        @pl.when(turn < length - 1)
-        def _():
-            load_acts(s, step - 1).start()
-            load_grad(s, step - 1).start()
+        if s == 0:
+            @pl.when(turn > 0)
+            def _():
+                pass_on(1, turn - 1)
+        else:
+            pass_on(0, turn)
 
         @pl.when(turn > 0)
         def _():
             for n in range(4):
                 to_core(s, turn - 1, n).wait_send()
-            for n in range(3):
-                to_chip(s, turn - 1, n).wait_send()
+            for h in range(2):
+                to_middle(s, turn - 1, h).wait_send()
+            for copy in chip_copies(s, turn - 1):
+                copy.wait_send()
 
         for n, block in enumerate(tuple(other_core(peer) for peer in peers) + (sibling,)):
             sent[s, n] = matmul(pre[s], w[d, block], NT).astype(jnp.bfloat16)
@@ -585,48 +664,63 @@
             part = matmul(pre[s], w[d, block], NT)
             to_core(s, turn, n).wait_recv()
             part += got[s, turn % 2, n].astype(jnp.float32)
-            if n < 3:
-                passed[s, n] = part.astype(jnp.bfloat16)
-                to_chip(s, turn, n).start()
+            if n == 0:
+                passed[s, 0] = part.astype(jnp.bfloat16)
+                for h in range(2):
+                    to_middle(s, turn, h).start()
+            elif n < 3:
+                now, later = n - 1, 2 - n
+                kept[s, later] = part[later * depth:(later + 1) * depth]
+                passed[s, n, now * depth:(now + 1) * depth] = (
+                    part[now * depth:(now + 1) * depth].astype(jnp.bfloat16)
+                )
+                to_chip(s, turn, n, now).start()
             else:
                 own[s] = part
 
-        if s % SPLIT == SPLIT - 1:
-            both = range(s - SPLIT + 1, s + 1)
-            for i in both:
-                load_whole(i, step).wait()
-            for b in range(w.shape[1]):
-                rec[d, b] += sum(matmul(whole[i, b], pre[i], TN) for i in both)
-
-            @pl.when(turn < length - 1)
-            def _():
-                for i in both:
-                    load_whole(i, step - 1).start()
-
-            letters = lax.broadcasted_iota(jnp.int32, (VOCAB_PAD, rows), 0).astype(jnp.float32)
-            terms = []
-            for i in both:
-                hot = letters == ids[i, pl.ds(step, 1), :]
-                terms.append(matmul(hot.astype(jnp.bfloat16), pre[i]))
-            letter_grad[d] += sum(terms)
+        @pl.when(turn < length - 1)
+        def _():
+            load_acts(s, step - 1).start()
+            load_grad(s, step - 1).start()
+
+        load_whole(s, step).wait()
+        for b in range(w.shape[1]):
+            rec[s, b] += matmul(whole[s, b], pre[s], TN)
+
+        @pl.when(turn < length - 1)
+        def _():
+            load_whole(s, step - 1).start()
+
+        letters = lax.broadcasted_iota(jnp.int32, (VOCAB_PAD, rows), 0).astype(jnp.float32)
+        hot = letters == ids[s, pl.ds(step, 1), :]
+        letter_grad[s] += matmul(hot.astype(jnp.bfloat16), pre[s])
 
     def every(turn, carry):
-        for s in stream_order():
+        for s in range(2):
             half(turn, s)
         return carry
 
     lax.fori_loop(0, length, every, 0)
-    for s in stream_order():
-        for n in range(3):
-            to_chip(s, length - 1, n).wait_recv()
+    pass_on(1, length - 1)
+    for n in range(1, seqs):
+        dec_copy(n).wait()
+    for d in range(2):
+        dec_out[d] = dec[seq, d].astype(jnp.float32) + sum(
+            dec_in[n, d].astype(jnp.float32) for n in range(seqs - 1)
+        )
+    for s in range(2):
+        for copy in chip_copies(s, length - 1):
+            copy.wait_recv()
         total = held[s] + own[s]
-        for n in range(3):
+        for n in range(2):
             total += taken[s, (length - 1) % 2, n].astype(jnp.float32)
         hidden_grad[s] = total
         for n in range(4):
             to_core(s, length - 1, n).wait_send()
-        for n in range(3):
-            to_chip(s, length - 1, n).wait_send()
+        for h in range(2):
+            to_middle(s, length - 1, h).wait_send()
+        for copy in chip_copies(s, length - 1):
+            copy.wait_send()
 
     def narrow(b, carry):
         for d in range(2):
@@ -639,22 +733,16 @@
     store.wait()
 
 
-def kernel_step(ids, lengths, order, count, h_init, c_init, embed, w_in, w_rec, bias, w_dec, b_dec, matrix):
+def kernel_step(ids, lengths, order, h_init, c_init, embed, w_in, w_rec, bias, w_dec, b_dec):
     seqs = lax.axis_size("seq")
     local_times, all_streams = ids.shape
     length = local_times * seqs
-    per_dev, units = h_init.shape[1:]
-    streams, rows = 2 * SPLIT, per_dev // SPLIT
+    rows, units = h_init.shape[1:]
+    streams = 2
     letters, width = embed.shape[1:]
     columns = w_rec.shape[2]
     blocks = w_rec.shape[1] // units
     any_space, vmem = pl.BlockSpec(memory_space=pl.ANY), pl.BlockSpec(memory_space=pltpu.VMEM)
-    own_order = lax.dynamic_slice_in_dim(order, lax.axis_index("seq") * per_dev, per_dev)
-    pad_letters = VOCAB_PAD - letters
-    embed_pad = jnp.pad(embed, ((0, 0), (0, pad_letters), (0, LANES - width)))
-    w_in_pad = jnp.pad(w_in, ((0, 0), (0, LANES - width), (0, 0)))
-    w_dec_pad = jnp.pad(w_dec, ((0, 0), (0, 0), (0, pad_letters)))
-    b_dec_pad = jnp.pad(b_dec, ((0, 0), (0, pad_letters)), constant_values=-1e30)[:, None]
     bias_grouped = jnp.swapaxes(bias.reshape(2, units // LANES, LANES, 4), -1, -2).reshape(2, 1, columns)
     f32, bf16 = jnp.float32, jnp.bfloat16
     dma = pltpu.SemaphoreType.DMA
@@ -675,7 +763,7 @@
             shape((streams, length, rows), f32),
             shape((2, LANES, columns), bf16),
         ),
-        in_specs=[vmem] * 4 + [pl.BlockSpec(memory_space=pltpu.SMEM)] + [vmem] * 8 + [any_space],
+        in_specs=[vmem] * 10 + [any_space],
         out_specs=(any_space,) * 4 + (vmem,) * 8,
         scratch_shapes=[
             pltpu.VMEM((2, blocks, units, columns), bf16),
@@ -688,13 +776,17 @@
             pltpu.VMEM((streams, rows, VOCAB_PAD), bf16),
             pltpu.VMEM((seqs, 8, all_streams), f32),
             pltpu.VMEM((LANES, all_streams), f32),
+            pltpu.VMEM((4 * LANES, 4 * LANES), bf16),
+            pltpu.VMEM((2, VOCAB_PAD, LANES), bf16),
+            pltpu.VMEM((2, 1, VOCAB_PAD), f32),
+            pltpu.VMEM((1, 1), f32),
             dma((2,)),
             dma((seqs - 1,)),
             dma((seqs,)),
             dma((7,)),
             dma((blocks,)),
-            dma((streams, 2, 7)),
-            dma((streams, 3, blocks)),
+            dma((streams, 2, 10)),
+            dma((streams, 3, blocks, 2)),
             dma((streams, 2)),
             dma((streams,)),
             dma((streams,)),
@@ -704,20 +796,20 @@
         ),
         name="forward_visits",
     )(
-        ids, lengths[None], own_order[None], own_order[:, None], (1.0 / count).reshape(1, 1),
-        h_init.reshape(streams, rows, units), c_init.reshape(streams, rows, units), embed_pad, w_in_pad,
-        bias_grouped, b_dec_pad, w_dec_pad, matrix, w_rec.reshape(2, blocks, units, columns),
-    )
-    rec_grad, letter_grad, hidden_grad, cell_grad = pl.pallas_call(
+        ids, lengths[None], order[None], h_init, c_init, embed, w_in, bias_grouped, b_dec, w_dec,
+        w_rec.reshape(2, blocks, units, columns),
+    )
+    rec_grad, letter_grad, hidden_grad, cell_grad, dec_part = pl.pallas_call(
         functools.partial(backward_kernel, length),
         out_shape=(
             shape((2, blocks, units, columns), bf16),
             shape((2, VOCAB_PAD, columns), f32),
             shape((streams, rows, units), f32),
             shape((streams, rows, units), f32),
+            shape((2, units // seqs, VOCAB_PAD), f32),
         ),
-        in_specs=[vmem] * 3 + [any_space] * 4,
-        out_specs=(any_space, vmem, vmem, vmem),
+        in_specs=[vmem] * 4 + [any_space] * 4,
+        out_specs=(any_space,) + (vmem,) * 4,
         scratch_shapes=[
             pltpu.VMEM((2, blocks, units, columns), bf16),
             pltpu.VMEM((2, blocks, units, columns), f32),
@@ -730,39 +822,107 @@
             pltpu.VMEM((streams, 4, rows, units), bf16),
             pltpu.VMEM((streams, 2, 4, rows, units), bf16),
             pltpu.VMEM((streams, 3, rows, units), bf16),
-            pltpu.VMEM((streams, 2, 3, rows, units), bf16),
+            pltpu.VMEM((streams, 2, 2, rows, units), bf16),
+            pltpu.VMEM((streams, 2, rows // 2, units), f32),
+            pltpu.VMEM((streams, 2, 2, rows // 2, units), bf16),
+            pltpu.VMEM((2, units, VOCAB_PAD), bf16),
+            pltpu.VMEM((seqs, 2, units // seqs, VOCAB_PAD), bf16),
+            pltpu.VMEM((seqs - 1, 2, units // seqs, VOCAB_PAD), bf16),
             dma,
             dma((streams,)),
             dma((streams,)),
             dma((streams,)),
             dma((streams, 4)),
             dma((streams, 2, 4)),
-            dma((streams, 3)),
-            dma((streams, 2, 3)),
+            dma((streams, 2, 2)),
+            dma((streams, 2, 2, 2)),
+            dma((streams, 2)),
+            dma((streams, 2, 2)),
+            dma((seqs - 1,)),
+            dma((seqs - 1,)),
         ],
         compiler_params=pltpu.CompilerParams(
             collective_id=1, has_side_effects=True, vmem_limit_bytes=VMEM_LIMIT
         ),
         name="backward_visits",
-    )(info, slot_ids, w_dec_pad, acts, grads, wholes, w_grouped)
-    rec_part, edge_part, dec_part, small = kernel_sums(
-        rec_grad, letter_grad, embed_pad, w_in_grouped, matrix, width, letters, dec_grad,
-        (loss, logit_sq, hidden_sq, dec_bias),
-    )
-    at = 2 * TABLE
-    return (
-        small[at, 0],
-        jnp.sum(small[at + 3:at + 5], axis=1),
-        jnp.sum(small[at + 1:at + 3], axis=1),
-        small[at + 5:at + 5 + 2 * (VOCAB_PAD // LANES)].reshape(2, VOCAB_PAD)[:, :letters],
-        dec_part[:, :, :letters],
-        hidden_grad.reshape(h_init.shape),
-        cell_grad.reshape(h_init.shape),
-        rec_part.reshape(2, -1, columns),
-        edge_part[:, :width],
-        edge_part[:, width],
-        small[:at].reshape(2, TABLE, LANES)[:, :letters, :width],
-    )
+    )(info, slot_ids, w_dec, dec_grad, acts, grads, wholes, w_grouped)
+    rec_part, edge_part, small = kernel_sums(
+        rec_grad, letter_grad, embed, w_in_grouped, (loss, logit_sq, hidden_sq, dec_bias)
+    )
+    outs = (
+        shape((1, 1), f32),
+        shape(h_init.shape, f32),
+        shape(h_init.shape, f32),
+        shape(embed.shape, f32),
+        shape((2, width, columns // seqs), f32),
+        shape((2, w_rec.shape[1] // seqs, columns), f32),
+        shape((2, columns // seqs), f32),
+        shape((2, units // seqs, letters), f32),
+        shape((2, letters), f32),
+        shape((1, 2), f32),
+        shape((1, 2), f32),
+        shape((1, 2), f32),
+    )
+    tile = rec_part.shape[2]
+    parts = rec_part.shape[1]
+    results = pl.pallas_call(
+        functools.partial(finish_kernel, w_rec.shape[1]),
+        grid=(2, parts),
+        out_shape=outs,
+        in_specs=[vmem] * 7 + [pl.BlockSpec((1, 1, tile, columns), lambda d, r: (d, r, 0, 0))],
+        out_specs=tuple(
+            pl.BlockSpec((1, tile, columns), lambda d, r: (d, r, 0)) if n == 5 else vmem for n in range(len(outs))
+        ),
+        scratch_shapes=[pltpu.VMEM((4 * LANES, 4 * LANES), bf16)],
+        compiler_params=pltpu.CompilerParams(
+            dimension_semantics=("arbitrary", "arbitrary"), vmem_limit_bytes=VMEM_LIMIT
+        ),
+        name="results",
+    )(lengths[None], embed, edge_part, dec_part, small, hidden_grad, cell_grad, rec_part)
+    scalar = (0, 9, 10, 11)
+    return tuple(
+        x.reshape(()) if n == 0 else x.reshape(2) if n in scalar else x for n, x in enumerate(results)
+    )
+
+
+def finish_kernel(
+    all_units, lens, embed, edge, dec, small, hidden_in, cell_in, rec,
+    loss, hidden_grad, cell_grad, embed_grad, in_grad, rec_grad, bias_grad, dec_grad, dec_bias, rms_embed, rms_hidden,
+    rms_logits, matrix,
+):
+    first = (pl.program_id(0) == 0) & (pl.program_id(1) == 0)
+    letters, width = embed.shape[1:]
+    span = matrix.shape[0]
+
+    @pl.when(first)
+    def _():
+        matrix[...] = regroup_matrix(span)
+        hidden_grad[...] = hidden_in[...]
+        cell_grad[...] = cell_in[...]
+        live = jnp.sum(lens[...].astype(jnp.float32), axis=1, keepdims=True)
+        count = 2.0 * (live - lens.shape[1])
+        at = 2 * TABLE
+        loss[...] = small[at:at + 1, :1] / count
+        for d in range(2):
+            embed_grad[d] = small[d * TABLE:d * TABLE + letters, :width]
+            in_grad[d] = edge[d, :width]
+            bias_grad[d:d + 1] = edge[d, width:width + 1]
+            dec_grad[d] = dec[d, :, :letters]
+            for n in range(VOCAB_PAD // LANES):
+                row = at + 5 + d * (VOCAB_PAD // LANES) + n
+                last = min(LANES, letters - n * LANES)
+                dec_bias[d:d + 1, n * LANES:n * LANES + last] = small[row:row + 1, :last]
+            table = embed[d].astype(jnp.float32)
+            square = jnp.sum(jnp.sum(table * table, axis=1, keepdims=True), axis=0, keepdims=True)
+            rms_embed[:, d:d + 1] = jnp.sqrt(square / (letters * width))
+            logit_sq = jnp.sum(small[at + 1 + d:at + 2 + d], axis=1, keepdims=True)
+            hidden_sq = jnp.sum(small[at + 3 + d:at + 4 + d], axis=1, keepdims=True)
+            rms_hidden[:, d:d + 1] = jnp.sqrt(hidden_sq / (all_units * live))
+            rms_logits[:, d:d + 1] = jnp.sqrt(logit_sq / (letters * count / 2.0))
+
+    for g in range(rec.shape[-1] // span):
+        columns = slice(g * span, (g + 1) * span)
+        rec_grad[0, :, columns] = matmul(rec[0, 0, :, columns], matrix[...], NT)
 
 
 PIECE = 128
@@ -778,10 +938,10 @@
 
 
 def reduce_kernel(
-    width, rec_hbm, letter_grad, embed, w_in, matrix, dec_grad, loss, logit_sq, hidden_sq, dec_bias,
-    rec_out, edge_out, dec_out, small_out,
-    own, ahead, behind, edge, edge_in, dec, dec_in, small, part, small_in, part_in, summed,
-    load_sem, line_send, line_recv, back_send, back_recv, edge_send, edge_recv, dec_send, dec_recv,
+    rec_hbm, letter_grad, embed_in, w_in, loss, logit_sq, hidden_sq, dec_bias,
+    rec_out, edge_out, small_out,
+    own, ahead, behind, edge, edge_in, small, part, small_in, part_in, summed, matrix, embed,
+    load_sem, line_send, line_recv, back_send, back_recv, edge_send, edge_recv,
     scatter_send, scatter_recv, seq_send, seq_recv, gather_send, gather_recv,
 ):
     seq, me = lax.axis_index("seq"), lax.axis_index("mp")
@@ -890,10 +1050,6 @@
         to = other_seq(n)
         return send(edge.at[to], edge_in.at[n - 1], edge_send.at[n - 1], edge_recv.at[n - 1], to, me)
 
-    def dec_copy(n):
-        to = other_seq(n)
-        return send(dec.at[to], dec_in.at[n - 1], dec_send.at[n - 1], dec_recv.at[n - 1], to, me)
-
     def scatter_copy(n):
         to = other_mp(n)
         rows = pl.ds(pl.multiple_of(to * share, 8), share)
@@ -916,6 +1072,12 @@
 
     start = 6
     lax.fori_loop(0, 2, advance, 0)
+    matrix[...] = regroup_matrix(matrix.shape[0])
+    letters, width = embed_in.shape[1:]
+    lanes = lax.broadcasted_iota(jnp.int32, (letters, LANES), 1)
+    padded(embed, embed_in)
+    for d in range(2):
+        embed[d, :letters] = jnp.where(lanes == width, 1.0, embed[d, :letters].astype(jnp.float32)).astype(jnp.bfloat16)
     first = jnp.where(me == 0, 1.0, 0.0)
     for d in range(2):
         small[d * TABLE:(d + 1) * TABLE] = spread(letter_grad[d], w_in[d], NT)[:TABLE]
@@ -943,11 +1105,8 @@
         for q in range(count):
             group, offset = (q * wide) // span, (q * wide) % span
             edge[q, d] = flat[group][:rows, offset:offset + wide]
-            depth = dec.shape[2]
-            dec[q, d] = dec_grad[d, q * depth:(q + 1) * depth].astype(jnp.bfloat16)
     for n in range(1, count):
         edge_copy(n).start()
-        dec_copy(n).start()
     lax.fori_loop(2, start, advance, 0)
     for n in range(1, peers):
         scatter_copy(n).wait()
@@ -971,18 +1130,11 @@
     small_out[...] = summed[...]
     for n in range(1, count):
         edge_copy(n).wait()
-        dec_copy(n).wait()
     for d in range(2):
         edge_out[d] = edge[seq, d].astype(jnp.float32) + sum(
             edge_in[n, d].astype(jnp.float32) for n in range(count - 1)
         )
-        dec_out[d] = dec[seq, d].astype(jnp.float32) + sum(
-            dec_in[n, d].astype(jnp.float32) for n in range(count - 1)
-        )
-        for r in range(parts):
-            for g in range(own.shape[-1] // span):
-                columns = slice(g * span, (g + 1) * span)
-                rec_out[d, r, :, columns] = matmul(own[d, seq, r, :, columns], matrix[...], NT)
+        rec_out[d] = own[d, seq]
 
     def finish(k, carry):
         i, d, r = slot(k)
@@ -1006,13 +1158,13 @@
     return matmul(other, high, TN) + matmul(other, low, TN)
 
 
-def kernel_sums(rec_grad, letter_grad, embed_pad, w_in_pad, matrix, width, letters, dec_grad, stats):
+def kernel_sums(rec_grad, letter_grad, embed, w_in_grouped, stats):
     count = lax.axis_size("seq")
     peers = lax.axis_size("mp")
     columns = rec_grad.shape[-1]
     all_rows = rec_grad.shape[1] * rec_grad.shape[2]
     parts = all_rows // count // PIECE
-    units = dec_grad.shape[1]
+    width = embed.shape[2]
     edge_rows = -(-(width + 1) // 8) * 8
     small_rows = -(-(2 * TABLE + 16) // (8 * peers)) * 8 * peers
     share = small_rows // peers
@@ -1020,38 +1172,33 @@
     dma = pltpu.SemaphoreType.DMA
     shape = jax.ShapeDtypeStruct
     vmem = pl.BlockSpec(memory_space=pltpu.VMEM)
-    ones = (jnp.arange(VOCAB_PAD) < letters).astype(bf16)
-    embed_one = embed_pad.at[:, :, width].set(ones[None])
     return pl.pallas_call(
-        functools.partial(reduce_kernel, width),
+        reduce_kernel,
         out_shape=(
-            shape((2, parts, PIECE, columns), f32),
+            shape((2, parts, PIECE, columns), bf16),
             shape((2, edge_rows, columns // count), f32),
-            shape((2, units // count, VOCAB_PAD), f32),
             shape((small_rows, LANES), f32),
         ),
-        in_specs=[pl.BlockSpec(memory_space=pl.ANY)] + [vmem] * 9,
-        out_specs=(vmem,) * 4,
+        in_specs=[pl.BlockSpec(memory_space=pl.ANY)] + [vmem] * 7,
+        out_specs=(vmem,) * 3,
         scratch_shapes=[
             pltpu.VMEM((2, count, parts, PIECE, columns), bf16),
             pltpu.VMEM((count - 1, 2, parts, PIECE, columns), bf16),
             pltpu.VMEM((count // 2, 2, parts, PIECE, columns), bf16),
             pltpu.VMEM((count, 2, edge_rows, columns // count), bf16),
             pltpu.VMEM((count - 1, 2, edge_rows, columns // count), bf16),
-            pltpu.VMEM((count, 2, units // count, VOCAB_PAD), bf16),
-            pltpu.VMEM((count - 1, 2, units // count, VOCAB_PAD), bf16),
             pltpu.VMEM((small_rows, LANES), f32),
             pltpu.VMEM((share, LANES), f32),
             pltpu.VMEM((peers - 1, share, LANES), f32),
             pltpu.VMEM((count - 1, share, LANES), f32),
             pltpu.VMEM((small_rows, LANES), f32),
+            pltpu.VMEM((4 * LANES, 4 * LANES), bf16),
+            pltpu.VMEM((2, VOCAB_PAD, LANES), bf16),
             dma,
             dma((count - 1, 2, parts)),
             dma((count - 1, 2, parts)),
             dma((count // 2, 2, parts)),
             dma((count // 2, 2, parts)),
-            dma((count - 1,)),
-            dma((count - 1,)),
             dma((count - 1,)),
             dma((count - 1,)),
             dma((peers - 1,)),
@@ -1066,8 +1213,7 @@
         ),
         name="gradient_sums",
     )(
-        rec_grad.reshape(2, count, parts, PIECE, columns), letter_grad, embed_one, w_in_pad, matrix, dec_grad,
-        *stats,
+        rec_grad.reshape(2, count, parts, PIECE, columns), letter_grad, embed, w_in_grouped, *stats,
     )
 
 
@@ -1114,20 +1260,17 @@
     streams = ids.shape[1]
     per_dev, own_units = h_init.shape[1:]
     all_units, letter_count = w_rec.shape[1], embed.shape[1]
+    fits = own_units % LANES == 0 and per_dev % LANES == 0 and per_dev <= 256 and own_units <= 256
+    fits = fits and all_units % (lax.axis_size("seq") * PIECE) == 0 and letter_count <= TABLE
+    if lax.axis_size("mp") == 8 and lax.axis_size("seq") == 4 and fits and embed.shape[2] < LANES:
+        return kernel_step(ids, lengths, order, h_init, c_init, embed, w_in, w_rec, bias, w_dec, b_dec)
     live_total = jnp.sum(lengths).astype(jnp.float32)
     count = 2.0 * (jnp.sum(lengths) - streams).astype(jnp.float32)
     _, matrix = column_order(own_units)
-    operands = (ids, lengths, order, count, h_init, c_init, embed, w_in, w_rec, bias, w_dec, b_dec, matrix)
-    fits = own_units % LANES == 0 and per_dev % (SPLIT * LANES) == 0 and per_dev <= 256
-    fits = fits and all_units % (lax.axis_size("seq") * PIECE) == 0 and letter_count <= TABLE
-    if lax.axis_size("mp") == 8 and lax.axis_size("seq") == 4 and fits:
-        results = kernel_step(*operands)
-    else:
-        results = plain_step(*operands)
     (
         loss_sum, hidden_all, logit_all, dec_bias_grad, dec_part, hidden_grad, cell_grad, rec_out, in_out, bias_out,
         embed_grad,
-    ) = results
+    ) = plain_step(ids, lengths, order, count, h_init, c_init, embed, w_in, w_rec, bias, w_dec, b_dec, matrix)
     embed_wide = embed.astype(jnp.float32)
     rms_embed = jnp.sqrt(jnp.mean(embed_wide * embed_wide, axis=(1, 2)))
     return (

time: 637 us -> 606 us (0.951)
  local copies, waits for them, and re-layouts: 26 us -> 10.5 us
    pallas_call x1, Pallas kernels: 223 us -> 216 us  [kernel_step(): pl.pallas_call(functools.partial(forward_kernel, length, letters), out_sh...]
    unnamed x24 -> x5, local copies, waits for them, and re-layouts: 14.1 us -> 8.87 us
    pallas_call x1 -> x2, Pallas kernels: 160 us -> 160 us  [the longest x1 151 us: kernel_sums(): pl.pallas_call(reduce_kernel, out_shape=(shape((2, parts, PIECE, columns)...]
where the time goes in v5:
time: 606 us; the launch traced here: 605 us
  Pallas kernels  594 us (98%)
  local copies, waits for them, and re-layouts  10.5 us (2%)
    pallas_call x1, Pallas kernels, kernel_step(): pl.pallas_call(functools.partial(backward_kernel, length), out_shape=(sha...  218 us
    pallas_call x1, Pallas kernels, kernel_step(): pl.pallas_call(functools.partial(forward_kernel, length, letters), out_sh...  216 us
    pallas_call x1, Pallas kernels, kernel_sums(): pl.pallas_call(reduce_kernel, out_shape=(shape((2, parts, PIECE, columns)...  151 us

profile of v5, /device:TPU:0, one launch (start us, length us, event | category | flops | bytes accessed | tf_op | source)
XLA Modules:
  0.0 605.3 jit_solution(1228267182782972937)
XLA Ops:
  0.6 1.6 copy.38.embed_in.embed
  2.2 1.0 reshape.48
  3.2 0.7 copy.32
  3.9 1.9 copy.35.w_dec_in
  5.8 1.8 copy.34.w_in_raw
  7.7 216.2 %forward_visits.1 = (bf16[16,2,8,256,256]{4,3,2,1,0:T(8,128)(2,1)}, f32[16,2,5,256,256]{4,3,2,1,0:T(8,128)}, bf16[16,2,256,384]{3,2,1,0:T(8,128)(2,1)}, bf16[2,8...) custom-call(s32[4,1024]{1,0:T(4,128)} %ids_in.1, ...), custom_call_target="tpu_custom_call" | custom-call | tf_op jit(solution)/shard_map/forward_visits/pallas_call | solution.py:750
  223.9 217.8 %backward_visits.1 = (bf16[2,8,256,1024]{3,2,1,0:T(8,128)(2,1)}, f32[2,384,1024]{2,1,0:T(8,128)}, f32[2,256,256]{2,1,0:T(8,128)}, f32[2,256,256]{2,1,0:T(8,128)}, f32[2,64,384]{2,1,0:T(8,128)}) custom-call(f32[2,256,128]{2,1,0:T(8,128)} %get-tuple-element.44.info, f32[2,16,256]{2,1,0:T(8,128)} %get-tuple-element.45.ids, bf16[2,256,275]{2,1,0:T(8,128)(2,1)} %copy.35.w_dec_in, ...), custom_call_target="tpu_custom_call" | custom-call | tf_op jit(solution)/shard_map/backward_visits/pallas_call | solution.py:802
  441.7 150.8 %gradient_sums.1 = (bf16[2,4,128,1024]{3,2,1,0:T(8,128)(2,1)}, f32[2,104,256]{2,1,0:T(8,128)}, f32[576,128]{1,0:T(8,128)}) custom-call(bf16[2,4,4,128,1024]{4,3,2,1,0:T(8,128)(2,1)} %bitcast.11, f32[2,384,1024]{2,1,0:T(8,128)} %get-tuple-element.52.letter_grad, bf16[2,275,100]{2,1,0:T(8,128)(2,1)} %copy.38.embed_in.embed, ...), custom_call_target="tpu_custom_call" | custom-call | tf_op jit(solution)/shard_map/gradient_sums/pallas_call | solution.py:1175
  592.5 9.2 %results.1 = (f32[1,1]{1,0:T(1,128)}, f32[2,256,256]{2,1,0:T(8,128)}, f32[2,256,256]{2,1,0:T(8,128)}, f32[2,275,100]{2,1,0:T(8,128)}, f32[2,100,256]{2,1,0:T(8,1...) custom-call(s32[1,1024]{1,0:T(1,128)} %bitcast.15, ...), custom_call_target="tpu_custom_call" | custom-call | tf_op jit(solution)/shard_map/results/pallas_call | solution.py:868
  601.7 1.7 copy.40
  603.5 1.8 copy.39

commit v6 on v5

--- a/solution.py
+++ b/solution.py
@@ -331,7 +331,8 @@
                 w[d, b, :, part] = matmul(w[d, b, :, part], matrix[...]).astype(jnp.bfloat16)
         return carry
 
-    lax.fori_loop(0, blocks, regroup, 0)
+    for b in range(blocks):
+        regroup(b, 0)
     store_w.start()
     for n in range(1, seqs):
         ids_arrival(n).wait_recv()
@@ -448,20 +449,20 @@
             for block in (me,) + peers:
                 advance(block)
 
-        for block in (sibling,) + others:
-            transfer_whole(s, step, block, 6).wait_recv()
-
-        @pl.when(step < length)
-        def _():
-            for block in (sibling,) + others:
-                advance(block)
-
         if s == 0:
             pass_on(1, step)
         else:
             @pl.when(step < length)
             def _():
                 pass_on(0, step + 1)
+
+        for block in (sibling,) + others:
+            transfer_whole(s, step, block, 6).wait_recv()
+
+        @pl.when(step < length)
+        def _():
+            for block in (sibling,) + others:
+                advance(block)
 
         @pl.when(step < length)
         def _():
@@ -524,7 +525,7 @@
     length, info, ids, w_dec_in, dec_grad, acts, grads, wholes, w_hbm,
     rec_out, letter_grad, hidden_grad, cell_grad, dec_out,
     w, rec, stage, grad, whole, pre, held, own, sent, got, passed, taken, kept, middle, w_dec, dec, dec_in, load_sem, act_sem,
-    grad_sem, whole_sem, core_send, core_recv, chip_send, chip_recv, middle_send, middle_recv, dec_send, dec_recv,
+    grad_sem, whole_sem, core_send, core_recv, chip_send, chip_recv, middle_send, middle_recv, dec_send, dec_recv, store_sem,
 ):
     me, sibling, peers = neighbours()
     rows, units = held.shape[1:]
@@ -641,6 +642,18 @@
             cell_grad[s, :, lanes] = new * forget + jnp.where(live, 0.0, later)
             held[s, :, lanes] = jnp.where(live, 0.0, total)
 
+        @pl.when(turn > 0)
+        def _():
+            for n in range(4):
+                to_core(s, turn - 1, n).wait_send()
+            for h in range(2):
+                to_middle(s, turn - 1, h).wait_send()
+            for copy in chip_copies(s, turn - 1):
+                copy.wait_send()
+
+        for n, block in enumerate(tuple(other_core(peer) for peer in peers) + (sibling,)):
+            sent[s, n] = matmul(pre[s], w[d, block], NT).astype(jnp.bfloat16)
+            to_core(s, turn, n).start()
         if s == 0:
             @pl.when(turn > 0)
             def _():
@@ -648,18 +661,6 @@
         else:
             pass_on(0, turn)
 
-        @pl.when(turn > 0)
-        def _():
-            for n in range(4):
-                to_core(s, turn - 1, n).wait_send()
-            for h in range(2):
-                to_middle(s, turn - 1, h).wait_send()
-            for copy in chip_copies(s, turn - 1):
-                copy.wait_send()
-
-        for n, block in enumerate(tuple(other_core(peer) for peer in peers) + (sibling,)):
-            sent[s, n] = matmul(pre[s], w[d, block], NT).astype(jnp.bfloat16)
-            to_core(s, turn, n).start()
         for n, block in enumerate(peers + (me,)):
             part = matmul(pre[s], w[d, block], NT)
             to_core(s, turn, n).wait_recv()
@@ -725,12 +726,16 @@
     def narrow(b, carry):
         for d in range(2):
             w[d, b] = rec[d, b].astype(jnp.bfloat16)
+        store(b).start()
         return carry
 
-    lax.fori_loop(0, w.shape[1], narrow, 0)
-    store = pltpu.make_async_copy(w, rec_out, load_sem)
-    store.start()
-    store.wait()
+    def store(b):
+        return pltpu.make_async_copy(w.at[:, b], rec_out.at[:, b], store_sem.at[b])
+
+    for b in range(w.shape[1]):
+        narrow(b, 0)
+    for b in range(w.shape[1]):
+        store(b).wait()
 
 
 def kernel_step(ids, lengths, order, h_init, c_init, embed, w_in, w_rec, bias, w_dec, b_dec):
@@ -840,6 +845,7 @@
             dma((streams, 2, 2)),
             dma((seqs - 1,)),
             dma((seqs - 1,)),
+            dma((blocks,)),
         ],
         compiler_params=pltpu.CompilerParams(
             collective_id=1, has_side_effects=True, vmem_limit_bytes=VMEM_LIMIT

time: 606 us -> 593 us (0.979)
  Pallas kernels: 594 us -> 581 us
    pallas_call x1, Pallas kernels: 216 us -> 204 us  [kernel_step(): pl.pallas_call(functools.partial(forward_kernel, length, letters), out_sh...]
where the time goes in v6:
time: 593 us; the launch traced here: 592 us
  Pallas kernels  581 us (98%)
  local copies, waits for them, and re-layouts  10.5 us (2%)
    pallas_call x1, Pallas kernels, kernel_step(): pl.pallas_call(functools.partial(backward_kernel, length), out_shape=(sha...  216 us
    pallas_call x1, Pallas kernels, kernel_step(): pl.pallas_call(functools.partial(forward_kernel, length, letters), out_sh...  204 us
    pallas_call x1, Pallas kernels, kernel_sums(): pl.pallas_call(reduce_kernel, out_shape=(shape((2, parts, PIECE, columns)...  152 us

profile of v6, /device:TPU:0, one launch (start us, length us, event | category | flops | bytes accessed | tf_op | source)
XLA Modules:
  0.0 592.0 jit_solution(12648233224987275945)
XLA Ops:
  0.6 1.6 copy.38.embed_in.embed
  2.2 1.0 reshape.48
  3.2 0.7 copy.32
  3.9 1.9 copy.35.w_dec_in
  5.8 1.8 copy.34.w_in_raw
  7.7 204.2 %forward_visits.1 = (bf16[16,2,8,256,256]{4,3,2,1,0:T(8,128)(2,1)}, f32[16,2,5,256,256]{4,3,2,1,0:T(8,128)}, bf16[16,2,256,384]{3,2,1,0:T(8,128)(2,1)}, bf16[2,8...) custom-call(s32[4,1024]{1,0:T(4,128)} %ids_in.1, ...), custom_call_target="tpu_custom_call" | custom-call | tf_op jit(solution)/shard_map/forward_visits/pallas_call | solution.py:755
  211.9 215.7 %backward_visits.1 = (bf16[2,8,256,1024]{3,2,1,0:T(8,128)(2,1)}, f32[2,384,1024]{2,1,0:T(8,128)}, f32[2,256,256]{2,1,0:T(8,128)}, f32[2,256,256]{2,1,0:T(8,128)}, f32[2,64,384]{2,1,0:T(8,128)}) custom-call(f32[2,256,128]{2,1,0:T(8,128)} %get-tuple-element.44.info, f32[2,16,256]{2,1,0:T(8,128)} %get-tuple-element.45.ids, bf16[2,256,275]{2,1,0:T(8,128)(2,1)} %copy.35.w_dec_in, ...), custom_call_target="tpu_custom_call" | custom-call | tf_op jit(solution)/shard_map/backward_visits/pallas_call | solution.py:807
  427.7 151.6 %gradient_sums.1 = (bf16[2,4,128,1024]{3,2,1,0:T(8,128)(2,1)}, f32[2,104,256]{2,1,0:T(8,128)}, f32[576,128]{1,0:T(8,128)}) custom-call(bf16[2,4,4,128,1024]{4,3,2,1,0:T(8,128)(2,1)} %bitcast.11, f32[2,384,1024]{2,1,0:T(8,128)} %get-tuple-element.52.letter_grad, bf16[2,275,100]{2,1,0:T(8,128)(2,1)} %copy.38.embed_in.embed, ...), custom_call_target="tpu_custom_call" | custom-call | tf_op jit(solution)/shard_map/gradient_sums/pallas_call | solution.py:1181
  579.3 9.2 %results.1 = (f32[1,1]{1,0:T(1,128)}, f32[2,256,256]{2,1,0:T(8,128)}, f32[2,256,256]{2,1,0:T(8,128)}, f32[2,275,100]{2,1,0:T(8,128)}, f32[2,100,256]{2,1,0:T(8,1...) custom-call(s32[1,1024]{1,0:T(1,128)} %bitcast.15, ...), custom_call_target="tpu_custom_call" | custom-call | tf_op jit(solution)/shard_map/results/pallas_call | solution.py:874
  588.4 1.7 copy.40
  590.2 1.8 copy.39

commit v7 on v6

--- a/solution.py
+++ b/solution.py
@@ -215,8 +215,8 @@
 def forward_kernel(
     length, letters, ids_in, lens, order, h_in, c_in, embed_in, w_in_raw, bias, b_dec_in, w_dec_in, w_hbm,
     wholes, acts, grads, w_out, loss, logit_sq, hidden_sq, dec_bias, dec_grad, info, ids, w_in,
-    w, wd, buf, cell, acc, logit, stage, grad, all_ids, table, matrix, embed, b_dec, inverse, load_sem, ids_send, ids_recv, wd_send, wd_recv,
-    send_sem, recv_sem, save_sem, act_sem, grad_sem,
+    w, wd, buf, cell, acc, logit, stage, grad, all_ids, table, matrix, embed, b_dec, inverse, load_sem, ids_send, ids_recv, wd_send, wd_recv, wd_plane_send,
+    wd_core_recv, send_sem, recv_sem, save_sem, act_sem, grad_sem,
 ):
     me, sibling, peers = neighbours()
     seq, seqs, times = lax.axis_index("seq"), all_ids.shape[0], ids_in.shape[0]
@@ -273,16 +273,28 @@
     def core_copies(s, step):
         return [transfer_whole(s, step, block, 6 + n) for n, block in enumerate((me, side, up, across))]
 
+    share = units // seqs
+
+    def wd_rows(source, quarter):
+        return wd.at[source, :, pl.ds(pl.multiple_of(quarter * share, 16), share)]
+
     def wd_copy(n):
-        peer = (peers + (sibling,))[n]
-        return remote(wd.at[me], wd.at[me], wd_send.at[n], wd_recv.at[me], peer)
-
-    def wd_relay(n):
-        block = wd.at[peers[n]]
-        return remote(block, block, wd_send.at[4 + n], wd_recv.at[peers[n]], sibling)
-
-    def wd_arrival(source):
-        return remote(wd.at[source], wd.at[source], wd_send.at[0], wd_recv.at[source], sibling)
+        ref = wd_rows(me, seq)
+        return remote(ref, ref, wd_send.at[n], wd_recv.at[me, seq], peers[n])
+
+    def wd_across(n, k):
+        ref = wd_rows(peers[n], seq)
+        return pltpu.make_async_remote_copy(
+            src_ref=ref, dst_ref=ref, send_sem=wd_plane_send.at[n, k - 1], recv_sem=wd_recv.at[peers[n], seq],
+            device_id=((seq + k) % seqs, me), device_id_type=MESH,
+        )
+
+    def wd_arrival(n, k):
+        ref = wd_rows(peers[n], (seq + k) % seqs)
+        return remote(ref, ref, wd_send.at[0], wd_recv.at[peers[n], (seq + k) % seqs], sibling)
+
+    def wd_core(n, block):
+        return remote(wd.at[block], wd.at[block], wd_send.at[3 + n], wd_core_recv.at[block], sibling)
 
     def save(s, step):
         return pltpu.make_async_copy(buf.at[s, step % 3], wholes.at[step, s], save_sem.at[s, step % 2])
@@ -306,8 +318,9 @@
             copy.start()
         transfer_whole(s, 0, me, 6).start()
     padded(wd.at[me], w_dec_in)
-    for n in range(4):
+    for n in range(3):
         wd_copy(n).start()
+    wd_core(3, me).start()
     padded(embed, embed_in)
     padded(w_in, w_in_raw)
     b_dec[...] = jnp.full(b_dec.shape, -1e30, jnp.float32)
@@ -334,6 +347,10 @@
     for b in range(blocks):
         regroup(b, 0)
     store_w.start()
+    for n in range(3):
+        wd_arrival(n, 0).wait_recv()
+        for k in range(1, seqs):
+            wd_across(n, k).start()
     for n in range(1, seqs):
         ids_arrival(n).wait_recv()
     streams = rows
@@ -420,6 +437,18 @@
     def half(step, s):
         d = s
 
+        @pl.when(step == 2)
+        def _():
+            if s == 0:
+                for n in range(3):
+                    for k in range(1, seqs):
+                        wd_arrival(n, k).wait_recv()
+                    wd_core(n, peers[n]).start()
+                for block in (sibling,) + others:
+                    wd_core(0, block).wait_recv()
+            decode(s, step - 1)
+            save_grad(s, step - 2).start()
+
         @pl.when(step < length)
         def _():
             now = column_of(info[s], step)
@@ -431,13 +460,6 @@
             for h in halves:
                 transfer(s, step, block, h, 0, sibling).wait_recv()
             transfer_whole(s, step, block, 7 + n).start()
-
-        if s == 0:
-            @pl.when(step == 1)
-            def _():
-                for n, peer in enumerate(peers):
-                    wd_arrival(peer).wait_recv()
-                    wd_relay(n).start()
 
         slot = step % 3
 
@@ -484,18 +506,9 @@
             save_acts(s, step).start()
             save(s, step).start()
 
-        if s == 0:
-            @pl.when(step == 1)
-            def _():
-                for block in (sibling,) + others:
-                    wd_arrival(block).wait_recv()
-
-        @pl.when(step > 0)
-        def _():
-            @pl.when(step > 1)
-            def _():
-                save_grad(s, step - 2).wait()
-
+        @pl.when(step > 1)
+        def _():
+            save_grad(s, step - 2).wait()
             decode(s, step)
             save_grad(s, step - 1).start()
 
@@ -509,10 +522,12 @@
     store_w.wait()
     for n in range(1, seqs):
         ids_copy(n).wait_send()
-    for n in range(4):
+    for n in range(3):
         wd_copy(n).wait_send()
-    for n in range(3):
-        wd_relay(n).wait_send()
+        for k in range(1, seqs):
+            wd_across(n, k).wait_send()
+    for n, block in enumerate(peers + (me,)):
+        wd_core(n, block).wait_send()
     for s in range(2):
         save(s, length - 1).wait()
         save_acts(s, length - 1).wait()
@@ -789,6 +804,8 @@
             dma((seqs - 1,)),
             dma((seqs,)),
             dma((7,)),
+            dma((blocks, seqs)),
+            dma((3, seqs - 1)),
             dma((blocks,)),
             dma((streams, 2, 10)),
             dma((streams, 3, blocks, 2)),

time: 593 us -> 586 us (0.988)
  Pallas kernels: 581 us -> 574 us
    pallas_call x1, Pallas kernels: 204 us -> 197 us  [kernel_step(): pl.pallas_call(functools.partial(forward_kernel, length, letters), out_sh...]
where the time goes in v7:
time: 586 us; the launch traced here: 585 us
  Pallas kernels  574 us (98%)
  local copies, waits for them, and re-layouts  10.5 us (2%)
    pallas_call x1, Pallas kernels, kernel_step(): pl.pallas_call(functools.partial(backward_kernel, length), out_shape=(sha...  216 us
    pallas_call x1, Pallas kernels, kernel_step(): pl.pallas_call(functools.partial(forward_kernel, length, letters), out_sh...  197 us
    pallas_call x1, Pallas kernels, kernel_sums(): pl.pallas_call(reduce_kernel, out_shape=(shape((2, parts, PIECE, columns)...  152 us

profile of v7, /device:TPU:0, one launch (start us, length us, event | category | flops | bytes accessed | tf_op | source)
XLA Modules:
  0.0 584.8 jit_solution(10656787901260297721)
XLA Ops:
  0.6 1.6 copy.38.embed_in.embed
  2.2 1.0 reshape.48
  3.2 0.7 copy.32
  3.9 1.9 copy.35.w_dec_in
  5.8 1.8 copy.34.w_in_raw
  7.7 196.6 %forward_visits.1 = (bf16[16,2,8,256,256]{4,3,2,1,0:T(8,128)(2,1)}, f32[16,2,5,256,256]{4,3,2,1,0:T(8,128)}, bf16[16,2,256,384]{3,2,1,0:T(8,128)(2,1)}, bf16[2,8...) custom-call(s32[4,1024]{1,0:T(4,128)} %ids_in.1, ...), custom_call_target="tpu_custom_call" | custom-call | tf_op jit(solution)/shard_map/forward_visits/pallas_call | solution.py:770
  204.3 216.3 %backward_visits.1 = (bf16[2,8,256,1024]{3,2,1,0:T(8,128)(2,1)}, f32[2,384,1024]{2,1,0:T(8,128)}, f32[2,256,256]{2,1,0:T(8,128)}, f32[2,256,256]{2,1,0:T(8,128)}, f32[2,64,384]{2,1,0:T(8,128)}) custom-call(f32[2,256,128]{2,1,0:T(8,128)} %get-tuple-element.44.info, f32[2,16,256]{2,1,0:T(8,128)} %get-tuple-element.45.ids, bf16[2,256,275]{2,1,0:T(8,128)(2,1)} %copy.35.w_dec_in, ...), custom_call_target="tpu_custom_call" | custom-call | tf_op jit(solution)/shard_map/backward_visits/pallas_call | solution.py:824
  420.6 151.5 %gradient_sums.1 = (bf16[2,4,128,1024]{3,2,1,0:T(8,128)(2,1)}, f32[2,104,256]{2,1,0:T(8,128)}, f32[576,128]{1,0:T(8,128)}) custom-call(bf16[2,4,4,128,1024]{4,3,2,1,0:T(8,128)(2,1)} %bitcast.11, f32[2,384,1024]{2,1,0:T(8,128)} %get-tuple-element.52.letter_grad, bf16[2,275,100]{2,1,0:T(8,128)(2,1)} %copy.38.embed_in.embed, ...), custom_call_target="tpu_custom_call" | custom-call | tf_op jit(solution)/shard_map/gradient_sums/pallas_call | solution.py:1198
  572.1 9.2 %results.1 = (f32[1,1]{1,0:T(1,128)}, f32[2,256,256]{2,1,0:T(8,128)}, f32[2,256,256]{2,1,0:T(8,128)}, f32[2,275,100]{2,1,0:T(8,128)}, f32[2,100,256]{2,1,0:T(8,1...) custom-call(s32[1,1024]{1,0:T(1,128)} %bitcast.15, ...), custom_call_target="tpu_custom_call" | custom-call | tf_op jit(solution)/shard_map/results/pallas_call | solution.py:891
  581.3 1.7 copy.40
  583.0 1.8 copy.39

commit v8 on v7

--- a/solution.py
+++ b/solution.py
@@ -621,6 +621,20 @@
             passed[s, 2 - h, h * depth:(h + 1) * depth] = total.astype(jnp.bfloat16)
             to_chip(s, turn, 2 - h, h).start()
 
+    def outer(turn, s):
+        step = length - 1 - turn
+        load_whole(s, step).wait()
+        for b in range(w.shape[1]):
+            rec[s, b] += matmul(whole[s, b], pre[s], TN)
+
+        @pl.when(turn < length - 1)
+        def _():
+            load_whole(s, step - 1).start()
+
+        letters = lax.broadcasted_iota(jnp.int32, (VOCAB_PAD, rows), 0).astype(jnp.float32)
+        hot = letters == ids[s, pl.ds(step, 1), :]
+        letter_grad[s] += matmul(hot.astype(jnp.bfloat16), pre[s])
+
     def half(turn, s):
         step = length - 1 - turn
         d = s
@@ -673,8 +687,10 @@
             @pl.when(turn > 0)
             def _():
                 pass_on(1, turn - 1)
+                outer(turn - 1, 1)
         else:
             pass_on(0, turn)
+            outer(turn, 0)
 
         for n, block in enumerate(peers + (me,)):
             part = matmul(pre[s], w[d, block], NT)
@@ -699,17 +715,6 @@
             load_acts(s, step - 1).start()
             load_grad(s, step - 1).start()
 
-        load_whole(s, step).wait()
-        for b in range(w.shape[1]):
-            rec[s, b] += matmul(whole[s, b], pre[s], TN)
-
-        @pl.when(turn < length - 1)
-        def _():
-            load_whole(s, step - 1).start()
-
-        letters = lax.broadcasted_iota(jnp.int32, (VOCAB_PAD, rows), 0).astype(jnp.float32)
-        hot = letters == ids[s, pl.ds(step, 1), :]
-        letter_grad[s] += matmul(hot.astype(jnp.bfloat16), pre[s])
 
     def every(turn, carry):
         for s in range(2):
@@ -718,6 +723,7 @@
 
     lax.fori_loop(0, length, every, 0)
     pass_on(1, length - 1)
+    outer(length - 1, 1)
     for n in range(1, seqs):
         dec_copy(n).wait()
     for d in range(2):

time: 586 us -> 583 us (level)
  no operation moved by 1% of the time
where the time goes in v8:
time: 583 us; the launch traced here: 582 us
  Pallas kernels  571 us (98%)
  local copies, waits for them, and re-layouts  10.5 us (2%)
    pallas_call x1, Pallas kernels, kernel_step(): pl.pallas_call(functools.partial(backward_kernel, length), out_shape=(sha...  214 us
    pallas_call x1, Pallas kernels, kernel_step(): pl.pallas_call(functools.partial(forward_kernel, length, letters), out_sh...  197 us
    pallas_call x1, Pallas kernels, kernel_sums(): pl.pallas_call(reduce_kernel, out_shape=(shape((2, parts, PIECE, columns)...  152 us

profile of v8, /device:TPU:0, one launch (start us, length us, event | category | flops | bytes accessed | tf_op | source)
XLA Modules:
  0.0 582.3 jit_solution(16304011590162480464)
XLA Ops:
  0.6 1.6 copy.38.embed_in.embed
  2.2 1.0 reshape.48
  3.2 0.7 copy.32
  3.9 1.9 copy.35.w_dec_in
  5.8 1.8 copy.34.w_in_raw
  7.7 196.6 %forward_visits.1 = (bf16[16,2,8,256,256]{4,3,2,1,0:T(8,128)(2,1)}, f32[16,2,5,256,256]{4,3,2,1,0:T(8,128)}, bf16[16,2,256,384]{3,2,1,0:T(8,128)(2,1)}, bf16[2,8...) custom-call(s32[4,1024]{1,0:T(4,128)} %ids_in.1, ...), custom_call_target="tpu_custom_call" | custom-call | tf_op jit(solution)/shard_map/forward_visits/pallas_call | solution.py:776
  204.3 213.7 %backward_visits.1 = (bf16[2,8,256,1024]{3,2,1,0:T(8,128)(2,1)}, f32[2,384,1024]{2,1,0:T(8,128)}, f32[2,256,256]{2,1,0:T(8,128)}, f32[2,256,256]{2,1,0:T(8,128)}, f32[2,64,384]{2,1,0:T(8,128)}) custom-call(f32[2,256,128]{2,1,0:T(8,128)} %get-tuple-element.44.info, f32[2,16,256]{2,1,0:T(8,128)} %get-tuple-element.45.ids, bf16[2,256,275]{2,1,0:T(8,128)(2,1)} %copy.35.w_dec_in, ...), custom_call_target="tpu_custom_call" | custom-call | tf_op jit(solution)/shard_map/backward_visits/pallas_call | solution.py:830
  418.0 151.6 %gradient_sums.1 = (bf16[2,4,128,1024]{3,2,1,0:T(8,128)(2,1)}, f32[2,104,256]{2,1,0:T(8,128)}, f32[576,128]{1,0:T(8,128)}) custom-call(bf16[2,4,4,128,1024]{4,3,2,1,0:T(8,128)(2,1)} %bitcast.11, f32[2,384,1024]{2,1,0:T(8,128)} %get-tuple-element.52.letter_grad, bf16[2,275,100]{2,1,0:T(8,128)(2,1)} %copy.38.embed_in.embed, ...), custom_call_target="tpu_custom_call" | custom-call | tf_op jit(solution)/shard_map/gradient_sums/pallas_call | solution.py:1204
  569.6 9.2 %results.1 = (f32[1,1]{1,0:T(1,128)}, f32[2,256,256]{2,1,0:T(8,128)}, f32[2,256,256]{2,1,0:T(8,128)}, f32[2,275,100]{2,1,0:T(8,128)}, f32[2,100,256]{2,1,0:T(8,1...) custom-call(s32[1,1024]{1,0:T(1,128)} %bitcast.15, ...), custom_call_target="tpu_custom_call" | custom-call | tf_op jit(solution)/shard_map/results/pallas_call | solution.py:897
  578.7 1.7 copy.40
  580.5 1.8 copy.39
